TPU v7x, 128 devices: a whole 4x4x4 slice. The times are simulated.
128 devices in a mesh: ty: 4 (over x_hi, core), tx: 8 (over y, x_lo), ta: 4 (over z).
Axes of the slice: x: 4 (x_hi: 2, x_lo: 2; x = x_hi * 2 + x_lo), y: 4, z: 4, core: 2. Of those that a mesh axis runs over, the one named last changes fastest.
Arguments:
- movie: bfloat16 [16, 4, 1024, 1024], P('ta', None, 'ty', 'tx'), may hold values from 0 to 2
- footprints: float32 [2048, 4096], P(('ty', 'tx')), may hold values from 0 to 1
- traces: float32 [16, 2048], P('ta', ('ty', 'tx')), may hold values from 0 to 1
- anchor_row: int32 [2048], P(('ty', 'tx')), may hold values from -1 to 15
- anchor_col: int32 [2048], P(('ty', 'tx')), may hold values from -1 to 7
Outputs:
- footprints_out: float32 [2048, 4096], P(('ty', 'tx'))
- traces_out: float32 [16, 2048], P('ta', ('ty', 'tx'))
Inputs may be any that keep to these rules, and one draw needn't show every extreme that they name: `anchor_row`: cell row within the owner tile at which a neuron's patch block starts; -1 puts its upper half into the tile above. `anchor_col`: cell column within the owner tile at which a neuron's patch block starts; -1 puts its left half into the tile beside it.
All inputs are finite; a program needn't handle non-finite values.
Results may differ from a plain program's by a relative error of at most 0.0003.
Values may be sent and summed in bfloat16 or wider, within the bound.
No kernel may reach another device: no remote copies, remote signals or barrier semaphores. Data moves between devices by JAX's collectives and lax.ppermute only.
A program may use at most 128 MiB of HBM per device.

v0:
```python
import jax
import jax.numpy as jnp
from jax import lax
from jax.sharding import PartitionSpec as P

CELL = 16
ITERS = 2


RIDGE = 1.0


def with_halo(cells, sides, width):
    for axis, dim in sides:
        count = lax.axis_size(axis)
        ends = count - 1
        head = lax.slice_in_dim(cells, 0, width, axis=dim)
        tail = lax.slice_in_dim(cells, cells.shape[dim] - width, cells.shape[dim], axis=dim)
        cells = jnp.concatenate(
            [
                lax.ppermute(tail, axis, [(i, (i + 1) % count) for i in range(ends)]),
                cells,
                lax.ppermute(head, axis, [((i + 1) % count, i) for i in range(ends)]),
            ],
            axis=dim,
        )
    return cells


def to_cells(movie):
    frames, planes, height, breadth = movie.shape
    cell_rows = height // CELL
    cell_cols = breadth // CELL
    blocks = movie.reshape(frames, planes, cell_rows, CELL, cell_cols, CELL).transpose(
        2, 4, 0, 1, 3, 5
    )
    return blocks.reshape(cell_rows, cell_cols, frames * planes * CELL * CELL)


def fold_rows(extended):
    central = extended[2:-2]
    central = central.at[:2].add(extended[:2])
    return central.at[-2:].add(extended[-2:])


def fold_cols(extended):
    central = extended[:, 2:-2]
    central = central.at[:, :2].add(extended[:, :2])
    return central.at[:, -2:].add(extended[:, -2:])


def combine(partial_value):
    extended = with_halo(partial_value, (("ty", 0), ("tx", 1)), 2)
    return fold_cols(fold_rows(extended))


def patch_residue(observed, footprints, traces, cell_ids, grid_rows, grid_cols):
    owned = footprints.shape[0]
    frames = traces.shape[0]
    shaped = footprints.reshape(owned, 4, 1, -1)
    products = shaped * jnp.transpose(traces)[:, None, :, None]
    partial_value = jax.ops.segment_sum(
        products.reshape(owned * 4, -1), cell_ids, num_segments=grid_rows * grid_cols
    )
    estimate = combine(partial_value.reshape(grid_rows, grid_cols, -1)).reshape(
        grid_rows * grid_cols, frames, -1
    )
    residue = observed - estimate
    return jnp.take(residue, cell_ids, axis=0).reshape(owned, 4, frames, -1)


def shards(movie, footprints, traces, anchor_row, anchor_col):
    owned = footprints.shape[0]
    frames = traces.shape[0]
    local_cells = to_cells(movie)
    grid_rows = local_cells.shape[0] + 2
    grid_cols = local_cells.shape[1] + 2
    rimmed = with_halo(local_cells, (("ty", 0), ("tx", 1)), 1)
    observed = rimmed.reshape(grid_rows * grid_cols, frames, -1).astype(jnp.float32)
    corner = (anchor_row + 1) * grid_cols + anchor_col + 1
    offsets = jnp.array([0, 1, grid_cols, grid_cols + 1], dtype=jnp.int32)
    cell_ids = (corner[:, None] + offsets[None, :]).reshape(-1)
    for sweep in range(ITERS):
        energy = jnp.sum(footprints * footprints, axis=1)
        shaped = footprints.reshape(owned, 4, -1)
        gathered = patch_residue(observed, footprints, traces, cell_ids, grid_rows, grid_cols)
        update = jnp.einsum("kse,ksfe->fk", shaped, gathered, precision=lax.Precision.HIGHEST)
        traces = jnp.maximum(traces + update / (energy + RIDGE)[None, :], 0.0)
        regathered = patch_residue(observed, footprints, traces, cell_ids, grid_rows, grid_cols)
        numer_part = jnp.einsum(
            "fk,ksfe->kse", traces, regathered, precision=lax.Precision.HIGHEST
        ).reshape(owned, -1)
        strength_part = jnp.sum(traces * traces, axis=0)
        numerator, strength = lax.psum((numer_part, strength_part), "ta")
        footprints = jnp.maximum(footprints + numerator / (strength + RIDGE)[:, None], 0.0)
    return (footprints, traces)


def solution(mesh):
    placed = (
        P("ta", None, "ty", "tx"),
        P(("ty", "tx"), None),
        P("ta", ("ty", "tx")),
        P(("ty", "tx")),
        P(("ty", "tx")),
    )
    return jax.shard_map(
        shards,
        mesh=mesh,
        in_specs=placed,
        out_specs=(P(("ty", "tx"), None), P("ta", ("ty", "tx"))),
        check_vma=False,
    )
```

profile of v0, /device:TPU:1, one launch (start us, length us, event | category | flops | bytes accessed | tf_op | source)
XLA Modules:
  0.0 614.4 jit_solution(15205451002402303284)
XLA Ops:
  12.6 5.7 copy.23
  18.3 8.4 %scatter_custom_fusion = f32[180,4096]{1,0:T(8,128)S(1)} fusion(s32[256]{0:T(256)S(1)} %reshape.627, f32[256,4096]{1,0:T(8,128)} %bitcast.79, f32[]{:T(128)} %constant.364.clone.1), kind=kCustom, calls=%fused_computation.32 | custom fusion | flops 1048576 | bytes 2949632 | tf_op jit(solution)/shard_map/scatter-add | solution.py:62
  29.4 6.0 collective-permute-start.4
  38.2 9.5 %reshape.581 = bf16[4,4,16,16,8,16]{5,4,3,2,1,0:T(8,128)(2,1)} reshape(bf16[4,4,256,128]{3,2,1,0:T(8,128)(2,1)} %param.40) | data formatting | bytes 2097152 | tf_op jit(solution)/shard_map/reshape | solution.py:34
  47.7 9.2 %copy.30 = bf16[4,4,16,16,8,16]{5,3,1,0,4,2:T(8,128)(2,1)} copy(bf16[4,4,16,16,8,16]{5,4,3,2,1,0:T(8,128)(2,1)} %reshape.581) | data formatting | bytes 2097152 | tf_op jit(solution)/shard_map/reshape | solution.py:34
  61.6 5.1 collective-permute-start
  72.6 15.9 %reshape.582 = bf16[16,8,4096]{2,1,0:T(8,128)(2,1)} reshape(bf16[16,8,4,4,16,16]{5,4,3,2,1,0:T(8,128)(2,1)} %bitcast.69) | data formatting | bytes 2097152 | tf_op jit(solution)/shard_map/reshape | solution.py:37
  94.2 2.7 constant_dynamic-update-slice_fusion.4
  102.6 4.7 collective-permute-start.2
  109.0 7.6 %collective-permute-done.6 = f32[22,2,4096]{2,1,0:T(2,128)S(1)} collective-permute-done((f32[22,2,4096]{2,1,0:T(2,128)S(1)}, f32[22,2,4096]{2,1,0:T(2,128)S(1)}, u32[]{:S(2)}, u32[]{:S(2)}) %collective-permute-start.6) | collective-permute-done | bytes 720928 | tf_op jit(solution)/shard_map/ppermute | solution.py:21
  116.6 18.1 %collective-permute-done.7 = f32[22,2,4096]{2,1,0:T(2,128)S(1)} collective-permute-done((f32[22,2,4096]{2,1,0:T(2,128)S(1)}, f32[22,2,4096]{2,1,0:T(2,128)S(1)}, u32[]{:S(2)}, u32[]{:S(2)}) %collective-permute-start.7) | collective-permute-done | bytes 720928 | tf_op jit(solution)/shard_map/ppermute | solution.py:23
  138.5 6.5 %collective-permute-done.3 = bf16[18,1,4096]{2,1,0:T(2,128)(2,1)S(1)} collective-permute-done((bf16[18,1,4096]{2,1,0:T(2,128)(2,1)S(1)}, bf16[18,1,4096]{2,1,0:T(2,128)(2,1)S(1)}, u32[]{:S(2)}, u32[]{:S(2)}) %collective-permute-start.3) | collective-permute-done | bytes 147488 | tf_op jit(solution)/shard_map/ppermute | solution.py:23
  145.7 3.4 convert_subtract_fusion.3
  149.2 5.5 sub.25
  154.6 6.6 %gather_fusion = f32[256,4,1024]{2,1,0:T(4,128)} fusion(f32[180,4,1024]{2,1,0:T(4,128)} %sub.25, s32[1024]{0:T(1024)S(1)} %pad_clamp_fusion), kind=kCustom, calls=%fused_computation.clone | custom fusion | bytes 8389632 | tf_op jit(solution)/shard_map/jit(_take)/gather | solution.py:69
  161.2 3.1 broadcast_select_fusion.3
  164.4 15.2 %fusion.38 = f32[64,1,4,1]{2,1,3,0:T(1,128)S(1)} fusion(f32[64,4,4,1024]{3,2,1,0:T(4,128)S(1)} %bitcast.77, f32[64,4,1024,1]{2,3,1,0:T(1,128)S(1)} %copy-done.15), kind=kOutput, calls=%fused_computation.112 | convolution fusion | flops 12582912 | bytes 5243904 | tf_op jit(solution)/shard_map/kse,ksfe->fk/dot_general | solution.py:87
  182.1 5.7 copy.24
  187.8 9.2 %scatter_custom_fusion.1 = f32[180,4096]{1,0:T(8,128)} fusion(s32[256]{0:T(256)S(1)} %reshape.627, f32[256,4096]{1,0:T(8,128)} %bitcast.80, f32[]{:T(128)} %constant.364.clone.1), kind=kCustom, calls=%fused_computation.30 | custom fusion | flops 1048576 | bytes 2949632 | tf_op jit(solution)/shard_map/scatter-add | solution.py:62
  199.1 4.9 collective-permute-start.8
  203.9 3.7 reshape.585
  211.9 2.8 constant_dynamic-update-slice_fusion.7
  214.8 5.9 collective-permute-done.9
  228.4 7.1 %collective-permute-done.10 = f32[22,2,4096]{2,1,0:T(2,128)S(1)} collective-permute-done((f32[22,2,4096]{2,1,0:T(2,128)}, f32[22,2,4096]{2,1,0:T(2,128)S(1)}, u32[]{:S(2)}, u32[]{:S(2)}) %collective-permute-start.10) | collective-permute-done | bytes 720928 | tf_op jit(solution)/shard_map/ppermute | solution.py:21
  235.5 18.1 %collective-permute-done.11 = f32[22,2,4096]{2,1,0:T(2,128)} collective-permute-done((f32[22,2,4096]{2,1,0:T(2,128)}, f32[22,2,4096]{2,1,0:T(2,128)}, u32[]{:S(2)}, u32[]{:S(2)}) %collective-permute-start.11) | collective-permute-done | bytes 720928 | tf_op jit(solution)/shard_map/ppermute | solution.py:23
  253.6 4.0 pad_maximum_fusion.1
  264.2 3.4 convert_subtract_fusion.2
  267.7 5.5 sub.27
  273.1 6.6 %gather_fusion.1 = f32[256,4,1024]{2,1,0:T(4,128)} fusion(f32[180,4,1024]{2,1,0:T(4,128)} %sub.27, s32[1024]{0:T(1024)S(1)} %pad_clamp_fusion), kind=kCustom, calls=%fused_computation.1.clone | custom fusion | bytes 8389632 | tf_op jit(solution)/shard_map/jit(_take)/gather | solution.py:69
  279.7 3.0 broadcast_select_fusion.2
  282.7 7.9 %fusion.39 = f32[64,1,4,1024]{3,1,2,0:T(1,128)S(1)} fusion(f32[4,64,1,1]{0,2,3,1:T(1,128)S(1)} %copy.17, f32[64,4,4,1024]{3,2,1,0:T(4,128)S(1)} %bitcast.71), kind=kOutput, calls=%fused_computation.113 | convolution fusion | flops 12582912 | bytes 5243904 | tf_op jit(solution)/shard_map/fk,ksfe->kse/dot_general | solution.py:90
  292.6 9.9 %psum.29 = f32[64]{0:T(128)S(1)} all-reduce(f32[64]{0:T(128)S(1)} %get-tuple-element.199), channel_id=1, replica_groups=mesh['ty'=4,'tx'=8,'ta'=4] {'ta'}, use_global_device_ids=true, to_apply=%region_5.7 | all-reduce | flops 64 | bytes 512 | tf_op jit(solution)/shard_map/psum | solution.py:94
  302.5 34.4 %all-reduce.3.cloned.1.call-done = f32[64,4096]{1,0:T(8,128)} async-done(((f32[64,4096]{1,0:T(8,128)}), f32[64,4096]{1,0:T(8,128)}) %all-reduce.3.cloned.1.call-update) | async-done | bytes 1048592 | tf_op jit(solution)/shard_map/psum | solution.py:94
  342.6 5.7 copy.26
  348.3 9.2 %scatter_custom_fusion.2 = f32[180,4096]{1,0:T(8,128)} fusion(s32[256]{0:T(256)S(1)} %reshape.627, f32[256,4096]{1,0:T(8,128)} %bitcast.81, f32[]{:T(128)} %constant.364.clone.1), kind=kCustom, calls=%fused_computation.28 | custom fusion | flops 1048576 | bytes 2949632 | tf_op jit(solution)/shard_map/scatter-add | solution.py:62
  358.8 7.3 %collective-permute-start.12 = (f32[2,10,4096]{2,1,0:T(8,128)S(1)}, f32[2,10,4096]{2,1,0:T(8,128)}, u32[]{:S(2)}, u32[]{:S(2)}) collective-permute-start(f32[2,10,4096]{2,1,0:T(8,128)S(1)} %slice.593), channel_id=1, source_target_pairs={{0,32},{32,64},{64,96},{1,33},{33,65},{65,97},{2,34},{34,66},{66,9... | collective-permute-start | bytes 983048 | tf_op jit(solution)/shard_map/ppermute | solution.py:21
  366.0 3.7 reshape.588
  373.2 2.8 constant_dynamic-update-slice_fusion.10
  376.1 5.7 collective-permute-done.13
  389.4 3.6 reshape.684
  393.0 3.6 collective-permute-done.14
  396.6 18.0 %collective-permute-done.15 = f32[22,2,4096]{2,1,0:T(2,128)} collective-permute-done((f32[22,2,4096]{2,1,0:T(2,128)}, f32[22,2,4096]{2,1,0:T(2,128)}, u32[]{:S(2)}, u32[]{:S(2)}) %collective-permute-start.15) | collective-permute-done | bytes 720928 | tf_op jit(solution)/shard_map/ppermute | solution.py:23
  414.6 4.0 pad_maximum_fusion.2
  422.8 3.4 convert_subtract_fusion.1
  426.2 5.9 sub.29
  432.1 6.6 %gather_fusion.2 = f32[256,4,1024]{2,1,0:T(4,128)} fusion(f32[180,4,1024]{2,1,0:T(4,128)} %sub.29, s32[1024]{0:T(1024)S(1)} %pad_clamp_fusion), kind=kCustom, calls=%fused_computation.2.clone | custom fusion | bytes 8389632 | tf_op jit(solution)/shard_map/jit(_take)/gather | solution.py:69
  438.7 3.1 broadcast_select_fusion.1
  441.8 15.2 %fusion.40 = f32[64,1,4,1]{2,1,3,0:T(1,128)S(1)} fusion(f32[64,4,4,1024]{3,2,1,0:T(4,128)S(1)} %bitcast.78, f32[64,4,1024,1]{2,3,1,0:T(1,128)S(1)} %copy-done.16), kind=kOutput, calls=%fused_computation.114 | convolution fusion | flops 12582912 | bytes 5243904 | tf_op jit(solution)/shard_map/kse,ksfe->fk/dot_general | solution.py:87
  458.3 5.7 copy.27
  464.1 9.2 %scatter_custom_fusion.3 = f32[180,4096]{1,0:T(8,128)} fusion(s32[256]{0:T(256)S(1)} %reshape.627, f32[256,4096]{1,0:T(8,128)} %bitcast.76, f32[]{:T(128)} %constant.364.clone.1), kind=kCustom, calls=%fused_computation.26 | custom fusion | flops 1048576 | bytes 2949632 | tf_op jit(solution)/shard_map/scatter-add | solution.py:62
  474.5 4.2 collective-permute-start.16
  478.8 3.7 reshape.590
  486.5 2.8 constant_dynamic-update-slice_fusion.13
  489.4 6.1 collective-permute-done.17
  503.3 7.5 %collective-permute-done.18 = f32[22,2,4096]{2,1,0:T(2,128)S(1)} collective-permute-done((f32[22,2,4096]{2,1,0:T(2,128)}, f32[22,2,4096]{2,1,0:T(2,128)S(1)}, u32[]{:S(2)}, u32[]{:S(2)}) %collective-permute-start.18) | collective-permute-done | bytes 720928 | tf_op jit(solution)/shard_map/ppermute | solution.py:21
  510.8 17.9 %collective-permute-done.19 = f32[22,2,4096]{2,1,0:T(2,128)S(1)} collective-permute-done((f32[22,2,4096]{2,1,0:T(2,128)}, f32[22,2,4096]{2,1,0:T(2,128)S(1)}, u32[]{:S(2)}, u32[]{:S(2)}) %collective-permute-start.19) | collective-permute-done | bytes 720928 | tf_op jit(solution)/shard_map/ppermute | solution.py:23
  528.7 3.8 pad_maximum_fusion.3
  537.4 3.4 convert_subtract_fusion
  540.8 4.2 sub.31
  545.0 4.7 gather_fusion.3
  549.7 3.0 broadcast_select_fusion
  552.7 7.9 %fusion.41 = f32[64,1,4,1024]{3,1,2,0:T(1,128)S(1)} fusion(f32[4,64,1,1]{0,2,3,1:T(1,128)S(1)} %copy.21, f32[64,4,4,1024]{3,2,1,0:T(4,128)S(1)} %bitcast.70), kind=kOutput, calls=%fused_computation.115 | convolution fusion | flops 12582912 | bytes 5243904 | tf_op jit(solution)/shard_map/fk,ksfe->kse/dot_general | solution.py:90
  562.5 7.7 %psum.31 = f32[64]{0:T(128)S(1)} all-reduce(f32[64]{0:T(128)S(1)} %get-tuple-element.195), channel_id=1, replica_groups=mesh['ty'=4,'tx'=8,'ta'=4] {'ta'}, use_global_device_ids=true, to_apply=%region_11.13 | all-reduce | flops 64 | bytes 512 | tf_op jit(solution)/shard_map/psum | solution.py:94
  570.2 34.6 %all-reduce.5.cloned.1.call-done = f32[64,4096]{1,0:T(8,128)} async-done(((f32[64,4096]{1,0:T(8,128)}), f32[64,4096]{1,0:T(8,128)}) %all-reduce.5.cloned.1.call-update) | async-done | bytes 1048592 | tf_op jit(solution)/shard_map/psum | solution.py:94
  (159 shorter events, 109.5 us)
Async XLA Ops:
  7.2 329.8 %all-reduce.3.cloned.1.call-start = ((), (), s32[]{:S(2)}) async-start(), calls=%async_computation | async-start | bytes 2097152 | tf_op jit(solution)/shard_map/psum | solution.py:94
  10.7 7.7 %copy-start.7 = (f32[64,4,1024]{2,1,0:T(4,128)}, f32[64,4,1024]{2,1,0:T(4,128)S(1)}, u32[]{:S(2)}) copy-start(f32[64,4,1024]{2,1,0:T(4,128)S(1)} %mul.86) | copy-start | bytes 3145732
  29.4 63.7 %collective-permute-start.4 = (f32[2,10,4096]{2,1,0:T(8,128)}, f32[2,10,4096]{2,1,0:T(8,128)}, u32[]{:S(2)}, u32[]{:S(2)}) collective-permute-start(f32[2,10,4096]{2,1,0:T(8,128)} %slice.561), channel_id=1, source_target_pairs={{0,32},{32,64},{64,96},{1,33},{33,65},{65,97},{2,34},{34,66},{66,9... | collective-permute-start | bytes 983048 | tf_op jit(solution)/shard_map/ppermute | solution.py:21
  36.3 60.6 %collective-permute-start.5 = (f32[2,10,4096]{2,1,0:T(8,128)}, f32[2,10,4096]{2,1,0:T(8,128)}, u32[]{:S(2)}, u32[]{:S(2)}) collective-permute-start(f32[2,10,4096]{2,1,0:T(8,128)} %slice.563), channel_id=1, source_target_pairs={{32,0},{64,32},{96,64},{33,1},{65,33},{97,65},{34,2},{66,34},{98,6... | collective-permute-start | bytes 983048 | tf_op jit(solution)/shard_map/ppermute | solution.py:23
  61.6 29.4 %collective-permute-start = (bf16[1,8,4096]{2,1,0:T(8,128)(2,1)}, bf16[1,8,4096]{2,1,0:T(8,128)(2,1)}, u32[]{:S(2)}, u32[]{:S(2)}) collective-permute-start(bf16[1,8,4096]{2,1,0:T(8,128)(2,1)} %slice.555), channel_id=1, source_target_pairs={{0,32},{32,64},{64,96},{1,33},{33,65},{65,97},{2,34},{34,66},{66,9... | collective-permute-start | bytes 196616 | tf_op jit(solution)/shard_map/ppermute | solution.py:21
  68.1 25.0 %collective-permute-start.1 = (bf16[1,8,4096]{2,1,0:T(8,128)(2,1)}, bf16[1,8,4096]{2,1,0:T(8,128)(2,1)S(1)}, u32[]{:S(2)}, u32[]{:S(2)}) collective-permute-start(bf16[1,8,4096]{2,1,0:T(8,128)(2,1)} %slice.557), channel_id=1, source_target_pairs={{32,0},{64,32},{96,64},{33,1},{65,33},{97,65},{34,2},{66,34},{98,6... | collective-permute-start | bytes 196616 | tf_op jit(solution)/shard_map/ppermute | solution.py:23
  72.6 15.9 %copy-start.5 = (f32[64,4096]{1,0:T(8,128)S(1)}, f32[64,4096]{1,0:T(8,128)}, u32[]{:S(2)}) copy-start(f32[64,4096]{1,0:T(8,128)} %param.41) | copy-start | bytes 3145732
  98.4 18.2 %collective-permute-start.6 = (f32[22,2,4096]{2,1,0:T(2,128)S(1)}, f32[22,2,4096]{2,1,0:T(2,128)S(1)}, u32[]{:S(2)}, u32[]{:S(2)}) collective-permute-start(f32[22,2,4096]{2,1,0:T(2,128)S(1)} %get-tuple-element.209), channel_id=1, source_target_pairs={{0,4},{4,8},{8,12},{12,16},{16,20},{20,24},{24,28},{1,5},{5,9},{9,... | collective-permute-start | bytes 2162696 | tf_op jit(solution)/shard_map/ppermute | solution.py:21
  100.7 33.9 %collective-permute-start.7 = (f32[22,2,4096]{2,1,0:T(2,128)S(1)}, f32[22,2,4096]{2,1,0:T(2,128)S(1)}, u32[]{:S(2)}, u32[]{:S(2)}) collective-permute-start(f32[22,2,4096]{2,1,0:T(2,128)S(1)} %get-tuple-element.210), channel_id=1, source_target_pairs={{4,0},{8,4},{12,8},{16,12},{20,16},{24,20},{28,24},{5,1},{9,5},{13... | collective-permute-start | bytes 2162696 | tf_op jit(solution)/shard_map/ppermute | solution.py:23
  102.6 35.9 %collective-permute-start.2 = (bf16[18,1,4096]{2,1,0:T(2,128)(2,1)S(1)}, bf16[18,1,4096]{2,1,0:T(2,128)(2,1)S(1)}, u32[]{:S(2)}, u32[]{:S(2)}) collective-permute-start(bf16[18,1,4096]{2,1,0:T(2,128)(2,1)S(1)} %get-tuple-element.219), channel_id=1, source_target_pairs={{0,4},{4,8},{8,12},{12,16},{16,20},{20,24},{24,28},{1,5},{5,9},{9,... | collective-permute-start | bytes 442376 | tf_op jit(solution)/shard_map/ppermute | solution.py:21
  107.3 37.7 %collective-permute-start.3 = (bf16[18,1,4096]{2,1,0:T(2,128)(2,1)S(1)}, bf16[18,1,4096]{2,1,0:T(2,128)(2,1)S(1)}, u32[]{:S(2)}, u32[]{:S(2)}) collective-permute-start(bf16[18,1,4096]{2,1,0:T(2,128)(2,1)S(1)} %get-tuple-element.220), channel_id=1, source_target_pairs={{4,0},{8,4},{12,8},{16,12},{20,16},{24,20},{28,24},{5,1},{9,5},{13... | collective-permute-start | bytes 442376 | tf_op jit(solution)/shard_map/ppermute | solution.py:23
  138.5 125.7 %copy-start.10 = (bf16[18,1,4096]{2,1,0:T(2,128)(2,1)}, bf16[18,1,4096]{2,1,0:T(2,128)(2,1)S(1)}, u32[]{:S(2)}) copy-start(bf16[18,1,4096]{2,1,0:T(2,128)(2,1)S(1)} %collective-permute-done.2) | copy-start | bytes 442372
  145.0 0.7 copy-start.12
  161.2 3.1 copy-start.15
  164.3 15.3 %copy-start.18 = (f32[4,64]{1,0:T(4,128)S(1)}, f32[4,64]{1,0:T(4,128)}, u32[]{:S(2)}) copy-start(f32[4,64]{1,0:T(4,128)} %param.42) | copy-start | bytes 3076
  199.1 11.8 %collective-permute-start.8 = (f32[2,10,4096]{2,1,0:T(8,128)}, f32[2,10,4096]{2,1,0:T(8,128)}, u32[]{:S(2)}, u32[]{:S(2)}) collective-permute-start(f32[2,10,4096]{2,1,0:T(8,128)} %slice.577), channel_id=1, source_target_pairs={{0,32},{32,64},{64,96},{1,33},{33,65},{65,97},{2,34},{34,66},{66,9... | collective-permute-start | bytes 983048 | tf_op jit(solution)/shard_map/ppermute | solution.py:21
  208.5 12.2 %collective-permute-start.9 = (f32[2,10,4096]{2,1,0:T(8,128)}, f32[2,10,4096]{2,1,0:T(8,128)S(1)}, u32[]{:S(2)}, u32[]{:S(2)}) collective-permute-start(f32[2,10,4096]{2,1,0:T(8,128)} %slice.579), channel_id=1, source_target_pairs={{32,0},{64,32},{96,64},{33,1},{65,33},{97,65},{34,2},{66,34},{98,6... | collective-permute-start | bytes 983048 | tf_op jit(solution)/shard_map/ppermute | solution.py:23
  220.7 2.5 copy-start
  224.8 10.7 %collective-permute-start.10 = (f32[22,2,4096]{2,1,0:T(2,128)}, f32[22,2,4096]{2,1,0:T(2,128)S(1)}, u32[]{:S(2)}, u32[]{:S(2)}) collective-permute-start(f32[22,2,4096]{2,1,0:T(2,128)} %get-tuple-element.207), channel_id=1, source_target_pairs={{0,4},{4,8},{8,12},{12,16},{16,20},{20,24},{24,28},{1,5},{5,9},{9,... | collective-permute-start | bytes 2162696 | tf_op jit(solution)/shard_map/ppermute | solution.py:21
  227.0 26.5 %collective-permute-start.11 = (f32[22,2,4096]{2,1,0:T(2,128)}, f32[22,2,4096]{2,1,0:T(2,128)}, u32[]{:S(2)}, u32[]{:S(2)}) collective-permute-start(f32[22,2,4096]{2,1,0:T(2,128)} %get-tuple-element.208), channel_id=1, source_target_pairs={{4,0},{8,4},{12,8},{16,12},{20,16},{24,20},{28,24},{5,1},{9,5},{13... | collective-permute-start | bytes 2162696 | tf_op jit(solution)/shard_map/ppermute | solution.py:23
  257.6 2.6 copy-start.1
  262.4 1.8 copy-start.13
  292.5 312.3 %all-reduce.5.cloned.1.call-start = ((), (), s32[]{:S(2)}) async-start(), calls=%async_computation.1 | async-start | bytes 2097152 | tf_op jit(solution)/shard_map/psum | solution.py:94
  341.4 6.9 %copy-start.8 = (f32[64,4,1024]{2,1,0:T(4,128)}, f32[64,4,1024]{2,1,0:T(4,128)S(1)}, u32[]{:S(2)}) copy-start(f32[64,4,1024]{2,1,0:T(4,128)S(1)} %mul.96) | copy-start | bytes 3145732
  358.8 13.4 %collective-permute-start.12 = (f32[2,10,4096]{2,1,0:T(8,128)S(1)}, f32[2,10,4096]{2,1,0:T(8,128)}, u32[]{:S(2)}, u32[]{:S(2)}) collective-permute-start(f32[2,10,4096]{2,1,0:T(8,128)S(1)} %slice.593), channel_id=1, source_target_pairs={{0,32},{32,64},{64,96},{1,33},{33,65},{65,97},{2,34},{34,66},{66,9... | collective-permute-start | bytes 983048 | tf_op jit(solution)/shard_map/ppermute | solution.py:21
  369.8 12.0 %collective-permute-start.13 = (f32[2,10,4096]{2,1,0:T(8,128)S(1)}, f32[2,10,4096]{2,1,0:T(8,128)S(1)}, u32[]{:S(2)}, u32[]{:S(2)}) collective-permute-start(f32[2,10,4096]{2,1,0:T(8,128)S(1)} %slice.595), channel_id=1, source_target_pairs={{32,0},{64,32},{96,64},{33,1},{65,33},{97,65},{34,2},{66,34},{98,6... | collective-permute-start | bytes 983048 | tf_op jit(solution)/shard_map/ppermute | solution.py:23
  381.8 2.5 copy-start.2
  385.9 10.7 %collective-permute-start.14 = (f32[22,2,4096]{2,1,0:T(2,128)}, f32[22,2,4096]{2,1,0:T(2,128)S(1)}, u32[]{:S(2)}, u32[]{:S(2)}) collective-permute-start(f32[22,2,4096]{2,1,0:T(2,128)} %get-tuple-element.205), channel_id=1, source_target_pairs={{0,4},{4,8},{8,12},{12,16},{16,20},{20,24},{24,28},{1,5},{5,9},{9,... | collective-permute-start | bytes 2162696 | tf_op jit(solution)/shard_map/ppermute | solution.py:21
  388.1 26.5 %collective-permute-start.15 = (f32[22,2,4096]{2,1,0:T(2,128)}, f32[22,2,4096]{2,1,0:T(2,128)}, u32[]{:S(2)}, u32[]{:S(2)}) collective-permute-start(f32[22,2,4096]{2,1,0:T(2,128)} %get-tuple-element.206), channel_id=1, source_target_pairs={{4,0},{8,4},{12,8},{16,12},{20,16},{24,20},{28,24},{5,1},{9,5},{13... | collective-permute-start | bytes 2162696 | tf_op jit(solution)/shard_map/ppermute | solution.py:23
  389.4 29.5 %slice-start = ((s8[5767168]{0:T(1024)(128)(4,1)}), s8[1572864]{0:T(1024)(128)(4,1)S(1)}, s32[]{:S(2)}) async-start(s8[5767168]{0:T(1024)(128)(4,1)} %bitcast.66), calls=%async_computation.2 | async-start | bytes 3145728
  393.0 25.9 %slice-start.1 = ((s8[5767168]{0:T(1024)(128)(4,1)}), s8[4194304]{0:T(1024)(128)(4,1)S(1)}, s32[]{:S(2)}) async-start(s8[5767168]{0:T(1024)(128)(4,1)} %bitcast.66), calls=%async_computation.3 | async-start | bytes 8388608
  421.1 1.7 copy-start.11
  421.1 1.7 copy-start.14
  438.7 3.1 copy-start.16
  441.8 15.4 %copy-start.9 = (f32[64,4,1024]{2,1,0:T(4,128)S(1)}, f32[64,4,1024]{2,1,0:T(4,128)}, u32[]{:S(2)}) copy-start(f32[64,4,1024]{2,1,0:T(4,128)} %copy-done.8) | copy-start | bytes 3145732
  457.1 46.1 %copy-start.17 = (f32[4,64]{1,0:T(4,128)}, f32[4,64]{1,0:T(4,128)S(1)}, u32[]{:S(2)}) copy-start(f32[4,64]{1,0:T(4,128)S(1)} %get-tuple-element.196) | copy-start | bytes 3076
  474.5 10.9 %collective-permute-start.16 = (f32[2,10,4096]{2,1,0:T(8,128)S(1)}, f32[2,10,4096]{2,1,0:T(8,128)}, u32[]{:S(2)}, u32[]{:S(2)}) collective-permute-start(f32[2,10,4096]{2,1,0:T(8,128)S(1)} %slice.609), channel_id=1, source_target_pairs={{0,32},{32,64},{64,96},{1,33},{33,65},{65,97},{2,34},{34,66},{66,9... | collective-permute-start | bytes 983048 | tf_op jit(solution)/shard_map/ppermute | solution.py:21
  483.3 12.2 %collective-permute-start.17 = (f32[2,10,4096]{2,1,0:T(8,128)}, f32[2,10,4096]{2,1,0:T(8,128)S(1)}, u32[]{:S(2)}, u32[]{:S(2)}) collective-permute-start(f32[2,10,4096]{2,1,0:T(8,128)} %slice.611), channel_id=1, source_target_pairs={{32,0},{64,32},{96,64},{33,1},{65,33},{97,65},{34,2},{66,34},{98,6... | collective-permute-start | bytes 983048 | tf_op jit(solution)/shard_map/ppermute | solution.py:23
  495.6 2.5 copy-start.3
  499.6 11.2 %collective-permute-start.18 = (f32[22,2,4096]{2,1,0:T(2,128)}, f32[22,2,4096]{2,1,0:T(2,128)S(1)}, u32[]{:S(2)}, u32[]{:S(2)}) collective-permute-start(f32[22,2,4096]{2,1,0:T(2,128)} %get-tuple-element.203), channel_id=1, source_target_pairs={{0,4},{4,8},{8,12},{12,16},{16,20},{20,24},{24,28},{1,5},{5,9},{9,... | collective-permute-start | bytes 2162696 | tf_op jit(solution)/shard_map/ppermute | solution.py:21
  501.9 26.8 %collective-permute-start.19 = (f32[22,2,4096]{2,1,0:T(2,128)}, f32[22,2,4096]{2,1,0:T(2,128)S(1)}, u32[]{:S(2)}, u32[]{:S(2)}) collective-permute-start(f32[22,2,4096]{2,1,0:T(2,128)} %get-tuple-element.204), channel_id=1, source_target_pairs={{4,0},{8,4},{12,8},{16,12},{20,16},{24,20},{28,24},{5,1},{9,5},{13... | collective-permute-start | bytes 2162696 | tf_op jit(solution)/shard_map/ppermute | solution.py:23
  532.4 2.6 copy-start.4
  552.7 52.1 %copy-start.6 = (f32[64,4096]{1,0:T(8,128)S(1)}, f32[64,4096]{1,0:T(8,128)}, u32[]{:S(2)}) copy-start(f32[64,4096]{1,0:T(8,128)} %get-tuple-element.198) | copy-start | bytes 3145732
Sparse Core Ops, SparseCore 0:
  292.7 44.2 all-reduce.2
  562.7 42.0 all-reduce.4
where the time goes:
time: 627 us; the launch traced here: 614 us
  waiting for transfers between devices  191 us (30%)
  local copies, waits for them, and re-layouts  188 us (30%)
  other arithmetic  97.1 us (15%)
  starting transfers between devices  58.3 us (9%)
  matrix products  46.2 us (7%)
  blocking collectives  17.6 us (3%)
  between operations  15.3 us (2%)
    ppermute x10, waiting for transfers between devices, with_halo(): lax.ppermute(head, axis, [((i + 1) % count, i) for i in range(ends)])  96.2 us
    psum x2, waiting for transfers between devices, shards(): numerator, strength = lax.psum((numer_part, strength_part), 'ta')  69 us
    unnamed x58, local copies, waits for them, and re-layouts  56.6 us
    ppermute x10, starting transfers between devices, with_halo(): lax.ppermute(tail, axis, [(i, (i + 1) % count) for i in range(ends)])  41.2 us
    scatter-add x4, other arithmetic, patch_residue(): jax.ops.segment_sum(products.reshape(owned * 4, -1), cell_ids, num_segmen...  36.2 us
    dot_general x2, matrix products, shards(): jnp.einsum('kse,ksfe->fk', shaped, gathered, precision=lax.Precision.HIGH...  30.3 us
    ppermute x10, waiting for transfers between devices, with_halo(): lax.ppermute(tail, axis, [(i, (i + 1) % count) for i in range(ends)])  26.3 us
    gather x4, local copies, waits for them, and re-layouts, patch_residue(): return jnp.take(residue, cell_ids, axis=0).reshape(owned, 4, frames, -1)  24.4 us
  transfers between devices with their start and end apart: 22, of which 15 were waited for; matrix products, arithmetic and copies ran while one was open for 14% of the time, Pallas kernels for 0%

commit v1 on v0

v1 whole, which is shorter than its diff:
```python
import functools

import jax
import jax.numpy as jnp
from jax import lax
from jax.experimental import pallas as pl
from jax.experimental.pallas import tpu as pltpu
from jax.sharding import PartitionSpec as P

ITERS = 2
RIDGE = 1.0
TX = 8
TA = 4
GROUP = TX * TA
OWNED = 64
COUNT = TX * OWNED
ROW = (TX * 8 + 2) * TA
CELL_ROWS = 16
FIELD = (CELL_ROWS + 2) * ROW
INNER = CELL_ROWS * ROW
VMEM = pl.BlockSpec(memory_space=pltpu.VMEM)
SMEM = pl.BlockSpec(memory_space=pltpu.SMEM)
F32 = jnp.float32


def iotas():
    return (
        lax.broadcasted_iota(jnp.int32, (8, 128), 0),
        lax.broadcasted_iota(jnp.int32, (8, 128), 1),
    )


def pick_lanes(value, index):
    return jnp.take_along_axis(value, index, axis=1, mode="promise_in_bounds")


def pick_rows(value, index):
    return jnp.take_along_axis(value, index, axis=0, mode="promise_in_bounds")


def merge_lanes(first, second, shift, lane):
    return jnp.where(
        (lane & shift) != 0,
        second + pltpu.roll(second, shift, 1),
        first + pltpu.roll(first, 128 - shift, 1),
    )


def merge_rows(first, second, shift, sub):
    return jnp.where(
        (sub & shift) != 0,
        second + pltpu.roll(second, shift, 0),
        first + pltpu.roll(first, 8 - shift, 0),
    )


def spread(value, m, sub, lane):
    wide = pick_lanes(value, (lane & 96) + m)
    turned = pltpu.roll(wide, 4, 0)
    low = sub < 4
    return jnp.where(low, wide, turned), jnp.where(low, turned, wide)


def print_pair(prints_ref, neuron, sub, lane):
    row = jnp.broadcast_to(prints_ref[pl.ds(neuron, 1), :], (8, 128))
    index = (lane & 31) + jnp.where(sub < 4, 0, 32)
    return pick_lanes(row, index), pick_lanes(row, index + 64)


def patch(neuron, places_ref):
    start = pl.multiple_of(places_ref[neuron], 4)
    return pl.ds(start, 8), pl.ds(start + ROW, 8)


def subtract_all(activity_ref, prints_ref, places_ref, field_ref):
    sub, lane = iotas()

    def tile(v, _):
        value = activity_ref[v]

        def some(mh, _):
            for ml in range(4):
                pair = spread(value, mh * 4 + ml, sub, lane)
                for half in range(2):
                    neuron = v * OWNED + mh * 8 + half * 4 + ml
                    upper, lower = print_pair(prints_ref, neuron, sub, lane)
                    top, bottom = patch(neuron, places_ref)
                    field_ref[top, :] -= pair[half] * upper
                    field_ref[bottom, :] -= pair[half] * lower
            return 0

        return lax.fori_loop(0, 8, some, 0)

    lax.fori_loop(0, TX, tile, 0)


def start_field(movie_ref, field_ref):
    field_ref[0:ROW, :] = jnp.zeros((ROW, 128), F32)
    field_ref[ROW + INNER :, :] = jnp.zeros((ROW, 128), F32)

    def one(r, _):
        field_ref[pl.ds((r + 1) * ROW, ROW), :] = movie_ref[pl.ds(r * ROW, ROW), :]
        return 0

    lax.fori_loop(0, CELL_ROWS, one, 0)


def add_halo(field_ref, above_ref, below_ref, whole_ref):
    whole_ref[0 : 2 * ROW, :] = field_ref[0 : 2 * ROW, :] + above_ref[...]

    def one(r, _):
        whole_ref[pl.ds(r * ROW, ROW), :] = field_ref[pl.ds(r * ROW, ROW), :]
        return 0

    lax.fori_loop(2, CELL_ROWS, one, 0)
    whole_ref[INNER:, :] = field_ref[INNER:, :] + below_ref[...]


def pack_kernel(rows_ref, tail_ref, out_ref):
    lane = lax.broadcasted_iota(jnp.int32, (16, 128), 1)
    for a in range(8):
        parts = [rows_ref[:, d * 1024 + a * 128 : d * 1024 + a * 128 + 128] for d in range(4)]
        for b in range(4):
            shard = 4 * a + b
            dest = (shard % TX) * TA + shard // TX
            block = parts[0] if b == 0 else pltpu.roll(parts[0], (128 - 32 * b) % 128, 1)
            for d in range(1, 4):
                turned = parts[d] if d == b else pltpu.roll(parts[d], (32 * (d - b)) % 128, 1)
                block = jnp.where((lane >> 5) == d, turned, block)
            out_ref[dest, 0:16, :] = block
            out_ref[dest, 16:24, :] = tail_ref[...]


def first_kernel(activity_ref, prints_ref, places_ref, field_ref):
    field_ref[...] = jnp.zeros((FIELD, 128), F32)
    subtract_all(activity_ref, prints_ref, places_ref, field_ref)


def unpack_kernel(blocks_ref, partial_ref, movie_ref, field_ref):
    sub, lane = iotas()
    skew = (lane - 16 * sub) & 127
    turn = ((lane >> 4) - sub) & 7
    back = (lane + 16 * sub) & 127
    for r in range(CELL_ROWS):
        movie_ref[r * ROW : r * ROW + 8, :] = jnp.zeros((8, 128), F32)
        movie_ref[(r + 1) * ROW - 8 : (r + 1) * ROW, :] = jnp.zeros((8, 128), F32)

    def block(g, _):
        base = (1 + 8 * (g // TA)) * TA + g % TA
        for t in range(8):
            both = blocks_ref[g, 16 * t : 16 * t + 16, :].astype(F32)
            for h in range(2):
                value = both[8 * h : 8 * h + 8]
                value = pick_lanes(pick_rows(pick_lanes(value, skew), turn), back)
                movie_ref[pl.ds(base + (2 * t + h) * ROW, 8, stride=TA), :] = value
        return 0

    lax.fori_loop(0, GROUP, block, 0)
    field_ref[0:ROW, :] = partial_ref[0:ROW, :]
    field_ref[ROW + INNER :, :] = partial_ref[ROW + INNER :, :]

    def one(r, _):
        field_ref[pl.ds((r + 1) * ROW, ROW), :] = (
            partial_ref[pl.ds((r + 1) * ROW, ROW), :] + movie_ref[pl.ds(r * ROW, ROW), :]
        )
        return 0

    lax.fori_loop(0, CELL_ROWS, one, 0)


def update_kernel(field_ref, above_ref, below_ref, prints_ref, places_ref, out_ref, whole_ref):
    sub, lane = iotas()
    add_halo(field_ref, above_ref, below_ref, whole_ref)

    def leaf(v, m):
        folded = []
        for half in range(2):
            neuron = v * OWNED + (m // 4) * 8 + half * 4 + m % 4
            upper, lower = print_pair(prints_ref, neuron, sub, lane)
            top, bottom = patch(neuron, places_ref)
            value = upper * whole_ref[top, :] + lower * whole_ref[bottom, :]
            folded.append(value + pltpu.roll(value, 4, 0))
        return jnp.where(sub < 4, folded[0], folded[1])

    def tree(v, m, level):
        if level == 0:
            return leaf(v, m)
        shift = 1 << (level - 1)
        return merge_lanes(tree(v, m, level - 1), tree(v, m + shift, level - 1), shift, lane)

    def tile(v, _):
        total = tree(v, 0, 5)
        for g in range(GROUP):
            out_ref[g, pl.ds(pl.multiple_of(v * 8, 8), 8), :] = total
        return 0

    lax.fori_loop(0, TX, tile, 0)

    def squares(k, level):
        if level == 0:
            rows = prints_ref[pl.ds(k, 8, stride=OWNED), :]
            return rows * rows
        shift = 1 << (level - 1)
        return merge_lanes(squares(k, level - 1), squares(k + shift, level - 1), shift, lane)

    energy = squares(0, 6)
    energy = energy + pltpu.roll(energy, 64, 1)
    for g in range(GROUP):
        out_ref[g, 64:72, :] = energy


def trace_kernel(
    parts_ref, old_ref, movie_ref, prints_ref, places_ref, new_ref, weight_ref, field_ref
):
    sub, lane = iotas()
    start_field(movie_ref, field_ref)

    def total(start):
        rows = pl.ds(start, 8)
        value = parts_ref[0, rows, :]
        for g in range(1, GROUP):
            value = value + parts_ref[g, rows, :]
        return value

    energy = total(64)
    m = lane & 31
    own = (m >> 2) * 8 + (m & 3) + jnp.where(sub < 4, 0, 4)
    for v in range(TX):
        scale = pick_lanes(jnp.broadcast_to(energy[v : v + 1], (8, 128)), own)
        value = jnp.maximum(old_ref[v] + total(8 * v) / (scale + RIDGE), 0.0)
        new_ref[v] = value
        power = value * value
        power = power + pltpu.roll(power, 64, 1)
        power = power + pltpu.roll(power, 32, 1)
        power = merge_rows(power, power, 1, sub)
        power = merge_rows(power, power, 2, sub)
        weight_ref[v] = value / (power + RIDGE)
    subtract_all(new_ref, prints_ref, places_ref, field_ref)


def improve_prints(field_ref, above_ref, below_ref, weight_ref, prints_ref, places_ref, whole_ref, new_ref):
    sub, lane = iotas()
    add_halo(field_ref, above_ref, below_ref, whole_ref)

    def tile(v, _):
        value = weight_ref[v]

        def eight(q, _):
            base = pl.multiple_of(v * OWNED + q * 8, 8)
            folded = []
            for b in range(4):
                pair = spread(value, q * 4 + b, sub, lane)
                sides = []
                for half in range(2):
                    top, bottom = patch(base + half * 4 + b, places_ref)
                    sides.append(
                        merge_lanes(pair[half] * whole_ref[top, :], pair[half] * whole_ref[bottom, :], 64, lane)
                    )
                folded.append(merge_lanes(sides[0], sides[1], 32, lane))
            low = merge_rows(folded[0], folded[1], 1, sub)
            high = merge_rows(folded[2], folded[3], 1, sub)
            step = merge_rows(low, high, 2, sub)
            turned = pltpu.roll(step, 4, 0)
            dx = (lane & 32) != 0
            swapped = jnp.where(dx, pltpu.roll(turned, 32, 1), pltpu.roll(turned, 96, 1))
            step = jnp.where(dx == (sub >= 4), step, swapped)
            new_ref[pl.ds(base, 8), :] = jnp.maximum(prints_ref[pl.ds(base, 8), :] + step, 0.0)
            return 0

        return lax.fori_loop(0, 8, eight, 0)

    lax.fori_loop(0, TX, tile, 0)


def print_kernel(
    field_ref, above_ref, below_ref, weight_ref, activity_ref, movie_ref, prints_ref, places_ref,
    new_ref, next_ref, whole_ref,
):
    improve_prints(field_ref, above_ref, below_ref, weight_ref, prints_ref, places_ref, whole_ref, new_ref)
    start_field(movie_ref, next_ref)
    subtract_all(activity_ref, new_ref, places_ref, next_ref)


def last_kernel(
    field_ref, above_ref, below_ref, weight_ref, prints_ref, places_ref, out_ref, whole_ref, new_ref
):
    improve_prints(field_ref, above_ref, below_ref, weight_ref, prints_ref, places_ref, whole_ref, new_ref)
    for j in range(TX):
        rows = new_ref[j * OWNED : (j + 1) * OWNED, :]
        for z in range(TA):
            out_ref[j * TA + z] = rows


def finish_kernel(blocks_ref, out_ref):
    lane = lax.broadcasted_iota(jnp.int32, (OWNED, 128), 1)
    for z in range(TA):
        for a in range(2):
            parts = [blocks_ref[(4 * a + b) * TA + z] for b in range(4)]
            for d in range(4):
                row = parts[0] if d == 0 else pltpu.roll(parts[0], (128 - 32 * d) % 128, 1)
                for b in range(1, 4):
                    turned = parts[b] if b == d else pltpu.roll(parts[b], (32 * (b - d)) % 128, 1)
                    row = jnp.where((lane >> 5) == b, turned, row)
                start = d * 1024 + (z * 2 + a) * 128
                out_ref[:, start : start + 128] = row


def shape(*sizes, dtype=F32):
    return jax.ShapeDtypeStruct(sizes, dtype)


def call(kernel, outs, places, scratch=(), smem=None):
    return pl.pallas_call(
        kernel,
        out_shape=outs,
        in_specs=[SMEM if at == smem else VMEM for at in range(places)],
        out_specs=jax.tree.map(lambda _: VMEM, outs),
        scratch_shapes=list(scratch),
    )


FIELD_SHAPE = shape(FIELD, 128)
WHOLE = pltpu.VMEM((FIELD, 128), F32)
AXES = ("tx", "ta")


def exchange(blocks):
    return lax.all_to_all(blocks, AXES, 0, 0, tiled=True)


def halo(field):
    ends = lax.axis_size("ty") - 1
    above = lax.ppermute(field[INNER:], "ty", [(i, i + 1) for i in range(ends)])
    below = lax.ppermute(field[: 2 * ROW], "ty", [(i + 1, i) for i in range(ends)])
    return above, below


def shards(movie, footprints, traces, anchor_row, anchor_col):
    layer = lax.axis_index("ta")
    column = lax.axis_index("tx")
    frames = traces.shape[0]
    cells = movie.reshape(frames, 4, CELL_ROWS, TX, 2, 128).transpose(3, 1, 2, 0, 4, 5)
    movie_blocks = exchange(cells.reshape(GROUP, 128, 128))

    own = traces.reshape(frames, 8, 2, 4).transpose(2, 0, 1, 3).reshape(2, 128)
    anchors = jnp.concatenate([anchor_row, anchor_col]).astype(F32).reshape(1, 128)
    tail = jnp.concatenate([own, anchors, jnp.zeros((5, 128), F32)])
    rows = lax.dynamic_slice_in_dim(footprints, layer * 16, 16, axis=0)
    sent = call(pack_kernel, shape(GROUP, 24, 128), 2)(rows, tail)
    got = exchange(sent)
    prints = got[:, :16].reshape(COUNT, 128)
    activity = got[:, 16:18].reshape(TX, TA, 2, 128).transpose(0, 2, 1, 3).reshape(TX, 8, 128)
    spots = got.reshape(TX, TA, 24, 128)[:, 0, 18].astype(jnp.int32)
    tiles = jnp.arange(TX, dtype=jnp.int32)[:, None] * 8
    places = ((spots[:, :64] + 1) * ROW + (tiles + spots[:, 64:] + 1) * TA).reshape(COUNT)

    partial = call(first_kernel, FIELD_SHAPE, 3, smem=2)(activity, prints, places)
    cells, field = call(unpack_kernel, (shape(INNER, 128), FIELD_SHAPE), 2)(movie_blocks, partial)
    for sweep in range(ITERS):
        above, below = halo(field)
        sums = call(update_kernel, shape(GROUP, 72, 128), 5, (WHOLE,), smem=4)(
            field, above, below, prints, places
        )
        parts = exchange(sums)
        activity, weight, field = call(
            trace_kernel, (shape(TX, 8, 128), shape(TX, 8, 128), FIELD_SHAPE), 5, smem=4
        )(parts, activity, cells, prints, places)
        above, below = halo(field)
        if sweep + 1 < ITERS:
            prints, field = call(print_kernel, (shape(COUNT, 128), FIELD_SHAPE), 8, (WHOLE,), smem=7)(
                field, above, below, weight, activity, cells, prints, places
            )
        else:
            sent = call(
                last_kernel, shape(GROUP, OWNED, 128), 6, (WHOLE, pltpu.VMEM((COUNT, 128), F32)), smem=5
            )(field, above, below, weight, prints, places)
    footprints_out = call(finish_kernel, shape(OWNED, 4096), 1)(exchange(sent))
    mine = lax.dynamic_index_in_dim(activity, column, 0, keepdims=False).reshape(2, TA, 128)
    mine = lax.dynamic_index_in_dim(mine, layer, 1, keepdims=False)
    traces_out = mine.reshape(2, frames, 8, 4).transpose(1, 2, 0, 3).reshape(frames, OWNED)
    return footprints_out, traces_out


def solution(mesh):
    placed = (
        P("ta", None, "ty", "tx"),
        P(("ty", "tx"), None),
        P("ta", ("ty", "tx")),
        P(("ty", "tx")),
        P(("ty", "tx")),
    )
    return jax.shard_map(
        shards,
        mesh=mesh,
        in_specs=placed,
        out_specs=(P(("ty", "tx"), None), P("ta", ("ty", "tx"))),
        check_vma=False,
    )
```

time: 627 us -> 263 us (0.42); the launches traced: 614 us -> 261 us
  local copies, waits for them, and re-layouts: 188 us -> 16.5 us
  waiting for transfers between devices: 191 us -> 32.7 us
  Pallas kernels: 0 us -> 119 us
  other arithmetic: 97.1 us -> 1.49 us
  matrix products: 46.2 us -> 0 us
  blocking collectives: 17.6 us -> 40.3 us
  between operations: 15.3 us -> 0.84 us
  starting transfers between devices: 58.3 us -> 50 us
    pallas_call x0 -> x10, Pallas kernels: none -> 119 us  [the longest x1 31.5 us: shards(): call(print_kernel, (shape(COUNT, 128), FIELD_SHAPE), 8, (WHOLE,), smem=7)]
    ppermute x20 -> x8, waiting for transfers between devices: 122 us -> 13.5 us  [the longest x4 8.8 us: halo(): lax.ppermute(field[:2 * ROW], 'ty', [(i + 1, i) for i in range(ends)])]
    psum x2 -> x0, waiting for transfers between devices: 69 us -> none  [shards(): numerator, strength = lax.psum((numer_part, strength_part), 'ta')]
    unnamed x58 -> x24, local copies, waits for them, and re-layouts: 56.6 us -> 4.79 us
    dot_general x4 -> x0, matrix products: 46.2 us -> none  [the longest x2 30.3 us: shards(): jnp.einsum('kse,ksfe->fk', shaped, gathered, precision=lax.Precision.HIGH...]
    scatter-add x20 -> x0, other arithmetic: 45.7 us -> none  [the longest x4 36.2 us: patch_residue(): jax.ops.segment_sum(products.reshape(owned * 4, -1), cell_ids, num_segmen...]
    reshape x7, local copies, waits for them, and re-layouts: 48.3 us -> 5.17 us  [the longest x1 2.08 us: shards(): movie.reshape(frames, 4, CELL_ROWS, TX, 2, 128).transpose(3, 1, 2, 0, 4, 5)]
    all_to_all x0 -> x2, blocking collectives: none -> 40.3 us  [exchange(): return lax.all_to_all(blocks, AXES, 0, 0, tiled=True)]
  transfers between devices with their start and end apart: 22 -> 11, of which waited for: 15 -> 11; matrix products, arithmetic and copies ran while one was open for 14% -> 2% of each run, Pallas kernels for 0% -> 4%
where the time goes in v1:
time: 263 us; the launch traced here: 261 us
  Pallas kernels  119 us (45%)
  starting transfers between devices  50 us (19%)
  blocking collectives  40.3 us (15%)
  waiting for transfers between devices  32.7 us (12%)
  local copies, waits for them, and re-layouts  16.5 us (6%)
    all_to_all x2, blocking collectives, exchange(): return lax.all_to_all(blocks, AXES, 0, 0, tiled=True)  40.3 us
    pallas_call x1, Pallas kernels, shards(): call(print_kernel, (shape(COUNT, 128), FIELD_SHAPE), 8, (WHOLE,), smem=7)  31.5 us
    pallas_call x2, Pallas kernels, shards(): call(trace_kernel, (shape(TX, 8, 128), shape(TX, 8, 128), FIELD_SHAPE), 5...  23 us
    pallas_call x1, Pallas kernels, shards(): call(last_kernel, shape(GROUP, OWNED, 128), 6, (WHOLE, pltpu.VMEM((COUNT,...  22.7 us
    ppermute x4, starting transfers between devices, halo(): above = lax.ppermute(field[INNER:], 'ty', [(i, i + 1) for i in range(ends)])  21.4 us
    all_to_all x3, waiting for transfers between devices, exchange(): return lax.all_to_all(blocks, AXES, 0, 0, tiled=True)  19.2 us
    all_to_all x3, starting transfers between devices, exchange(): return lax.all_to_all(blocks, AXES, 0, 0, tiled=True)  18 us
    pallas_call x2, Pallas kernels, shards(): call(update_kernel, shape(GROUP, 72, 128), 5, (WHOLE,), smem=4)  17.2 us
  transfers between devices with their start and end apart: 11, of which 11 were waited for; matrix products, arithmetic and copies ran while one was open for 2% of the time, Pallas kernels for 4%

profile of v1, /device:TPU:1, one launch (start us, length us, event | category | flops | bytes accessed | tf_op | source)
XLA Modules:
  0.0 260.8 jit_solution(4480302089356571655)
XLA Ops:
  0.6 0.0 copy-start
  0.6 0.0 copy-start.3
  0.7 0.9 reshape.80
  1.6 0.1 reshape.81
  1.7 0.8 add_convert_fusion
  2.5 0.1 pad.2.clone
  2.5 0.0 copy-done
  2.5 0.7 constant_dynamic-slice_fusion.1.rows_ref
  3.3 0.7 maximum_maximum_fusion.tail_ref
  3.9 2.0 shard_map.68
  5.9 9.8 %all-to-all-start.1 = ((f32[32,24,128]{2,1,0:T(8,128)}), f32[32,24,128]{2,1,0:T(8,128)S(1)}, u32[]{:S(2)}, u32[]{:S(2)}) async-start(f32[32,24,128]{2,1,0:T(8,128)} %shard_map.68), calls=%async_computation.1 | async-start | bytes 786432 | tf_op jit(solution)/shard_map/all_to_all | solution.py:328
  15.7 0.0 copy-done.3
  15.7 2.1 copy.14
  17.8 6.5 %all-to-all-done.1 = f32[32,24,128]{2,1,0:T(8,128)S(1)} async-done(((f32[32,24,128]{2,1,0:T(8,128)}), f32[32,24,128]{2,1,0:T(8,128)S(1)}, u32[]{:S(2)}, u32[]{:S(2)}) %all-to-all-start.1) | async-done | bytes 393248 | tf_op jit(solution)/shard_map/all_to_all | solution.py:328
  24.3 4.2 %all-to-all-start = ((bf16[32,128,128]{2,1,0:T(8,128)(2,1)}), bf16[32,128,128]{2,1,0:T(8,128)(2,1)S(1)}, u32[]{:S(2)}, u32[]{:S(2)}) async-start(bf16[32,128,128]{2,1,0:T(8,128)(2,1)} %bitcast.2), calls=%async_computation | async-start | bytes 2097152 | tf_op jit(solution)/shard_map/all_to_all | solution.py:328
  28.6 0.1 multiply_add_fusion
  28.7 0.7 reshape.86.places_ref
  29.4 0.6 copy.16
  30.0 0.7 slice.53
  30.7 10.1 %shard_map.69.partial_ref = f32[4752,128]{1,0:T(8,128)} custom-call(f32[8,8,128]{2,1,0:T(8,128)} %bitcast.24, f32[512,128]{1,0:T(8,128)} %bitcast.18, s32[512]{0:T(512)} %reshape.86.places_ref), custom_call_target="tpu_custom_call" | custom-call | tf_op jit(solution)/shard_map/pallas_call | solution.py:357
  40.8 2.2 all-to-all-done.blocks_ref
  43.0 1.0 copy-done.2
  44.0 9.4 %shard_map.70 = (f32[4224,128]{1,0:T(8,128)}, f32[4752,128]{1,0:T(8,128)}) custom-call(bf16[32,128,128]{2,1,0:T(8,128)(2,1)} %copy-done.2, f32[4752,128]{1,0:T(8,128)} %shard_map.69.partial_ref), custom_call_target="tpu_custom_call" | custom-call | tf_op jit(solution)/shard_map/pallas_call | solution.py:358
  53.4 1.1 fusion.3
  54.5 4.9 %collective-permute-start.1 = (f32[528,128]{1,0:T(8,128)S(1)}, f32[528,128]{1,0:T(8,128)S(1)}, u32[]{:S(2)}, u32[]{:S(2)}) collective-permute-start(f32[528,128]{1,0:T(8,128)S(1)} %get-tuple-element.28), channel_id=1, source_target_pairs={{32,0},{64,32},{96,64},{33,1},{65,33},{97,65},{34,2},{66,34},{98,6... | collective-permute-start | bytes 811016 | tf_op jit(solution)/shard_map/ppermute | solution.py:334
  59.4 4.3 %collective-permute-start = (f32[528,128]{1,0:T(8,128)S(1)}, f32[528,128]{1,0:T(8,128)S(1)}, u32[]{:S(2)}, u32[]{:S(2)}) collective-permute-start(f32[528,128]{1,0:T(8,128)S(1)} %get-tuple-element.29), channel_id=1, source_target_pairs={{0,32},{32,64},{64,96},{1,33},{33,65},{65,97},{2,34},{34,66},{66,9... | collective-permute-start | bytes 811016 | tf_op jit(solution)/shard_map/ppermute | solution.py:333
  63.7 2.2 collective-permute-done.1.below_ref
  65.9 1.2 collective-permute-done.above_ref
  67.0 0.0 copy-done.8
  67.0 0.7 copy-done.11
  67.7 8.6 %shard_map.71 = f32[32,72,128]{2,1,0:T(8,128)} custom-call(f32[4752,128]{1,0:T(8,128)} %get-tuple-element.12.field_ref, f32[528,128]{1,0:T(8,128)} %copy-done.11, f32[528,128]{1,0:T(8,128)} %copy-done.8, f32[512,128]{1,0:T(8,128)} %bitcast.19, s32[512]{0:T(512)} %reshape.86.places_ref), custom_call_target="tpu_custom_call" | custom-call | tf_op jit(solution)/shard_map/pallas_call | solution.py:361
  76.4 21.4 %all_to_all.25.parts_ref = f32[32,72,128]{2,1,0:T(8,128)} all-to-all(f32[32,72,128]{2,1,0:T(8,128)} %shard_map.71), channel_id=1, replica_groups=mesh['ty'=4,'tx'=8,'ta'=4] {'tx','ta'}, dimensions={0} | all-to-all | bytes 2359296 | tf_op jit(solution)/shard_map/all_to_all | solution.py:328
  97.8 11.5 %shard_map.72 = (f32[8,8,128]{2,1,0:T(8,128)}, f32[8,8,128]{2,1,0:T(8,128)}, f32[4752,128]{1,0:T(8,128)}) custom-call(f32[32,72,128]{2,1,0:T(8,128)} %all_to_all.25.parts_ref, f32[8,8,128]{2,1,0:T(8,128)} %bitcast.25, f32[4224,128]{1,0:T(8,128)} %get-tuple-element.13.movie_ref, f32[512,128]{1,0:T(8,128)} %bitcast.20, s32[512]{0:T(512)} %reshape.86.places_ref), custom_call_target="tpu_custom_call" | custom-call | tf_op jit(solution)/shard_map/pallas_call | solution.py:365
  109.3 1.1 fusion.2
  110.4 1.9 collective-permute-start.3
  112.3 5.1 %collective-permute-start.2 = (f32[528,128]{1,0:T(8,128)S(1)}, f32[528,128]{1,0:T(8,128)S(1)}, u32[]{:S(2)}, u32[]{:S(2)}) collective-permute-start(f32[528,128]{1,0:T(8,128)S(1)} %get-tuple-element.27), channel_id=1, source_target_pairs={{0,32},{32,64},{64,96},{1,33},{33,65},{65,97},{2,34},{34,66},{66,9... | collective-permute-start | bytes 811016 | tf_op jit(solution)/shard_map/ppermute | solution.py:333
  117.5 2.2 collective-permute-done.3.below_ref
  119.7 1.2 collective-permute-done.2.above_ref
  120.8 0.7 copy-done.5
  121.5 31.5 %shard_map.73 = (f32[512,128]{1,0:T(8,128)}, f32[4752,128]{1,0:T(8,128)}) custom-call(f32[4752,128]{1,0:T(8,128)} %get-tuple-element.14.field_ref, f32[528,128]{1,0:T(8,128)} %copy-done.5, f32[528,128]{1,0:T(8,128)} %copy-done.4, f32[8,8,128]{2,1,0:T(8,128)} %get-tuple-element.15.weight_ref, f32[8,8,128]{2,1,0:T(8,128)} %get-tuple-element.16.activity_ref.old_ref, ...), custom_call_target="tpu_custom_call" | custom-call | tf_op jit(solution)/shard_map/pallas_call | solution.py:370
  153.0 1.1 fusion.1
  154.1 1.9 collective-permute-start.5
  156.0 5.9 %collective-permute-start.4 = (f32[528,128]{1,0:T(8,128)S(1)}, f32[528,128]{1,0:T(8,128)S(1)}, u32[]{:S(2)}, u32[]{:S(2)}) collective-permute-start(f32[528,128]{1,0:T(8,128)S(1)} %get-tuple-element.25), channel_id=1, source_target_pairs={{0,32},{32,64},{64,96},{1,33},{33,65},{65,97},{2,34},{34,66},{66,9... | collective-permute-start | bytes 811016 | tf_op jit(solution)/shard_map/ppermute | solution.py:333
  162.0 2.2 collective-permute-done.5.below_ref
  164.2 1.2 collective-permute-done.4.above_ref
  165.3 0.7 copy-done.10
  166.0 8.6 %shard_map.74 = f32[32,72,128]{2,1,0:T(8,128)} custom-call(f32[4752,128]{1,0:T(8,128)} %get-tuple-element.17.field_ref, f32[528,128]{1,0:T(8,128)} %copy-done.10, f32[528,128]{1,0:T(8,128)} %copy-done.7, f32[512,128]{1,0:T(8,128)} %get-tuple-element.18.prints_ref, s32[512]{0:T(512)} %reshape.86.places_ref), custom_call_target="tpu_custom_call" | custom-call | tf_op jit(solution)/shard_map/pallas_call | solution.py:361
  174.7 18.9 %all_to_all.26.parts_ref = f32[32,72,128]{2,1,0:T(8,128)} all-to-all(f32[32,72,128]{2,1,0:T(8,128)} %shard_map.74), channel_id=1, replica_groups=mesh['ty'=4,'tx'=8,'ta'=4] {'tx','ta'}, dimensions={0} | all-to-all | bytes 2359296 | tf_op jit(solution)/shard_map/all_to_all | solution.py:328
  193.6 11.5 %shard_map.75 = (f32[8,8,128]{2,1,0:T(8,128)}, f32[8,8,128]{2,1,0:T(8,128)}, f32[4752,128]{1,0:T(8,128)}) custom-call(f32[32,72,128]{2,1,0:T(8,128)} %all_to_all.26.parts_ref, f32[8,8,128]{2,1,0:T(8,128)} %get-tuple-element.16.activity_ref.old_ref, f32[4224,128]{1,0:T(8,128)} %get-tuple-element.13.movie_ref, f32[512,128]{1,0:T(8,128)} %get-tuple-element.18.prints_ref, ...), custom_call_target="tpu_custom_call" | custom-call | tf_op jit(solution)/shard_map/pallas_call | solution.py:365
  205.0 1.1 fusion
  206.1 1.9 collective-permute-start.7
  208.0 6.0 %collective-permute-start.6 = (f32[528,128]{1,0:T(8,128)S(1)}, f32[528,128]{1,0:T(8,128)S(1)}, u32[]{:S(2)}, u32[]{:S(2)}) collective-permute-start(f32[528,128]{1,0:T(8,128)S(1)} %get-tuple-element.23), channel_id=1, source_target_pairs={{0,32},{32,64},{64,96},{1,33},{33,65},{65,97},{2,34},{34,66},{66,9... | collective-permute-start | bytes 811016 | tf_op jit(solution)/shard_map/ppermute | solution.py:333
  214.1 2.2 collective-permute-done.7.below_ref
  216.3 1.2 collective-permute-done.6.above_ref
  217.5 0.0 copy-done.6
  217.5 0.7 copy-done.9
  218.2 22.7 %shard_map.76 = f32[32,64,128]{2,1,0:T(8,128)} custom-call(f32[4752,128]{1,0:T(8,128)} %get-tuple-element.19.field_ref, f32[528,128]{1,0:T(8,128)} %copy-done.9, f32[528,128]{1,0:T(8,128)} %copy-done.6, f32[8,8,128]{2,1,0:T(8,128)} %get-tuple-element.20.weight_ref, f32[512,128]{1,0:T(8,128)} %get-tuple-element.18.prints_ref, s32[512]{0:T(512)} %reshape.86.places_ref), custom_call_target="tpu_custom_call" | custom-call | tf_op jit(solution)/shard_map/pallas_call | solution.py:374
  240.9 3.9 %all-to-all-start.4 = ((f32[32,64,128]{2,1,0:T(8,128)}), f32[32,64,128]{2,1,0:T(8,128)S(1)}, u32[]{:S(2)}, u32[]{:S(2)}) async-start(f32[32,64,128]{2,1,0:T(8,128)} %shard_map.76), calls=%async_computation.4 | async-start | bytes 2097152 | tf_op jit(solution)/shard_map/all_to_all | solution.py:328
  244.8 0.7 constant_dynamic-slice_fusion
  245.5 0.1 reshape.88
  245.7 0.7 reshape.89
  246.4 10.4 %all-to-all-done.4.blocks_ref = f32[32,64,128]{2,1,0:T(8,128)S(1)} async-done(((f32[32,64,128]{2,1,0:T(8,128)}), f32[32,64,128]{2,1,0:T(8,128)S(1)}, u32[]{:S(2)}, u32[]{:S(2)}) %all-to-all-start.4) | async-done | bytes 1048608 | tf_op jit(solution)/shard_map/all_to_all | solution.py:328
  256.8 1.0 copy-done.1
  257.8 3.1 %shard_map.77 = f32[64,4096]{1,0:T(8,128)} custom-call(f32[32,64,128]{2,1,0:T(8,128)} %copy-done.1), custom_call_target="tpu_custom_call" | custom-call | tf_op jit(solution)/shard_map/pallas_call | solution.py:377
  (19 shorter events, 0.1 us)
Async XLA Ops:
  0.6 1.9 copy-start
  0.6 15.1 %copy-start.3 = (bf16[4,4,256,128]{3,2,1,0:T(8,128)(2,1)S(1)}, bf16[4,4,256,128]{3,2,1,0:T(8,128)(2,1)}, u32[]{:S(2)}) copy-start(bf16[4,4,256,128]{3,2,1,0:T(8,128)(2,1)} %param.5) | copy-start | bytes 3145732
  5.9 18.4 %all-to-all-start.1 = ((f32[32,24,128]{2,1,0:T(8,128)}), f32[32,24,128]{2,1,0:T(8,128)S(1)}, u32[]{:S(2)}, u32[]{:S(2)}) async-start(f32[32,24,128]{2,1,0:T(8,128)} %shard_map.68), calls=%async_computation.1 | async-start | bytes 786432 | tf_op jit(solution)/shard_map/all_to_all | solution.py:328
  24.3 18.7 %all-to-all-start = ((bf16[32,128,128]{2,1,0:T(8,128)(2,1)}), bf16[32,128,128]{2,1,0:T(8,128)(2,1)S(1)}, u32[]{:S(2)}, u32[]{:S(2)}) async-start(bf16[32,128,128]{2,1,0:T(8,128)(2,1)} %bitcast.2), calls=%async_computation | async-start | bytes 2097152 | tf_op jit(solution)/shard_map/all_to_all | solution.py:328
  43.0 1.0 copy-start.2
  54.5 11.4 %collective-permute-start.1 = (f32[528,128]{1,0:T(8,128)S(1)}, f32[528,128]{1,0:T(8,128)S(1)}, u32[]{:S(2)}, u32[]{:S(2)}) collective-permute-start(f32[528,128]{1,0:T(8,128)S(1)} %get-tuple-element.28), channel_id=1, source_target_pairs={{32,0},{64,32},{96,64},{33,1},{65,33},{97,65},{34,2},{66,34},{98,6... | collective-permute-start | bytes 811016 | tf_op jit(solution)/shard_map/ppermute | solution.py:334
  59.4 7.6 %collective-permute-start = (f32[528,128]{1,0:T(8,128)S(1)}, f32[528,128]{1,0:T(8,128)S(1)}, u32[]{:S(2)}, u32[]{:S(2)}) collective-permute-start(f32[528,128]{1,0:T(8,128)S(1)} %get-tuple-element.29), channel_id=1, source_target_pairs={{0,32},{32,64},{64,96},{1,33},{33,65},{65,97},{2,34},{34,66},{66,9... | collective-permute-start | bytes 811016 | tf_op jit(solution)/shard_map/ppermute | solution.py:333
  65.9 1.2 copy-start.8
  67.0 0.7 copy-start.11
  110.4 9.3 %collective-permute-start.3 = (f32[528,128]{1,0:T(8,128)S(1)}, f32[528,128]{1,0:T(8,128)S(1)}, u32[]{:S(2)}, u32[]{:S(2)}) collective-permute-start(f32[528,128]{1,0:T(8,128)S(1)} %get-tuple-element.26), channel_id=1, source_target_pairs={{32,0},{64,32},{96,64},{33,1},{65,33},{97,65},{34,2},{66,34},{98,6... | collective-permute-start | bytes 811016 | tf_op jit(solution)/shard_map/ppermute | solution.py:334
  112.3 8.5 %collective-permute-start.2 = (f32[528,128]{1,0:T(8,128)S(1)}, f32[528,128]{1,0:T(8,128)S(1)}, u32[]{:S(2)}, u32[]{:S(2)}) collective-permute-start(f32[528,128]{1,0:T(8,128)S(1)} %get-tuple-element.27), channel_id=1, source_target_pairs={{0,32},{32,64},{64,96},{1,33},{33,65},{65,97},{2,34},{34,66},{66,9... | collective-permute-start | bytes 811016 | tf_op jit(solution)/shard_map/ppermute | solution.py:333
  119.7 1.2 copy-start.4
  120.8 0.7 copy-start.5
  154.1 10.1 %collective-permute-start.5 = (f32[528,128]{1,0:T(8,128)S(1)}, f32[528,128]{1,0:T(8,128)S(1)}, u32[]{:S(2)}, u32[]{:S(2)}) collective-permute-start(f32[528,128]{1,0:T(8,128)S(1)} %get-tuple-element.24), channel_id=1, source_target_pairs={{32,0},{64,32},{96,64},{33,1},{65,33},{97,65},{34,2},{66,34},{98,6... | collective-permute-start | bytes 811016 | tf_op jit(solution)/shard_map/ppermute | solution.py:334
  156.0 9.3 %collective-permute-start.4 = (f32[528,128]{1,0:T(8,128)S(1)}, f32[528,128]{1,0:T(8,128)S(1)}, u32[]{:S(2)}, u32[]{:S(2)}) collective-permute-start(f32[528,128]{1,0:T(8,128)S(1)} %get-tuple-element.25), channel_id=1, source_target_pairs={{0,32},{32,64},{64,96},{1,33},{33,65},{65,97},{2,34},{34,66},{66,9... | collective-permute-start | bytes 811016 | tf_op jit(solution)/shard_map/ppermute | solution.py:333
  164.2 1.2 copy-start.7
  165.3 0.7 copy-start.10
  206.1 10.2 %collective-permute-start.7 = (f32[528,128]{1,0:T(8,128)S(1)}, f32[528,128]{1,0:T(8,128)S(1)}, u32[]{:S(2)}, u32[]{:S(2)}) collective-permute-start(f32[528,128]{1,0:T(8,128)S(1)} %get-tuple-element.22), channel_id=1, source_target_pairs={{32,0},{64,32},{96,64},{33,1},{65,33},{97,65},{34,2},{66,34},{98,6... | collective-permute-start | bytes 811016 | tf_op jit(solution)/shard_map/ppermute | solution.py:334
  208.0 9.4 %collective-permute-start.6 = (f32[528,128]{1,0:T(8,128)S(1)}, f32[528,128]{1,0:T(8,128)S(1)}, u32[]{:S(2)}, u32[]{:S(2)}) collective-permute-start(f32[528,128]{1,0:T(8,128)S(1)} %get-tuple-element.23), channel_id=1, source_target_pairs={{0,32},{32,64},{64,96},{1,33},{33,65},{65,97},{2,34},{34,66},{66,9... | collective-permute-start | bytes 811016 | tf_op jit(solution)/shard_map/ppermute | solution.py:333
  216.3 1.2 copy-start.6
  217.5 0.7 copy-start.9
  240.9 15.9 %all-to-all-start.4 = ((f32[32,64,128]{2,1,0:T(8,128)}), f32[32,64,128]{2,1,0:T(8,128)S(1)}, u32[]{:S(2)}, u32[]{:S(2)}) async-start(f32[32,64,128]{2,1,0:T(8,128)} %shard_map.76), calls=%async_computation.4 | async-start | bytes 2097152 | tf_op jit(solution)/shard_map/all_to_all | solution.py:328
  256.8 1.0 copy-start.1

commit v2 on v1

v2 whole, which is shorter than its diff:
```python
import functools

import jax
import jax.numpy as jnp
from jax import lax
from jax.experimental import pallas as pl
from jax.experimental.pallas import tpu as pltpu
from jax.sharding import PartitionSpec as P

ITERS = 2
RIDGE = 1.0
TX = 8
TA = 4
GROUP = TX * TA
OWNED = 64
COUNT = TX * OWNED
ROW = (TX * 8 + 2) * TA
CELL_ROWS = 16
FIELD = (CELL_ROWS + 2) * ROW
INNER = CELL_ROWS * ROW
VMEM = pl.BlockSpec(memory_space=pltpu.VMEM)
SMEM = pl.BlockSpec(memory_space=pltpu.SMEM)
F32 = jnp.float32


def iotas():
    return (
        lax.broadcasted_iota(jnp.int32, (8, 128), 0),
        lax.broadcasted_iota(jnp.int32, (8, 128), 1),
    )


def pick_lanes(value, index):
    return jnp.take_along_axis(value, index, axis=1, mode="promise_in_bounds")


def pick_rows(value, index):
    return jnp.take_along_axis(value, index, axis=0, mode="promise_in_bounds")


def merge_lanes(first, second, shift, lane):
    if shift == 64:
        high = lane >= 64
        return jnp.where(high, second, first) + pltpu.roll(jnp.where(high, first, second), 64, 1)
    return jnp.where(
        (lane & shift) != 0,
        second + pltpu.roll(second, shift, 1),
        first + pltpu.roll(first, 128 - shift, 1),
    )


def merge_rows(first, second, shift, sub):
    return jnp.where(
        (sub & shift) != 0,
        second + pltpu.roll(second, shift, 0),
        first + pltpu.roll(first, 8 - shift, 0),
    )


def spread(value, m, sub, lane):
    wide = pick_lanes(value, (lane & 96) + m)
    turned = pltpu.roll(wide, 4, 0)
    low = sub < 4
    return jnp.where(low, wide, turned), jnp.where(low, turned, wide)


def widen(prints, wide_ref):
    source = lax.broadcasted_iota(jnp.int32, (128, 512), 0)
    target = lax.broadcasted_iota(jnp.int32, (128, 512), 1)
    copies = (source == (target >> 7) * 32 + (target & 31)).astype(F32)
    wide = jnp.dot(prints, copies, precision=lax.Precision.HIGHEST, preferred_element_type=F32)
    for d in range(4):
        wide_ref[d] = wide[:, 128 * d : 128 * d + 128]


def print_pair(wide_ref, neuron, sub):
    rows = [jnp.broadcast_to(wide_ref[d, pl.ds(neuron, 1), :], (8, 128)) for d in range(4)]
    return jnp.where(sub < 4, rows[0], rows[1]), jnp.where(sub < 4, rows[2], rows[3])


def patch(v, k, places_ref):
    start = pl.multiple_of(places_ref[v, k], 4)
    return pl.ds(start, 8), pl.ds(start + ROW, 8)


def subtract_all(activity_ref, wide_ref, places_ref, field_ref):
    sub, lane = iotas()
    for first in range(2):
        tiles = [first + 2 * t for t in range(4)]
        values = [activity_ref[v] for v in tiles]

        def some(mh, _):
            for ml in range(4):
                pairs = [spread(value, mh * 4 + ml, sub, lane) for value in values]
                for half in range(2):
                    spots, changed = [], []
                    for v, pair in zip(tiles, pairs):
                        k = mh * 8 + half * 4 + ml
                        for at, side in zip(patch(v, k, places_ref), print_pair(wide_ref, v * OWNED + k, sub)):
                            spots.append(at)
                            changed.append(field_ref[at, :] - pair[half] * side)
                    for at, value in zip(spots, changed):
                        field_ref[at, :] = value
            return 0

        lax.fori_loop(0, 8, some, 0)


def start_field(movie_ref, field_ref):
    field_ref[0:ROW, :] = jnp.zeros((ROW, 128), F32)
    field_ref[ROW + INNER :, :] = jnp.zeros((ROW, 128), F32)

    def one(r, _):
        field_ref[pl.ds((r + 1) * ROW, ROW), :] = movie_ref[pl.ds(r * ROW, ROW), :]
        return 0

    lax.fori_loop(0, CELL_ROWS, one, 0)


def add_halo(field_ref, above_ref, below_ref):
    field_ref[0 : 2 * ROW, :] += above_ref[...]
    field_ref[INNER:, :] += below_ref[...]


def show_edges(field_ref, up_ref, down_ref):
    up_ref[...] = field_ref[0 : 2 * ROW, :]
    down_ref[...] = field_ref[INNER:, :]


def thirds(value):
    high = value.astype(jnp.bfloat16)
    rest = value - high.astype(F32)
    middle = rest.astype(jnp.bfloat16)
    return high, middle, (rest - middle.astype(F32)).astype(jnp.bfloat16)


def pack_kernel(cells_ref, prints_ref, traces_ref, row_ref, col_ref, layer_ref, out_ref):
    lane = lax.broadcasted_iota(jnp.int32, (16, 128), 1)
    rows = pl.ds(pl.multiple_of(layer_ref[0] * 16, 16), 16)
    tail = [piece.astype(F32) for piece in thirds(traces_ref[...])]
    tail = jnp.concatenate(tail + [row_ref[...].astype(F32), col_ref[...].astype(F32), jnp.zeros((2, OWNED), F32)], axis=0)
    tail = jnp.concatenate([tail, jnp.zeros((16, 128 - OWNED), F32)], axis=1).astype(jnp.bfloat16)
    for a in range(8):
        blocks = swap_lanes(
            [prints_ref[rows, d * 1024 + a * 128 : d * 1024 + a * 128 + 128] for d in range(4)], lane
        )
        for b in range(4):
            shard = 4 * a + b
            dest = (shard % TX) * TA + shard // TX
            out_ref[dest, 0:128, :] = cells_ref[dest]
            for at, piece in enumerate(thirds(blocks[b])):
                out_ref[dest, 128 + 16 * at : 144 + 16 * at, :] = piece
            out_ref[dest, 176:192, :] = tail


def unpack_kernel(got_ref, movie_ref, prints_ref, activity_ref, places_ref):
    sub, lane = iotas()
    skew = (lane - 16 * sub) & 127
    turn = ((lane >> 4) - sub) & 7
    back = (lane + 16 * sub) & 127
    for r in range(CELL_ROWS):
        movie_ref[r * ROW : r * ROW + 8, :] = jnp.zeros((8, 128), F32)
        movie_ref[(r + 1) * ROW - 8 : (r + 1) * ROW, :] = jnp.zeros((8, 128), F32)

    def block(g, _):
        base = (1 + 8 * (g // TA)) * TA + g % TA
        for t in range(8):
            both = got_ref[g, 16 * t : 16 * t + 16, :].astype(F32)
            for h in range(2):
                value = both[8 * h : 8 * h + 8]
                value = pick_lanes(pick_rows(pick_lanes(value, skew), turn), back)
                movie_ref[pl.ds(base + (2 * t + h) * ROW, 8, stride=TA), :] = value
        high, middle, low = [got_ref[g, 128 + 16 * at : 144 + 16 * at, :].astype(F32) for at in range(3)]
        prints_ref[pl.ds(pl.multiple_of(g * 16, 16), 16), :] = high + (middle + low)
        return 0

    lax.fori_loop(0, GROUP, block, 0)
    m = lane & 31
    own = (m >> 2) * 8 + (m & 3) + jnp.where(sub < 4, 0, 4)
    for v in range(TX):
        tails = [got_ref[v * TA + z, 176:192, :].astype(F32) for z in range(TA)]
        value = jnp.zeros((8, 128), F32)
        for f in range(4):
            rows = jnp.concatenate(
                [tail[f : f + 1] + (tail[4 + f : 5 + f] + tail[8 + f : 9 + f]) for tail in tails] * 2, axis=0
            )
            value = jnp.where((lane >> 5) == f, pick_lanes(rows, own), value)
        activity_ref[v] = value
        spots = (tails[0][12:13] + 1) * ROW + (tails[0][13:14] + (8 * v + 1)) * TA
        places_ref[v : v + 1, :] = spots.astype(jnp.int32)


def first_kernel(
    movie_ref, prints_ref, activity_ref, places_ref, wide_ref, field_ref, up_ref, down_ref
):
    widen(prints_ref[...], wide_ref)
    start_field(movie_ref, field_ref)
    subtract_all(activity_ref, wide_ref, places_ref, field_ref)
    show_edges(field_ref, up_ref, down_ref)


def update_kernel(old_ref, above_ref, below_ref, prints_ref, wide_ref, places_ref, out_ref, whole_ref):
    sub, lane = iotas()
    add_halo(whole_ref, above_ref, below_ref)

    def leaf(v, m):
        folded = []
        for half in range(2):
            k = (m // 4) * 8 + half * 4 + m % 4
            upper, lower = print_pair(wide_ref, v * OWNED + k, sub)
            top, bottom = patch(v, k, places_ref)
            value = upper * whole_ref[top, :] + lower * whole_ref[bottom, :]
            folded.append(value + pltpu.roll(value, 4, 0))
        return jnp.where(sub < 4, folded[0], folded[1])

    def tree(v, m, level):
        if level == 0:
            return leaf(v, m)
        shift = 1 << (level - 1)
        return merge_lanes(tree(v, m, level - 1), tree(v, m + shift, level - 1), shift, lane)

    def tile(v, _):
        total = tree(v, 0, 5)
        for g in range(GROUP):
            out_ref[g, pl.ds(pl.multiple_of(v * 8, 8), 8), :] = total
        return 0

    lax.fori_loop(0, TX, tile, 0)

    def squares(k, level):
        if level == 0:
            rows = prints_ref[pl.ds(k, 8, stride=OWNED), :]
            return rows * rows
        shift = 1 << (level - 1)
        return merge_lanes(squares(k, level - 1), squares(k + shift, level - 1), shift, lane)

    energy = squares(0, 6)
    energy = energy + pltpu.roll(energy, 64, 1)
    for g in range(GROUP):
        out_ref[g, 64:72, :] = energy


def trace_kernel(
    parts_ref, old_ref, movie_ref, wide_ref, places_ref, new_ref, weight_ref, field_ref, up_ref, down_ref
):
    sub, lane = iotas()
    start_field(movie_ref, field_ref)

    def total(start):
        rows = pl.ds(start, 8)
        value = parts_ref[0, rows, :]
        for g in range(1, GROUP):
            value = value + parts_ref[g, rows, :]
        return value

    energy = total(64)
    m = lane & 31
    own = (m >> 2) * 8 + (m & 3) + jnp.where(sub < 4, 0, 4)
    for v in range(TX):
        scale = pick_lanes(jnp.broadcast_to(energy[v : v + 1], (8, 128)), own)
        value = jnp.maximum(old_ref[v] + total(8 * v) / (scale + RIDGE), 0.0)
        new_ref[v] = value
        power = value * value
        power = power + pltpu.roll(power, 64, 1)
        power = power + pltpu.roll(power, 32, 1)
        power = merge_rows(power, power, 1, sub)
        power = merge_rows(power, power, 2, sub)
        weight_ref[v] = value / (power + RIDGE)
    subtract_all(new_ref, wide_ref, places_ref, field_ref)
    show_edges(field_ref, up_ref, down_ref)


def improve_prints(above_ref, below_ref, weight_ref, prints_ref, places_ref, whole_ref, new_ref):
    sub, lane = iotas()
    add_halo(whole_ref, above_ref, below_ref)

    def tile(v, _):
        value = weight_ref[v]

        def eight(q, _):
            base = pl.multiple_of(v * OWNED + q * 8, 8)
            folded = []
            for b in range(4):
                pair = spread(value, q * 4 + b, sub, lane)
                sides = []
                for half in range(2):
                    top, bottom = patch(v, q * 8 + half * 4 + b, places_ref)
                    sides.append(
                        merge_lanes(pair[half] * whole_ref[top, :], pair[half] * whole_ref[bottom, :], 64, lane)
                    )
                folded.append(merge_lanes(sides[0], sides[1], 32, lane))
            low = merge_rows(folded[0], folded[1], 1, sub)
            high = merge_rows(folded[2], folded[3], 1, sub)
            step = merge_rows(low, high, 2, sub)
            turned = pltpu.roll(step, 4, 0)
            dx = (lane & 32) != 0
            swapped = jnp.where(dx, pltpu.roll(turned, 32, 1), pltpu.roll(turned, 96, 1))
            step = jnp.where(dx == (sub >= 4), step, swapped)
            new_ref[pl.ds(base, 8), :] = jnp.maximum(prints_ref[pl.ds(base, 8), :] + step, 0.0)
            return 0

        return lax.fori_loop(0, 8, eight, 0, unroll=8)

    lax.fori_loop(0, TX, tile, 0)


def print_kernel(
    old_ref, above_ref, below_ref, weight_ref, activity_ref, movie_ref, prints_ref, places_ref,
    new_ref, wide_ref, next_ref, up_ref, down_ref, whole_ref,
):
    improve_prints(above_ref, below_ref, weight_ref, prints_ref, places_ref, whole_ref, new_ref)
    widen(new_ref[...], wide_ref)
    start_field(movie_ref, next_ref)
    subtract_all(activity_ref, wide_ref, places_ref, next_ref)
    show_edges(next_ref, up_ref, down_ref)


def last_kernel(
    old_ref, above_ref, below_ref, weight_ref, prints_ref, places_ref, out_ref, whole_ref, new_ref
):
    improve_prints(above_ref, below_ref, weight_ref, prints_ref, places_ref, whole_ref, new_ref)
    for j in range(TX):
        rows = new_ref[j * OWNED : (j + 1) * OWNED, :]
        for z in range(TA):
            out_ref[j * TA + z] = rows


def swap_lanes(parts, lane):
    for shift in (1, 2):
        high = (lane & (32 * shift)) != 0
        turned = []
        for b in range(4):
            other = pltpu.roll(parts[b ^ shift], 32 * shift if b & shift == 0 else 128 - 32 * shift, 1)
            turned.append(jnp.where(high, other, parts[b]) if b & shift == 0 else jnp.where(high, parts[b], other))
        parts = turned
    return parts


def finish_kernel(blocks_ref, out_ref):
    lane = lax.broadcasted_iota(jnp.int32, (OWNED, 128), 1)
    for z in range(TA):
        for a in range(2):
            rows = swap_lanes([blocks_ref[(4 * a + b) * TA + z] for b in range(4)], lane)
            for d in range(4):
                start = d * 1024 + (z * 2 + a) * 128
                out_ref[:, start : start + 128] = rows[d]


def shape(*sizes, dtype=F32):
    return jax.ShapeDtypeStruct(sizes, dtype)


def call(kernel, outs, places, scratch=(), smem=None, alias=None):
    return pl.pallas_call(
        kernel,
        out_shape=outs,
        in_specs=[SMEM if at == smem else VMEM for at in range(places)],
        out_specs=jax.tree.map(lambda _: VMEM, outs),
        scratch_shapes=list(scratch),
        input_output_aliases={} if alias is None else {0: alias},
        compiler_params=pltpu.CompilerParams(vmem_limit_bytes=16 << 20),
    )


FIELD_SHAPE = shape(FIELD, 128)
EDGE_SHAPE = shape(2 * ROW, 128)
WIDE_SHAPE = shape(4, COUNT, 128)
AXES = ("tx", "ta")


def exchange(blocks):
    return lax.all_to_all(blocks, AXES, 0, 0, tiled=True)


def halo(up, down):
    ends = lax.axis_size("ty") - 1
    above = lax.ppermute(down, "ty", [(i, i + 1) for i in range(ends)])
    below = lax.ppermute(up, "ty", [(i + 1, i) for i in range(ends)])
    return above, below


def shards(movie, footprints, traces, anchor_row, anchor_col):
    layer = lax.axis_index("ta")
    column = lax.axis_index("tx")
    frames = traces.shape[0]
    blocks = movie.reshape(frames, 4, CELL_ROWS, TX, 2, 128).transpose(3, 1, 2, 0, 4, 5)
    got = exchange(
        call(pack_kernel, shape(GROUP, 192, 128, dtype=jnp.bfloat16), 6, smem=5)(
            blocks.reshape(GROUP, 128, 128),
            footprints,
            traces,
            anchor_row.reshape(1, OWNED),
            anchor_col.reshape(1, OWNED),
            layer.reshape(1),
        )
    )
    cells, prints, activity, places = call(
        unpack_kernel,
        (shape(INNER, 128), shape(COUNT, 128), shape(TX, 8, 128), shape(TX, 128, dtype=jnp.int32)),
        1,
    )(got)
    wide, field, up, down = call(
        first_kernel, (WIDE_SHAPE, FIELD_SHAPE, EDGE_SHAPE, EDGE_SHAPE), 4, smem=3
    )(cells, prints, activity, places)
    for sweep in range(ITERS):
        above, below = halo(up, down)
        sums, _ = call(update_kernel, (shape(GROUP, 72, 128), FIELD_SHAPE), 6, smem=5, alias=1)(
            field, above, below, prints, wide, places
        )
        parts = exchange(sums)
        activity, weight, field, up, down = call(
            trace_kernel,
            (shape(TX, 8, 128), shape(TX, 8, 128), FIELD_SHAPE, EDGE_SHAPE, EDGE_SHAPE),
            5,
            smem=4,
        )(parts, activity, cells, wide, places)
        above, below = halo(up, down)
        if sweep + 1 < ITERS:
            prints, wide, field, up, down, _ = call(
                print_kernel,
                (shape(COUNT, 128), WIDE_SHAPE, FIELD_SHAPE, EDGE_SHAPE, EDGE_SHAPE, FIELD_SHAPE),
                8,
                smem=7,
                alias=5,
            )(field, above, below, weight, activity, cells, prints, places)
        else:
            sent, _ = call(
                last_kernel,
                (shape(GROUP, OWNED, 128), FIELD_SHAPE),
                6,
                (pltpu.VMEM((COUNT, 128), F32),),
                smem=5,
                alias=1,
            )(field, above, below, weight, prints, places)
    footprints_out = call(finish_kernel, shape(OWNED, 4096), 1)(exchange(sent))
    mine = lax.dynamic_index_in_dim(activity, column, 0, keepdims=False).reshape(2, TA, 128)
    mine = lax.dynamic_index_in_dim(mine, layer, 1, keepdims=False)
    traces_out = mine.reshape(2, frames, 8, 4).transpose(1, 2, 0, 3).reshape(frames, OWNED)
    return footprints_out, traces_out


def solution(mesh):
    placed = (
        P("ta", None, "ty", "tx"),
        P(("ty", "tx"), None),
        P("ta", ("ty", "tx")),
        P(("ty", "tx")),
        P(("ty", "tx")),
    )
    return jax.shard_map(
        shards,
        mesh=mesh,
        in_specs=placed,
        out_specs=(P(("ty", "tx"), None), P("ta", ("ty", "tx"))),
        check_vma=False,
    )
```

time: 263 us -> 178 us (0.68)
  Pallas kernels: 119 us -> 39.2 us
  blocking collectives: 40.3 us -> 66.4 us
  starting transfers between devices: 50 us -> 25.7 us
  local copies, waits for them, and re-layouts: 16.5 us -> 5.23 us
  waiting for transfers between devices: 32.7 us -> 39.6 us
    pallas_call x9, Pallas kernels: 116 us -> 37.2 us  [the longest x2 9.9 us: shards(): call(update_kernel, (shape(GROUP, 72, 128), FIELD_SHAPE), 6, smem=5, alia...]
    all_to_all x2 -> x3, blocking collectives: 40.3 us -> 66.4 us  [exchange(): return lax.all_to_all(blocks, AXES, 0, 0, tiled=True)]
    ppermute x8, waiting for transfers between devices: 13.5 us -> 28.2 us  [the longest x4 23.6 us: halo(): below = lax.ppermute(up, 'ty', [(i + 1, i) for i in range(ends)])]
    all_to_all x3 -> x1, starting transfers between devices: 18 us -> 3.93 us  [exchange(): return lax.all_to_all(blocks, AXES, 0, 0, tiled=True)]
    ppermute x8, starting transfers between devices: 32 us -> 21.8 us  [the longest x4 12.9 us: halo(): above = lax.ppermute(down, 'ty', [(i, i + 1) for i in range(ends)])]
    all_to_all x3 -> x1, waiting for transfers between devices: 19.2 us -> 11.4 us  [exchange(): return lax.all_to_all(blocks, AXES, 0, 0, tiled=True)]
    slice x6 -> x0, local copies, waits for them, and re-layouts: 5.01 us -> none  [the longest x4 4.28 us: halo(): field[:2 * ROW]]
    unnamed x24 -> x8, local copies, waits for them, and re-layouts: 4.79 us -> 1.99 us
  transfers between devices with their start and end apart: 11 -> 9, of which waited for: 11 -> 9; matrix products, arithmetic and copies ran while one was open for 2% -> 0% of each run, Pallas kernels for 4% -> 0%
where the time goes in v2:
time: 178 us; the launch traced here: 177 us
  blocking collectives  66.4 us (37%)
  waiting for transfers between devices  39.6 us (22%)
  Pallas kernels  39.2 us (22%)
  starting transfers between devices  25.7 us (14%)
  local copies, waits for them, and re-layouts  5.23 us (3%)
    all_to_all x3, blocking collectives, exchange(): return lax.all_to_all(blocks, AXES, 0, 0, tiled=True)  66.4 us
    ppermute x4, waiting for transfers between devices, halo(): below = lax.ppermute(up, 'ty', [(i + 1, i) for i in range(ends)])  23.6 us
    ppermute x4, starting transfers between devices, halo(): above = lax.ppermute(down, 'ty', [(i, i + 1) for i in range(ends)])  12.9 us
    all_to_all x1, waiting for transfers between devices, exchange(): return lax.all_to_all(blocks, AXES, 0, 0, tiled=True)  11.4 us
    pallas_call x2, Pallas kernels, shards(): call(update_kernel, (shape(GROUP, 72, 128), FIELD_SHAPE), 6, smem=5, alia...  9.9 us
    ppermute x4, starting transfers between devices, halo(): below = lax.ppermute(up, 'ty', [(i + 1, i) for i in range(ends)])  8.9 us
    pallas_call x1, Pallas kernels, shards(): call(print_kernel, (shape(COUNT, 128), WIDE_SHAPE, FIELD_SHAPE, EDGE_SHAP...  6.96 us
    pallas_call x2, Pallas kernels, shards(): call(trace_kernel, (shape(TX, 8, 128), shape(TX, 8, 128), FIELD_SHAPE, ED...  6.36 us
  transfers between devices with their start and end apart: 9, of which 9 were waited for; matrix products, arithmetic and copies ran while one was open for 0% of the time, Pallas kernels for 0%

profile of v2, /device:TPU:1, one launch (start us, length us, event | category | flops | bytes accessed | tf_op | source)
XLA Modules:
  0.0 177.1 jit_solution(1548064645870679103)
XLA Ops:
  0.6 0.0 copy-start
  0.6 2.4 %copy.14 = bf16[4,4,16,8,2,128]{5,4,0,2,1,3:T(2,128)(2,1)S(1)} copy(bf16[4,4,16,8,2,128]{5,4,3,2,1,0:T(2,128)(2,1)} %bitcast.12) | data formatting | bytes 2097152 | tf_op jit(solution)/shard_map/reshape | solution.py:386
  3.0 0.0 copy-done
  3.1 0.0 copy-start.1
  3.1 0.7 copy-done.1
  3.7 0.0 copy-start.2
  3.7 0.7 copy-done.2
  4.4 0.0 copy-start.3
  4.4 0.7 copy-done.3
  5.0 0.3 shard_map.68
  5.4 30.7 %all_to_all.20.got_ref = bf16[32,192,128]{2,1,0:T(8,128)(2,1)S(1)} all-to-all(bf16[32,192,128]{2,1,0:T(8,128)(2,1)S(1)} %shard_map.68), channel_id=1, replica_groups=mesh['ty'=4,'tx'=8,'ta'=4] {'tx','ta'}, dimensions={0} | all-to-all | bytes 3145728 | tf_op jit(solution)/shard_map/all_to_all | solution.py:372
  36.1 5.1 %shard_map.69 = (f32[4224,128]{1,0:T(8,128)S(1)}, f32[512,128]{1,0:T(8,128)S(1)}, f32[8,8,128]{2,1,0:T(8,128)S(1)}, s32[8,128]{1,0:T(8,128)S(1)}) custom-call(bf16[32,192,128]{2,1,0:T(8,128)(2,1)S(1)} %all_to_all.20.got_ref), custom_call_target="tpu_custom_call" | custom-call | tf_op jit(solution)/shard_map/pallas_call | solution.py:397
  41.2 3.9 %shard_map.70 = (f32[4,512,128]{2,1,0:T(8,128)S(1)}, f32[4752,128]{1,0:T(8,128)S(1)}, f32[528,128]{1,0:T(8,128)S(1)}, f32[528,128]{1,0:T(8,128)S(1)}) custom-call(f32[4224,128]{1,0:T(8,128)S(1)} %get-tuple-element.28.movie_ref, f32[512,128]{1,0:T(8,128)S(1)} %get-tuple-element.29.prints_ref, f32[8,8,128]{2,1,0:T(8,128)S(1)} %get-tuple-element.30.activity_ref.old_ref, ...), custom_call_target="tpu_custom_call" | custom-call | tf_op jit(solution)/shard_map/pallas_call | solution.py:402
  45.1 6.8 %collective-permute-start = (f32[528,128]{1,0:T(8,128)S(1)}, f32[528,128]{1,0:T(8,128)S(1)}, u32[]{:S(2)}, u32[]{:S(2)}) collective-permute-start(f32[528,128]{1,0:T(8,128)S(1)} %get-tuple-element.33), channel_id=1, source_target_pairs={{0,32},{32,64},{64,96},{1,33},{33,65},{65,97},{2,34},{34,66},{66,9... | collective-permute-start | bytes 811016 | tf_op jit(solution)/shard_map/ppermute | solution.py:377
  52.0 1.9 %collective-permute-start.1 = (f32[528,128]{1,0:T(8,128)S(1)}, f32[528,128]{1,0:T(8,128)S(1)}, u32[]{:S(2)}, u32[]{:S(2)}) collective-permute-start(f32[528,128]{1,0:T(8,128)S(1)} %get-tuple-element.34), channel_id=1, source_target_pairs={{32,0},{64,32},{96,64},{33,1},{65,33},{97,65},{34,2},{66,34},{98,6... | collective-permute-start | bytes 811016 | tf_op jit(solution)/shard_map/ppermute | solution.py:378
  53.9 1.5 collective-permute-done.above_ref
  55.3 5.9 %collective-permute-done.1.below_ref = f32[528,128]{1,0:T(8,128)S(1)} collective-permute-done((f32[528,128]{1,0:T(8,128)S(1)}, f32[528,128]{1,0:T(8,128)S(1)}, u32[]{:S(2)}, u32[]{:S(2)}) %collective-permute-start.1) | collective-permute-done | bytes 270368 | tf_op jit(solution)/shard_map/ppermute | solution.py:378
  61.2 4.9 %shard_map.71 = (f32[32,72,128]{2,1,0:T(8,128)S(1)}, f32[4752,128]{1,0:T(8,128)S(1)}) custom-call(f32[4752,128]{1,0:T(8,128)S(1)} %get-tuple-element.32.old_ref, f32[528,128]{1,0:T(8,128)S(1)} %collective-permute-done.above_ref, f32[528,128]{1,0:T(8,128)S(1)} %collective-permute-done.1.below_ref, ...), custom_call_target="tpu_custom_call", output_to_operand_aliasing={{1}: (0, {})} | custom-call | tf_op jit(solution)/shard_map/pallas_call | solution.py:407
  66.2 17.8 %all_to_all.21.parts_ref = f32[32,72,128]{2,1,0:T(8,128)S(1)} all-to-all(f32[32,72,128]{2,1,0:T(8,128)S(1)} %get-tuple-element.36), channel_id=1, replica_groups=mesh['ty'=4,'tx'=8,'ta'=4] {'tx','ta'}, dimensions={0} | all-to-all | bytes 2359296 | tf_op jit(solution)/shard_map/all_to_all | solution.py:372
  84.0 3.2 %shard_map.72 = (f32[8,8,128]{2,1,0:T(8,128)S(1)}, f32[8,8,128]{2,1,0:T(8,128)S(1)}, f32[4752,128]{1,0:T(8,128)S(1)}, f32[528,128]{1,0:T(8,128)S(1)}, f32[528,128]{1,0:T(8,128)S(1)}) custom-call(f32[32,72,128]{2,1,0:T(8,128)S(1)} %all_to_all.21.parts_ref, f32[8,8,128]{2,1,0:T(8,128)S(1)} %get-tuple-element.30.activity_ref.old_ref, ...), custom_call_target="tpu_custom_call" | custom-call | tf_op jit(solution)/shard_map/pallas_call | solution.py:411
  87.2 2.1 %collective-permute-start.2 = (f32[528,128]{1,0:T(8,128)S(1)}, f32[528,128]{1,0:T(8,128)S(1)}, u32[]{:S(2)}, u32[]{:S(2)}) collective-permute-start(f32[528,128]{1,0:T(8,128)S(1)} %get-tuple-element.38), channel_id=1, source_target_pairs={{0,32},{32,64},{64,96},{1,33},{33,65},{65,97},{2,34},{34,66},{66,9... | collective-permute-start | bytes 811016 | tf_op jit(solution)/shard_map/ppermute | solution.py:377
  89.3 2.3 %collective-permute-start.3 = (f32[528,128]{1,0:T(8,128)S(1)}, f32[528,128]{1,0:T(8,128)S(1)}, u32[]{:S(2)}, u32[]{:S(2)}) collective-permute-start(f32[528,128]{1,0:T(8,128)S(1)} %get-tuple-element.39), channel_id=1, source_target_pairs={{32,0},{64,32},{96,64},{33,1},{65,33},{97,65},{34,2},{66,34},{98,6... | collective-permute-start | bytes 811016 | tf_op jit(solution)/shard_map/ppermute | solution.py:378
  91.5 1.1 collective-permute-done.2.above_ref
  92.6 5.9 %collective-permute-done.3.below_ref = f32[528,128]{1,0:T(8,128)S(1)} collective-permute-done((f32[528,128]{1,0:T(8,128)S(1)}, f32[528,128]{1,0:T(8,128)S(1)}, u32[]{:S(2)}, u32[]{:S(2)}) %collective-permute-start.3) | collective-permute-done | bytes 270368 | tf_op jit(solution)/shard_map/ppermute | solution.py:378
  98.5 7.0 %shard_map.73 = (f32[512,128]{1,0:T(8,128)S(1)}, f32[4,512,128]{2,1,0:T(8,128)S(1)}, f32[4752,128]{1,0:T(8,128)S(1)}, f32[528,128]{1,0:T(8,128)S(1)}, f32[528,128]{1,0:T(8,128)S(1)}, /*index=5*/f32[4752,128]{1,0:T(8,128)S(1)}) custom-call(f32[4752,128]{1,0:T(8,128)S(1)} %get-tuple-element.37.old_ref, ...), custom_call_target="tpu_custom_call", output_to_operand_aliasing={{5}: (0, {})} | custom-call | tf_op jit(solution)/shard_map/pallas_call | solution.py:419
  105.5 1.9 %collective-permute-start.4 = (f32[528,128]{1,0:T(8,128)S(1)}, f32[528,128]{1,0:T(8,128)S(1)}, u32[]{:S(2)}, u32[]{:S(2)}) collective-permute-start(f32[528,128]{1,0:T(8,128)S(1)} %get-tuple-element.43), channel_id=1, source_target_pairs={{0,32},{32,64},{64,96},{1,33},{33,65},{65,97},{2,34},{34,66},{66,9... | collective-permute-start | bytes 811016 | tf_op jit(solution)/shard_map/ppermute | solution.py:377
  107.4 2.4 %collective-permute-start.5 = (f32[528,128]{1,0:T(8,128)S(1)}, f32[528,128]{1,0:T(8,128)S(1)}, u32[]{:S(2)}, u32[]{:S(2)}) collective-permute-start(f32[528,128]{1,0:T(8,128)S(1)} %get-tuple-element.44), channel_id=1, source_target_pairs={{32,0},{64,32},{96,64},{33,1},{65,33},{97,65},{34,2},{66,34},{98,6... | collective-permute-start | bytes 811016 | tf_op jit(solution)/shard_map/ppermute | solution.py:378
  109.9 1.0 collective-permute-done.4.above_ref
  110.8 5.9 %collective-permute-done.5.below_ref = f32[528,128]{1,0:T(8,128)S(1)} collective-permute-done((f32[528,128]{1,0:T(8,128)S(1)}, f32[528,128]{1,0:T(8,128)S(1)}, u32[]{:S(2)}, u32[]{:S(2)}) %collective-permute-start.5) | collective-permute-done | bytes 270368 | tf_op jit(solution)/shard_map/ppermute | solution.py:378
  116.7 4.9 %shard_map.74 = (f32[32,72,128]{2,1,0:T(8,128)S(1)}, f32[4752,128]{1,0:T(8,128)S(1)}) custom-call(f32[4752,128]{1,0:T(8,128)S(1)} %get-tuple-element.42.old_ref, f32[528,128]{1,0:T(8,128)S(1)} %collective-permute-done.4.above_ref, f32[528,128]{1,0:T(8,128)S(1)} %collective-permute-done.5.below_ref, ...), custom_call_target="tpu_custom_call", output_to_operand_aliasing={{1}: (0, {})} | custom-call | tf_op jit(solution)/shard_map/pallas_call | solution.py:407
  121.7 17.9 %all_to_all.22.parts_ref = f32[32,72,128]{2,1,0:T(8,128)S(1)} all-to-all(f32[32,72,128]{2,1,0:T(8,128)S(1)} %get-tuple-element.47), channel_id=1, replica_groups=mesh['ty'=4,'tx'=8,'ta'=4] {'tx','ta'}, dimensions={0} | all-to-all | bytes 2359296 | tf_op jit(solution)/shard_map/all_to_all | solution.py:372
  139.6 3.2 %shard_map.75 = (f32[8,8,128]{2,1,0:T(8,128)S(1)}, f32[8,8,128]{2,1,0:T(8,128)S(1)}, f32[4752,128]{1,0:T(8,128)S(1)}, f32[528,128]{1,0:T(8,128)S(1)}, f32[528,128]{1,0:T(8,128)S(1)}) custom-call(f32[32,72,128]{2,1,0:T(8,128)S(1)} %all_to_all.22.parts_ref, f32[8,8,128]{2,1,0:T(8,128)S(1)} %get-tuple-element.41.activity_ref.old_ref, ...), custom_call_target="tpu_custom_call" | custom-call | tf_op jit(solution)/shard_map/pallas_call | solution.py:411
  142.8 2.0 %collective-permute-start.6 = (f32[528,128]{1,0:T(8,128)S(1)}, f32[528,128]{1,0:T(8,128)S(1)}, u32[]{:S(2)}, u32[]{:S(2)}) collective-permute-start(f32[528,128]{1,0:T(8,128)S(1)} %get-tuple-element.49), channel_id=1, source_target_pairs={{0,32},{32,64},{64,96},{1,33},{33,65},{65,97},{2,34},{34,66},{66,9... | collective-permute-start | bytes 811016 | tf_op jit(solution)/shard_map/ppermute | solution.py:377
  144.8 2.3 %collective-permute-start.7 = (f32[528,128]{1,0:T(8,128)S(1)}, f32[528,128]{1,0:T(8,128)S(1)}, u32[]{:S(2)}, u32[]{:S(2)}) collective-permute-start(f32[528,128]{1,0:T(8,128)S(1)} %get-tuple-element.50), channel_id=1, source_target_pairs={{32,0},{64,32},{96,64},{33,1},{65,33},{97,65},{34,2},{66,34},{98,6... | collective-permute-start | bytes 811016 | tf_op jit(solution)/shard_map/ppermute | solution.py:378
  147.1 1.1 collective-permute-done.6.above_ref
  148.2 5.9 %collective-permute-done.7.below_ref = f32[528,128]{1,0:T(8,128)S(1)} collective-permute-done((f32[528,128]{1,0:T(8,128)S(1)}, f32[528,128]{1,0:T(8,128)S(1)}, u32[]{:S(2)}, u32[]{:S(2)}) %collective-permute-start.7) | collective-permute-done | bytes 270368 | tf_op jit(solution)/shard_map/ppermute | solution.py:378
  154.1 4.7 %shard_map.76 = (f32[32,64,128]{2,1,0:T(8,128)}, f32[4752,128]{1,0:T(8,128)S(1)}) custom-call(f32[4752,128]{1,0:T(8,128)S(1)} %get-tuple-element.48.old_ref, f32[528,128]{1,0:T(8,128)S(1)} %collective-permute-done.6.above_ref, f32[528,128]{1,0:T(8,128)S(1)} %collective-permute-done.7.below_ref, ...), custom_call_target="tpu_custom_call", output_to_operand_aliasing={{1}: (0, {})} | custom-call | tf_op jit(solution)/shard_map/pallas_call | solution.py:427
  158.8 3.9 %all-to-all-start.3 = ((f32[32,64,128]{2,1,0:T(8,128)}), f32[32,64,128]{2,1,0:T(8,128)S(1)}, u32[]{:S(2)}, u32[]{:S(2)}) async-start(f32[32,64,128]{2,1,0:T(8,128)} %get-tuple-element.52), calls=%async_computation.3 | async-start | bytes 2097152 | tf_op jit(solution)/shard_map/all_to_all | solution.py:372
  162.8 0.1 reshape.36
  162.9 0.7 reshape.37
  163.6 11.4 %all-to-all-done.3.blocks_ref = f32[32,64,128]{2,1,0:T(8,128)S(1)} async-done(((f32[32,64,128]{2,1,0:T(8,128)}), f32[32,64,128]{2,1,0:T(8,128)S(1)}, u32[]{:S(2)}, u32[]{:S(2)}) %all-to-all-start.3) | async-done | bytes 1048608 | tf_op jit(solution)/shard_map/all_to_all | solution.py:372
  175.1 2.0 %shard_map.77 = f32[64,4096]{1,0:T(8,128)} custom-call(f32[32,64,128]{2,1,0:T(8,128)S(1)} %all-to-all-done.3.blocks_ref), custom_call_target="tpu_custom_call" | custom-call | tf_op jit(solution)/shard_map/pallas_call | solution.py:435
  (3 shorter events, 0.1 us)
Async XLA Ops:
  0.6 2.4 %copy-start = (f32[64,4096]{1,0:T(8,128)S(1)}, f32[64,4096]{1,0:T(8,128)}, u32[]{:S(2)}) copy-start(f32[64,4096]{1,0:T(8,128)} %prints_ref.1) | copy-start | bytes 3145732
  3.1 0.7 copy-start.1
  3.7 0.7 copy-start.2
  4.4 0.7 copy-start.3
  45.1 10.2 %collective-permute-start = (f32[528,128]{1,0:T(8,128)S(1)}, f32[528,128]{1,0:T(8,128)S(1)}, u32[]{:S(2)}, u32[]{:S(2)}) collective-permute-start(f32[528,128]{1,0:T(8,128)S(1)} %get-tuple-element.33), channel_id=1, source_target_pairs={{0,32},{32,64},{64,96},{1,33},{33,65},{65,97},{2,34},{34,66},{66,9... | collective-permute-start | bytes 811016 | tf_op jit(solution)/shard_map/ppermute | solution.py:377
  52.0 9.3 %collective-permute-start.1 = (f32[528,128]{1,0:T(8,128)S(1)}, f32[528,128]{1,0:T(8,128)S(1)}, u32[]{:S(2)}, u32[]{:S(2)}) collective-permute-start(f32[528,128]{1,0:T(8,128)S(1)} %get-tuple-element.34), channel_id=1, source_target_pairs={{32,0},{64,32},{96,64},{33,1},{65,33},{97,65},{34,2},{66,34},{98,6... | collective-permute-start | bytes 811016 | tf_op jit(solution)/shard_map/ppermute | solution.py:378
  87.2 5.5 %collective-permute-start.2 = (f32[528,128]{1,0:T(8,128)S(1)}, f32[528,128]{1,0:T(8,128)S(1)}, u32[]{:S(2)}, u32[]{:S(2)}) collective-permute-start(f32[528,128]{1,0:T(8,128)S(1)} %get-tuple-element.38), channel_id=1, source_target_pairs={{0,32},{32,64},{64,96},{1,33},{33,65},{65,97},{2,34},{34,66},{66,9... | collective-permute-start | bytes 811016 | tf_op jit(solution)/shard_map/ppermute | solution.py:377
  89.3 9.3 %collective-permute-start.3 = (f32[528,128]{1,0:T(8,128)S(1)}, f32[528,128]{1,0:T(8,128)S(1)}, u32[]{:S(2)}, u32[]{:S(2)}) collective-permute-start(f32[528,128]{1,0:T(8,128)S(1)} %get-tuple-element.39), channel_id=1, source_target_pairs={{32,0},{64,32},{96,64},{33,1},{65,33},{97,65},{34,2},{66,34},{98,6... | collective-permute-start | bytes 811016 | tf_op jit(solution)/shard_map/ppermute | solution.py:378
  105.5 5.3 %collective-permute-start.4 = (f32[528,128]{1,0:T(8,128)S(1)}, f32[528,128]{1,0:T(8,128)S(1)}, u32[]{:S(2)}, u32[]{:S(2)}) collective-permute-start(f32[528,128]{1,0:T(8,128)S(1)} %get-tuple-element.43), channel_id=1, source_target_pairs={{0,32},{32,64},{64,96},{1,33},{33,65},{65,97},{2,34},{34,66},{66,9... | collective-permute-start | bytes 811016 | tf_op jit(solution)/shard_map/ppermute | solution.py:377
  107.4 9.3 %collective-permute-start.5 = (f32[528,128]{1,0:T(8,128)S(1)}, f32[528,128]{1,0:T(8,128)S(1)}, u32[]{:S(2)}, u32[]{:S(2)}) collective-permute-start(f32[528,128]{1,0:T(8,128)S(1)} %get-tuple-element.44), channel_id=1, source_target_pairs={{32,0},{64,32},{96,64},{33,1},{65,33},{97,65},{34,2},{66,34},{98,6... | collective-permute-start | bytes 811016 | tf_op jit(solution)/shard_map/ppermute | solution.py:378
  142.8 5.4 %collective-permute-start.6 = (f32[528,128]{1,0:T(8,128)S(1)}, f32[528,128]{1,0:T(8,128)S(1)}, u32[]{:S(2)}, u32[]{:S(2)}) collective-permute-start(f32[528,128]{1,0:T(8,128)S(1)} %get-tuple-element.49), channel_id=1, source_target_pairs={{0,32},{32,64},{64,96},{1,33},{33,65},{65,97},{2,34},{34,66},{66,9... | collective-permute-start | bytes 811016 | tf_op jit(solution)/shard_map/ppermute | solution.py:377
  144.8 9.3 %collective-permute-start.7 = (f32[528,128]{1,0:T(8,128)S(1)}, f32[528,128]{1,0:T(8,128)S(1)}, u32[]{:S(2)}, u32[]{:S(2)}) collective-permute-start(f32[528,128]{1,0:T(8,128)S(1)} %get-tuple-element.50), channel_id=1, source_target_pairs={{32,0},{64,32},{96,64},{33,1},{65,33},{97,65},{34,2},{66,34},{98,6... | collective-permute-start | bytes 811016 | tf_op jit(solution)/shard_map/ppermute | solution.py:378
  158.8 16.3 %all-to-all-start.3 = ((f32[32,64,128]{2,1,0:T(8,128)}), f32[32,64,128]{2,1,0:T(8,128)S(1)}, u32[]{:S(2)}, u32[]{:S(2)}) async-start(f32[32,64,128]{2,1,0:T(8,128)} %get-tuple-element.52), calls=%async_computation.3 | async-start | bytes 2097152 | tf_op jit(solution)/shard_map/all_to_all | solution.py:372

commit v3 on v2

--- a/solution.py
+++ b/solution.py
@@ -117,29 +117,35 @@
     lax.fori_loop(0, CELL_ROWS, one, 0)
 
 
-def add_halo(field_ref, above_ref, below_ref):
-    field_ref[0 : 2 * ROW, :] += above_ref[...]
-    field_ref[INNER:, :] += below_ref[...]
-
-
-def show_edges(field_ref, up_ref, down_ref):
-    up_ref[...] = field_ref[0 : 2 * ROW, :]
-    down_ref[...] = field_ref[INNER:, :]
-
-
-def thirds(value):
-    high = value.astype(jnp.bfloat16)
-    rest = value - high.astype(F32)
-    middle = rest.astype(jnp.bfloat16)
-    return high, middle, (rest - middle.astype(F32)).astype(jnp.bfloat16)
-
-
-def pack_kernel(cells_ref, prints_ref, traces_ref, row_ref, col_ref, layer_ref, out_ref):
+def add_halo(field_ref, above_ref, below_ref, near_ref):
+    even = near_ref[0] == 0
+    top = jnp.where(even, below_ref[...], above_ref[...])
+    bottom = jnp.where(even, above_ref[...], below_ref[...])
+    field_ref[0 : 2 * ROW, :] += top
+    field_ref[INNER:, :] += bottom
+
+
+def show_edges(field_ref, near_ref, near_out, far_out):
+    even = near_ref[0] == 0
+    top = field_ref[0 : 2 * ROW, :]
+    bottom = field_ref[INNER:, :]
+    near_out[...] = jnp.where(even, bottom, top)
+    far_out[...] = jnp.where(even, top, bottom)
+
+
+def pieces(value, count):
+    out = []
+    for _ in range(count):
+        out.append(value.astype(jnp.bfloat16))
+        value = value - out[-1].astype(F32)
+    return out
+
+
+def pack_kernel(cells_ref, prints_ref, small_ref, layer_ref, out_ref):
     lane = lax.broadcasted_iota(jnp.int32, (16, 128), 1)
     rows = pl.ds(pl.multiple_of(layer_ref[0] * 16, 16), 16)
-    tail = [piece.astype(F32) for piece in thirds(traces_ref[...])]
-    tail = jnp.concatenate(tail + [row_ref[...].astype(F32), col_ref[...].astype(F32), jnp.zeros((2, OWNED), F32)], axis=0)
-    tail = jnp.concatenate([tail, jnp.zeros((16, 128 - OWNED), F32)], axis=1).astype(jnp.bfloat16)
+    tail = [piece.astype(F32) for piece in pieces(small_ref[0:2, :], 3)]
+    tail = jnp.concatenate(tail + [small_ref[2:3, :], jnp.zeros((9, 128), F32)], axis=0).astype(jnp.bfloat16)
     for a in range(8):
         blocks = swap_lanes(
             [prints_ref[rows, d * 1024 + a * 128 : d * 1024 + a * 128 + 128] for d in range(4)], lane
@@ -148,9 +154,9 @@
             shard = 4 * a + b
             dest = (shard % TX) * TA + shard // TX
             out_ref[dest, 0:128, :] = cells_ref[dest]
-            for at, piece in enumerate(thirds(blocks[b])):
+            for at, piece in enumerate(pieces(blocks[b], 2)):
                 out_ref[dest, 128 + 16 * at : 144 + 16 * at, :] = piece
-            out_ref[dest, 176:192, :] = tail
+            out_ref[dest, 160:168, :] = tail[0:8]
 
 
 def unpack_kernel(got_ref, movie_ref, prints_ref, activity_ref, places_ref):
@@ -170,38 +176,31 @@
                 value = both[8 * h : 8 * h + 8]
                 value = pick_lanes(pick_rows(pick_lanes(value, skew), turn), back)
                 movie_ref[pl.ds(base + (2 * t + h) * ROW, 8, stride=TA), :] = value
-        high, middle, low = [got_ref[g, 128 + 16 * at : 144 + 16 * at, :].astype(F32) for at in range(3)]
-        prints_ref[pl.ds(pl.multiple_of(g * 16, 16), 16), :] = high + (middle + low)
+        high, low = [got_ref[g, 128 + 16 * at : 144 + 16 * at, :].astype(F32) for at in range(2)]
+        prints_ref[pl.ds(pl.multiple_of(g * 16, 16), 16), :] = high + low
         return 0
 
-    lax.fori_loop(0, GROUP, block, 0)
-    m = lane & 31
-    own = (m >> 2) * 8 + (m & 3) + jnp.where(sub < 4, 0, 4)
+    lax.fori_loop(0, GROUP, block, 0, unroll=2)
     for v in range(TX):
-        tails = [got_ref[v * TA + z, 176:192, :].astype(F32) for z in range(TA)]
-        value = jnp.zeros((8, 128), F32)
-        for f in range(4):
-            rows = jnp.concatenate(
-                [tail[f : f + 1] + (tail[4 + f : 5 + f] + tail[8 + f : 9 + f]) for tail in tails] * 2, axis=0
-            )
-            value = jnp.where((lane >> 5) == f, pick_lanes(rows, own), value)
-        activity_ref[v] = value
-        spots = (tails[0][12:13] + 1) * ROW + (tails[0][13:14] + (8 * v + 1)) * TA
-        places_ref[v : v + 1, :] = spots.astype(jnp.int32)
+        tails = [got_ref[v * TA + z, 160:168, :].astype(F32) for z in range(TA)]
+        values = [tail[0:2] + (tail[2:4] + tail[4:6]) for tail in tails]
+        activity_ref[v] = jnp.concatenate([value[h : h + 1] for h in range(2) for value in values], axis=0)
+        row, col = tails[0][6:7], pltpu.roll(tails[0], 64, 1)[6:7]
+        places_ref[v : v + 1, :] = ((row + 1) * ROW + (col + (8 * v + 1)) * TA).astype(jnp.int32)
 
 
 def first_kernel(
-    movie_ref, prints_ref, activity_ref, places_ref, wide_ref, field_ref, up_ref, down_ref
+    movie_ref, prints_ref, activity_ref, near_ref, places_ref, wide_ref, field_ref, up_ref, down_ref
 ):
     widen(prints_ref[...], wide_ref)
     start_field(movie_ref, field_ref)
     subtract_all(activity_ref, wide_ref, places_ref, field_ref)
-    show_edges(field_ref, up_ref, down_ref)
-
-
-def update_kernel(old_ref, above_ref, below_ref, prints_ref, wide_ref, places_ref, out_ref, whole_ref):
+    show_edges(field_ref, near_ref, up_ref, down_ref)
+
+
+def update_kernel(old_ref, above_ref, below_ref, prints_ref, wide_ref, near_ref, places_ref, out_ref, whole_ref):
     sub, lane = iotas()
-    add_halo(whole_ref, above_ref, below_ref)
+    add_halo(whole_ref, above_ref, below_ref, near_ref)
 
     def leaf(v, m):
         folded = []
@@ -241,7 +240,7 @@
 
 
 def trace_kernel(
-    parts_ref, old_ref, movie_ref, wide_ref, places_ref, new_ref, weight_ref, field_ref, up_ref, down_ref
+    parts_ref, old_ref, movie_ref, wide_ref, near_ref, places_ref, new_ref, weight_ref, field_ref, up_ref, down_ref
 ):
     sub, lane = iotas()
     start_field(movie_ref, field_ref)
@@ -267,12 +266,12 @@
         power = merge_rows(power, power, 2, sub)
         weight_ref[v] = value / (power + RIDGE)
     subtract_all(new_ref, wide_ref, places_ref, field_ref)
-    show_edges(field_ref, up_ref, down_ref)
-
-
-def improve_prints(above_ref, below_ref, weight_ref, prints_ref, places_ref, whole_ref, new_ref):
+    show_edges(field_ref, near_ref, up_ref, down_ref)
+
+
+def improve_prints(above_ref, below_ref, weight_ref, prints_ref, near_ref, places_ref, whole_ref, new_ref):
     sub, lane = iotas()
-    add_halo(whole_ref, above_ref, below_ref)
+    add_halo(whole_ref, above_ref, below_ref, near_ref)
 
     def tile(v, _):
         value = weight_ref[v]
@@ -305,20 +304,20 @@
 
 
 def print_kernel(
-    old_ref, above_ref, below_ref, weight_ref, activity_ref, movie_ref, prints_ref, places_ref,
+    old_ref, above_ref, below_ref, weight_ref, activity_ref, movie_ref, prints_ref, near_ref, places_ref,
     new_ref, wide_ref, next_ref, up_ref, down_ref, whole_ref,
 ):
-    improve_prints(above_ref, below_ref, weight_ref, prints_ref, places_ref, whole_ref, new_ref)
+    improve_prints(above_ref, below_ref, weight_ref, prints_ref, near_ref, places_ref, whole_ref, new_ref)
     widen(new_ref[...], wide_ref)
     start_field(movie_ref, next_ref)
     subtract_all(activity_ref, wide_ref, places_ref, next_ref)
-    show_edges(next_ref, up_ref, down_ref)
+    show_edges(next_ref, near_ref, up_ref, down_ref)
 
 
 def last_kernel(
-    old_ref, above_ref, below_ref, weight_ref, prints_ref, places_ref, out_ref, whole_ref, new_ref
+    old_ref, above_ref, below_ref, weight_ref, prints_ref, near_ref, places_ref, out_ref, whole_ref, new_ref
 ):
-    improve_prints(above_ref, below_ref, weight_ref, prints_ref, places_ref, whole_ref, new_ref)
+    improve_prints(above_ref, below_ref, weight_ref, prints_ref, near_ref, places_ref, whole_ref, new_ref)
     for j in range(TX):
         rows = new_ref[j * OWNED : (j + 1) * OWNED, :]
         for z in range(TA):
@@ -350,11 +349,11 @@
     return jax.ShapeDtypeStruct(sizes, dtype)
 
 
-def call(kernel, outs, places, scratch=(), smem=None, alias=None):
+def call(kernel, outs, places, scratch=(), smem=(), alias=None):
     return pl.pallas_call(
         kernel,
         out_shape=outs,
-        in_specs=[SMEM if at == smem else VMEM for at in range(places)],
+        in_specs=[SMEM if at in smem else VMEM for at in range(places)],
         out_specs=jax.tree.map(lambda _: VMEM, outs),
         scratch_shapes=list(scratch),
         input_output_aliases={} if alias is None else {0: alias},
@@ -372,26 +371,23 @@
     return lax.all_to_all(blocks, AXES, 0, 0, tiled=True)
 
 
-def halo(up, down):
-    ends = lax.axis_size("ty") - 1
-    above = lax.ppermute(down, "ty", [(i, i + 1) for i in range(ends)])
-    below = lax.ppermute(up, "ty", [(i + 1, i) for i in range(ends)])
-    return above, below
+def halo(near, far):
+    near = lax.ppermute(near, "ty", [(0, 1), (1, 0), (2, 3), (3, 2)])
+    return near, lax.ppermute(far, "ty", [(1, 2), (2, 1)])
 
 
 def shards(movie, footprints, traces, anchor_row, anchor_col):
     layer = lax.axis_index("ta")
     column = lax.axis_index("tx")
     frames = traces.shape[0]
+    index = lax.axis_index("ty")
+    near = (index % 2).reshape(1)
     blocks = movie.reshape(frames, 4, CELL_ROWS, TX, 2, 128).transpose(3, 1, 2, 0, 4, 5)
+    own = traces.reshape(frames, 8, 2, 4).transpose(2, 0, 1, 3).reshape(2, 128)
+    spots = jnp.concatenate([anchor_row, anchor_col]).astype(F32).reshape(1, 128)
     got = exchange(
-        call(pack_kernel, shape(GROUP, 192, 128, dtype=jnp.bfloat16), 6, smem=5)(
-            blocks.reshape(GROUP, 128, 128),
-            footprints,
-            traces,
-            anchor_row.reshape(1, OWNED),
-            anchor_col.reshape(1, OWNED),
-            layer.reshape(1),
+        call(pack_kernel, shape(GROUP, 168, 128, dtype=jnp.bfloat16), 4, smem=(3,))(
+            blocks.reshape(GROUP, 128, 128), footprints, jnp.concatenate([own, spots]), layer.reshape(1)
         )
     )
     cells, prints, activity, places = call(
@@ -400,38 +396,38 @@
         1,
     )(got)
     wide, field, up, down = call(
-        first_kernel, (WIDE_SHAPE, FIELD_SHAPE, EDGE_SHAPE, EDGE_SHAPE), 4, smem=3
-    )(cells, prints, activity, places)
+        first_kernel, (WIDE_SHAPE, FIELD_SHAPE, EDGE_SHAPE, EDGE_SHAPE), 5, smem=(3, 4)
+    )(cells, prints, activity, near, places)
     for sweep in range(ITERS):
         above, below = halo(up, down)
-        sums, _ = call(update_kernel, (shape(GROUP, 72, 128), FIELD_SHAPE), 6, smem=5, alias=1)(
-            field, above, below, prints, wide, places
+        sums, _ = call(update_kernel, (shape(GROUP, 72, 128), FIELD_SHAPE), 7, smem=(5, 6), alias=1)(
+            field, above, below, prints, wide, near, places
         )
         parts = exchange(sums)
         activity, weight, field, up, down = call(
             trace_kernel,
             (shape(TX, 8, 128), shape(TX, 8, 128), FIELD_SHAPE, EDGE_SHAPE, EDGE_SHAPE),
-            5,
-            smem=4,
-        )(parts, activity, cells, wide, places)
+            6,
+            smem=(4, 5),
+        )(parts, activity, cells, wide, near, places)
         above, below = halo(up, down)
         if sweep + 1 < ITERS:
             prints, wide, field, up, down, _ = call(
                 print_kernel,
                 (shape(COUNT, 128), WIDE_SHAPE, FIELD_SHAPE, EDGE_SHAPE, EDGE_SHAPE, FIELD_SHAPE),
-                8,
-                smem=7,
+                9,
+                smem=(7, 8),
                 alias=5,
-            )(field, above, below, weight, activity, cells, prints, places)
+            )(field, above, below, weight, activity, cells, prints, near, places)
         else:
             sent, _ = call(
                 last_kernel,
                 (shape(GROUP, OWNED, 128), FIELD_SHAPE),
-                6,
+                7,
                 (pltpu.VMEM((COUNT, 128), F32),),
-                smem=5,
+                smem=(5, 6),
                 alias=1,
-            )(field, above, below, weight, prints, places)
+            )(field, above, below, weight, prints, near, places)
     footprints_out = call(finish_kernel, shape(OWNED, 4096), 1)(exchange(sent))
     mine = lax.dynamic_index_in_dim(activity, column, 0, keepdims=False).reshape(2, TA, 128)
     mine = lax.dynamic_index_in_dim(mine, layer, 1, keepdims=False)

time: 178 us -> 163 us (0.916)
  blocking collectives: 66.4 us -> 33.9 us
  starting transfers between devices: 25.7 us -> 38 us
  waiting for transfers between devices: 39.6 us -> 46.4 us
    all_to_all x3 -> x2, blocking collectives: 66.4 us -> 33.9 us  [exchange(): return lax.all_to_all(blocks, AXES, 0, 0, tiled=True)]
    all_to_all x1 -> x2, waiting for transfers between devices: 11.4 us -> 29.1 us  [exchange(): return lax.all_to_all(blocks, AXES, 0, 0, tiled=True)]
    ppermute x8, waiting for transfers between devices: 28.2 us -> 17.4 us  [the longest x4 17.3 us: halo(): return (near, lax.ppermute(far, 'ty', [(1, 2), (2, 1)]))]
    all_to_all x1 -> x2, starting transfers between devices: 3.93 us -> 13.7 us  [exchange(): return lax.all_to_all(blocks, AXES, 0, 0, tiled=True)]
    ppermute x8, starting transfers between devices: 21.8 us -> 24.3 us  [the longest x4 21.9 us: halo(): return (near, lax.ppermute(far, 'ty', [(1, 2), (2, 1)]))]
    pallas_call x1, Pallas kernels: 5.09 us -> 2.78 us  [shards(): call(unpack_kernel, (shape(INNER, 128), shape(COUNT, 128), shape(TX, 8, 1...]
    unnamed x8 -> x2, local copies, waits for them, and re-layouts: 1.99 us -> 0.01 us
  transfers between devices with their start and end apart: 9 -> 10, of which waited for: 9 -> 6; matrix products, arithmetic and copies ran while one was open for 0% -> 1% of each run, Pallas kernels for 0% -> 0%
where the time goes in v3:
time: 163 us; the launch traced here: 162 us
  waiting for transfers between devices  46.4 us (28%)
  Pallas kernels  38 us (23%)
  starting transfers between devices  38 us (23%)
  blocking collectives  33.9 us (21%)
  local copies, waits for them, and re-layouts  4.14 us (3%)
    all_to_all x2, blocking collectives, exchange(): return lax.all_to_all(blocks, AXES, 0, 0, tiled=True)  33.9 us
    all_to_all x2, waiting for transfers between devices, exchange(): return lax.all_to_all(blocks, AXES, 0, 0, tiled=True)  29.1 us
    ppermute x4, starting transfers between devices, halo(): return (near, lax.ppermute(far, 'ty', [(1, 2), (2, 1)]))  21.9 us
    ppermute x4, waiting for transfers between devices, halo(): return (near, lax.ppermute(far, 'ty', [(1, 2), (2, 1)]))  17.3 us
    all_to_all x2, starting transfers between devices, exchange(): return lax.all_to_all(blocks, AXES, 0, 0, tiled=True)  13.7 us
    pallas_call x2, Pallas kernels, shards(): call(update_kernel, (shape(GROUP, 72, 128), FIELD_SHAPE), 7, smem=(5, 6),...  9.94 us
    pallas_call x1, Pallas kernels, shards(): call(print_kernel, (shape(COUNT, 128), WIDE_SHAPE, FIELD_SHAPE, EDGE_SHAP...  6.98 us
    pallas_call x2, Pallas kernels, shards(): call(trace_kernel, (shape(TX, 8, 128), shape(TX, 8, 128), FIELD_SHAPE, ED...  6.35 us
  transfers between devices with their start and end apart: 10, of which 6 were waited for; matrix products, arithmetic and copies ran while one was open for 1% of the time, Pallas kernels for 0%

profile of v3, /device:TPU:1, one launch (start us, length us, event | category | flops | bytes accessed | tf_op | source)
XLA Modules:
  0.0 162.2 jit_solution(10183486462799662365)
XLA Ops:
  0.6 0.0 copy-start
  0.6 0.9 reshape.65
  1.5 0.1 reshape.66
  1.6 2.3 %copy.16 = bf16[4,4,16,8,2,128]{5,4,0,2,1,3:T(2,128)(2,1)S(1)} copy(bf16[4,4,16,8,2,128]{5,4,3,2,1,0:T(2,128)(2,1)} %bitcast.14) | data formatting | bytes 2097152 | tf_op jit(solution)/shard_map/reshape | solution.py:385
  4.0 0.8 add_convert_fusion
  4.7 0.0 copy-done
  4.7 1.4 shard_map.68
  6.1 9.8 %all-to-all-start = ((bf16[32,168,128]{2,1,0:T(8,128)(2,1)}), bf16[32,168,128]{2,1,0:T(8,128)(2,1)S(1)}, u32[]{:S(2)}, u32[]{:S(2)}) async-start(bf16[32,168,128]{2,1,0:T(8,128)(2,1)} %shard_map.68), calls=%async_computation | async-start | bytes 2752512 | tf_op jit(solution)/shard_map/all_to_all | solution.py:371
  15.9 18.8 %all-to-all-done.got_ref = bf16[32,168,128]{2,1,0:T(8,128)(2,1)S(1)} async-done(((bf16[32,168,128]{2,1,0:T(8,128)(2,1)}), bf16[32,168,128]{2,1,0:T(8,128)(2,1)S(1)}, u32[]{:S(2)}, u32[]{:S(2)}) %all-to-all-start) | async-done | bytes 1376288 | tf_op jit(solution)/shard_map/all_to_all | solution.py:371
  34.7 2.8 %shard_map.69 = (f32[4224,128]{1,0:T(8,128)S(1)}, f32[512,128]{1,0:T(8,128)S(1)}, f32[8,8,128]{2,1,0:T(8,128)S(1)}, s32[8,128]{1,0:T(8,128)S(1)}) custom-call(bf16[32,168,128]{2,1,0:T(8,128)(2,1)S(1)} %all-to-all-done.got_ref), custom_call_target="tpu_custom_call" | custom-call | tf_op jit(solution)/shard_map/pallas_call | solution.py:393
  37.5 3.9 %shard_map.70 = (f32[4,512,128]{2,1,0:T(8,128)S(1)}, f32[4752,128]{1,0:T(8,128)S(1)}, f32[528,128]{1,0:T(8,128)S(1)}, f32[528,128]{1,0:T(8,128)S(1)}) custom-call(f32[4224,128]{1,0:T(8,128)S(1)} %get-tuple-element.28.movie_ref, f32[512,128]{1,0:T(8,128)S(1)} %get-tuple-element.29.prints_ref, f32[8,8,128]{2,1,0:T(8,128)S(1)} %get-tuple-element.30.activity_ref.old_ref, ...), custom_call_target="tpu_custom_call" | custom-call | tf_op jit(solution)/shard_map/pallas_call | solution.py:398
  41.4 2.1 %collective-permute-start = (f32[528,128]{1,0:T(8,128)S(1)}, f32[528,128]{1,0:T(8,128)S(1)}, u32[]{:S(2)}, u32[]{:S(2)}) collective-permute-start(f32[528,128]{1,0:T(8,128)S(1)} %get-tuple-element.33), channel_id=1, source_target_pairs={{0,32},{32,0},{64,96},{96,64},{1,33},{33,1},{65,97},{97,65},{2,34}... | collective-permute-start | bytes 811016 | tf_op jit(solution)/shard_map/ppermute | solution.py:375
  43.5 4.3 %collective-permute-start.1 = (f32[528,128]{1,0:T(8,128)S(1)}, f32[528,128]{1,0:T(8,128)S(1)}, u32[]{:S(2)}, u32[]{:S(2)}) collective-permute-start(f32[528,128]{1,0:T(8,128)S(1)} %get-tuple-element.34), channel_id=1, source_target_pairs={{32,64},{64,32},{33,65},{65,33},{34,66},{66,34},{35,67},{67,35},{3... | collective-permute-start | bytes 811016 | tf_op jit(solution)/shard_map/ppermute | solution.py:376
  47.8 0.0 collective-permute-done.above_ref
  47.8 5.0 %collective-permute-done.1.below_ref = f32[528,128]{1,0:T(8,128)S(1)} collective-permute-done((f32[528,128]{1,0:T(8,128)S(1)}, f32[528,128]{1,0:T(8,128)S(1)}, u32[]{:S(2)}, u32[]{:S(2)}) %collective-permute-start.1) | collective-permute-done | bytes 270368 | tf_op jit(solution)/shard_map/ppermute | solution.py:376
  52.8 5.0 %shard_map.71 = (f32[32,72,128]{2,1,0:T(8,128)S(1)}, f32[4752,128]{1,0:T(8,128)S(1)}) custom-call(f32[4752,128]{1,0:T(8,128)S(1)} %get-tuple-element.32.old_ref, f32[528,128]{1,0:T(8,128)S(1)} %collective-permute-done.above_ref, f32[528,128]{1,0:T(8,128)S(1)} %collective-permute-done.1.below_ref, ...), custom_call_target="tpu_custom_call", output_to_operand_aliasing={{1}: (0, {})} | custom-call | tf_op jit(solution)/shard_map/pallas_call | solution.py:403
  57.8 17.8 %all_to_all.20.parts_ref = f32[32,72,128]{2,1,0:T(8,128)S(1)} all-to-all(f32[32,72,128]{2,1,0:T(8,128)S(1)} %get-tuple-element.36), channel_id=1, replica_groups=mesh['ty'=4,'tx'=8,'ta'=4] {'tx','ta'}, dimensions={0} | all-to-all | bytes 2359296 | tf_op jit(solution)/shard_map/all_to_all | solution.py:371
  75.5 3.2 %shard_map.72 = (f32[8,8,128]{2,1,0:T(8,128)S(1)}, f32[8,8,128]{2,1,0:T(8,128)S(1)}, f32[4752,128]{1,0:T(8,128)S(1)}, f32[528,128]{1,0:T(8,128)S(1)}, f32[528,128]{1,0:T(8,128)S(1)}) custom-call(f32[32,72,128]{2,1,0:T(8,128)S(1)} %all_to_all.20.parts_ref, f32[8,8,128]{2,1,0:T(8,128)S(1)} %get-tuple-element.30.activity_ref.old_ref, ...), custom_call_target="tpu_custom_call" | custom-call | tf_op jit(solution)/shard_map/pallas_call | solution.py:407
  78.7 0.1 collective-permute-start.2
  78.8 5.7 %collective-permute-start.3 = (f32[528,128]{1,0:T(8,128)S(1)}, f32[528,128]{1,0:T(8,128)S(1)}, u32[]{:S(2)}, u32[]{:S(2)}) collective-permute-start(f32[528,128]{1,0:T(8,128)S(1)} %get-tuple-element.39), channel_id=1, source_target_pairs={{32,64},{64,32},{33,65},{65,33},{34,66},{66,34},{35,67},{67,35},{3... | collective-permute-start | bytes 811016 | tf_op jit(solution)/shard_map/ppermute | solution.py:376
  84.6 0.0 collective-permute-done.2.above_ref
  84.6 4.1 %collective-permute-done.3.below_ref = f32[528,128]{1,0:T(8,128)S(1)} collective-permute-done((f32[528,128]{1,0:T(8,128)S(1)}, f32[528,128]{1,0:T(8,128)S(1)}, u32[]{:S(2)}, u32[]{:S(2)}) %collective-permute-start.3) | collective-permute-done | bytes 270368 | tf_op jit(solution)/shard_map/ppermute | solution.py:376
  88.7 7.0 %shard_map.73 = (f32[512,128]{1,0:T(8,128)S(1)}, f32[4,512,128]{2,1,0:T(8,128)S(1)}, f32[4752,128]{1,0:T(8,128)S(1)}, f32[528,128]{1,0:T(8,128)S(1)}, f32[528,128]{1,0:T(8,128)S(1)}, /*index=5*/f32[4752,128]{1,0:T(8,128)S(1)}) custom-call(f32[4752,128]{1,0:T(8,128)S(1)} %get-tuple-element.37.old_ref, ...), custom_call_target="tpu_custom_call", output_to_operand_aliasing={{5}: (0, {})} | custom-call | tf_op jit(solution)/shard_map/pallas_call | solution.py:415
  95.7 0.1 collective-permute-start.4
  95.8 5.2 %collective-permute-start.5 = (f32[528,128]{1,0:T(8,128)S(1)}, f32[528,128]{1,0:T(8,128)S(1)}, u32[]{:S(2)}, u32[]{:S(2)}) collective-permute-start(f32[528,128]{1,0:T(8,128)S(1)} %get-tuple-element.44), channel_id=1, source_target_pairs={{32,64},{64,32},{33,65},{65,33},{34,66},{66,34},{35,67},{67,35},{3... | collective-permute-start | bytes 811016 | tf_op jit(solution)/shard_map/ppermute | solution.py:376
  100.9 0.0 collective-permute-done.4.above_ref
  101.0 4.1 %collective-permute-done.5.below_ref = f32[528,128]{1,0:T(8,128)S(1)} collective-permute-done((f32[528,128]{1,0:T(8,128)S(1)}, f32[528,128]{1,0:T(8,128)S(1)}, u32[]{:S(2)}, u32[]{:S(2)}) %collective-permute-start.5) | collective-permute-done | bytes 270368 | tf_op jit(solution)/shard_map/ppermute | solution.py:376
  105.1 5.0 %shard_map.74 = (f32[32,72,128]{2,1,0:T(8,128)S(1)}, f32[4752,128]{1,0:T(8,128)S(1)}) custom-call(f32[4752,128]{1,0:T(8,128)S(1)} %get-tuple-element.42.old_ref, f32[528,128]{1,0:T(8,128)S(1)} %collective-permute-done.4.above_ref, f32[528,128]{1,0:T(8,128)S(1)} %collective-permute-done.5.below_ref, ...), custom_call_target="tpu_custom_call", output_to_operand_aliasing={{1}: (0, {})} | custom-call | tf_op jit(solution)/shard_map/pallas_call | solution.py:403
  110.1 16.2 %all_to_all.21.parts_ref = f32[32,72,128]{2,1,0:T(8,128)S(1)} all-to-all(f32[32,72,128]{2,1,0:T(8,128)S(1)} %get-tuple-element.47), channel_id=1, replica_groups=mesh['ty'=4,'tx'=8,'ta'=4] {'tx','ta'}, dimensions={0} | all-to-all | bytes 2359296 | tf_op jit(solution)/shard_map/all_to_all | solution.py:371
  126.2 3.2 %shard_map.75 = (f32[8,8,128]{2,1,0:T(8,128)S(1)}, f32[8,8,128]{2,1,0:T(8,128)S(1)}, f32[4752,128]{1,0:T(8,128)S(1)}, f32[528,128]{1,0:T(8,128)S(1)}, f32[528,128]{1,0:T(8,128)S(1)}) custom-call(f32[32,72,128]{2,1,0:T(8,128)S(1)} %all_to_all.21.parts_ref, f32[8,8,128]{2,1,0:T(8,128)S(1)} %get-tuple-element.41.activity_ref.old_ref, ...), custom_call_target="tpu_custom_call" | custom-call | tf_op jit(solution)/shard_map/pallas_call | solution.py:407
  129.4 0.1 collective-permute-start.6
  129.5 6.8 %collective-permute-start.7 = (f32[528,128]{1,0:T(8,128)S(1)}, f32[528,128]{1,0:T(8,128)S(1)}, u32[]{:S(2)}, u32[]{:S(2)}) collective-permute-start(f32[528,128]{1,0:T(8,128)S(1)} %get-tuple-element.50), channel_id=1, source_target_pairs={{32,64},{64,32},{33,65},{65,33},{34,66},{66,34},{35,67},{67,35},{3... | collective-permute-start | bytes 811016 | tf_op jit(solution)/shard_map/ppermute | solution.py:376
  136.3 0.0 collective-permute-done.6.above_ref
  136.3 4.1 %collective-permute-done.7.below_ref = f32[528,128]{1,0:T(8,128)S(1)} collective-permute-done((f32[528,128]{1,0:T(8,128)S(1)}, f32[528,128]{1,0:T(8,128)S(1)}, u32[]{:S(2)}, u32[]{:S(2)}) %collective-permute-start.7) | collective-permute-done | bytes 270368 | tf_op jit(solution)/shard_map/ppermute | solution.py:376
  140.4 4.7 %shard_map.76 = (f32[32,64,128]{2,1,0:T(8,128)}, f32[4752,128]{1,0:T(8,128)S(1)}) custom-call(f32[4752,128]{1,0:T(8,128)S(1)} %get-tuple-element.48.old_ref, f32[528,128]{1,0:T(8,128)S(1)} %collective-permute-done.6.above_ref, f32[528,128]{1,0:T(8,128)S(1)} %collective-permute-done.7.below_ref, ...), custom_call_target="tpu_custom_call", output_to_operand_aliasing={{1}: (0, {})} | custom-call | tf_op jit(solution)/shard_map/pallas_call | solution.py:423
  145.1 3.9 %all-to-all-start.3 = ((f32[32,64,128]{2,1,0:T(8,128)}), f32[32,64,128]{2,1,0:T(8,128)S(1)}, u32[]{:S(2)}, u32[]{:S(2)}) async-start(f32[32,64,128]{2,1,0:T(8,128)} %get-tuple-element.52), calls=%async_computation.3 | async-start | bytes 2097152 | tf_op jit(solution)/shard_map/all_to_all | solution.py:371
  149.1 0.1 reshape.70
  149.3 0.7 reshape.71
  149.9 10.3 %all-to-all-done.3.blocks_ref = f32[32,64,128]{2,1,0:T(8,128)S(1)} async-done(((f32[32,64,128]{2,1,0:T(8,128)}), f32[32,64,128]{2,1,0:T(8,128)S(1)}, u32[]{:S(2)}, u32[]{:S(2)}) %all-to-all-start.3) | async-done | bytes 1048608 | tf_op jit(solution)/shard_map/all_to_all | solution.py:371
  160.2 2.0 %shard_map.77 = f32[64,4096]{1,0:T(8,128)} custom-call(f32[32,64,128]{2,1,0:T(8,128)S(1)} %all-to-all-done.3.blocks_ref), custom_call_target="tpu_custom_call" | custom-call | tf_op jit(solution)/shard_map/pallas_call | solution.py:431
  (5 shorter events, 0.1 us)
Async XLA Ops:
  0.6 4.1 %copy-start = (f32[64,4096]{1,0:T(8,128)S(1)}, f32[64,4096]{1,0:T(8,128)}, u32[]{:S(2)}) copy-start(f32[64,4096]{1,0:T(8,128)} %prints_ref.1) | copy-start | bytes 3145732
  6.1 28.6 %all-to-all-start = ((bf16[32,168,128]{2,1,0:T(8,128)(2,1)}), bf16[32,168,128]{2,1,0:T(8,128)(2,1)S(1)}, u32[]{:S(2)}, u32[]{:S(2)}) async-start(bf16[32,168,128]{2,1,0:T(8,128)(2,1)} %shard_map.68), calls=%async_computation | async-start | bytes 2752512 | tf_op jit(solution)/shard_map/all_to_all | solution.py:371
  41.4 6.4 %collective-permute-start = (f32[528,128]{1,0:T(8,128)S(1)}, f32[528,128]{1,0:T(8,128)S(1)}, u32[]{:S(2)}, u32[]{:S(2)}) collective-permute-start(f32[528,128]{1,0:T(8,128)S(1)} %get-tuple-element.33), channel_id=1, source_target_pairs={{0,32},{32,0},{64,96},{96,64},{1,33},{33,1},{65,97},{97,65},{2,34}... | collective-permute-start | bytes 811016 | tf_op jit(solution)/shard_map/ppermute | solution.py:375
  43.5 9.3 %collective-permute-start.1 = (f32[528,128]{1,0:T(8,128)S(1)}, f32[528,128]{1,0:T(8,128)S(1)}, u32[]{:S(2)}, u32[]{:S(2)}) collective-permute-start(f32[528,128]{1,0:T(8,128)S(1)} %get-tuple-element.34), channel_id=1, source_target_pairs={{32,64},{64,32},{33,65},{65,33},{34,66},{66,34},{35,67},{67,35},{3... | collective-permute-start | bytes 811016 | tf_op jit(solution)/shard_map/ppermute | solution.py:376
  78.7 5.8 %collective-permute-start.2 = (f32[528,128]{1,0:T(8,128)S(1)}, f32[528,128]{1,0:T(8,128)S(1)}, u32[]{:S(2)}, u32[]{:S(2)}) collective-permute-start(f32[528,128]{1,0:T(8,128)S(1)} %get-tuple-element.38), channel_id=1, source_target_pairs={{0,32},{32,0},{64,96},{96,64},{1,33},{33,1},{65,97},{97,65},{2,34}... | collective-permute-start | bytes 811016 | tf_op jit(solution)/shard_map/ppermute | solution.py:375
  78.8 9.9 %collective-permute-start.3 = (f32[528,128]{1,0:T(8,128)S(1)}, f32[528,128]{1,0:T(8,128)S(1)}, u32[]{:S(2)}, u32[]{:S(2)}) collective-permute-start(f32[528,128]{1,0:T(8,128)S(1)} %get-tuple-element.39), channel_id=1, source_target_pairs={{32,64},{64,32},{33,65},{65,33},{34,66},{66,34},{35,67},{67,35},{3... | collective-permute-start | bytes 811016 | tf_op jit(solution)/shard_map/ppermute | solution.py:376
  95.7 5.3 %collective-permute-start.4 = (f32[528,128]{1,0:T(8,128)S(1)}, f32[528,128]{1,0:T(8,128)S(1)}, u32[]{:S(2)}, u32[]{:S(2)}) collective-permute-start(f32[528,128]{1,0:T(8,128)S(1)} %get-tuple-element.43), channel_id=1, source_target_pairs={{0,32},{32,0},{64,96},{96,64},{1,33},{33,1},{65,97},{97,65},{2,34}... | collective-permute-start | bytes 811016 | tf_op jit(solution)/shard_map/ppermute | solution.py:375
  95.8 9.3 %collective-permute-start.5 = (f32[528,128]{1,0:T(8,128)S(1)}, f32[528,128]{1,0:T(8,128)S(1)}, u32[]{:S(2)}, u32[]{:S(2)}) collective-permute-start(f32[528,128]{1,0:T(8,128)S(1)} %get-tuple-element.44), channel_id=1, source_target_pairs={{32,64},{64,32},{33,65},{65,33},{34,66},{66,34},{35,67},{67,35},{3... | collective-permute-start | bytes 811016 | tf_op jit(solution)/shard_map/ppermute | solution.py:376
  129.4 6.9 %collective-permute-start.6 = (f32[528,128]{1,0:T(8,128)S(1)}, f32[528,128]{1,0:T(8,128)S(1)}, u32[]{:S(2)}, u32[]{:S(2)}) collective-permute-start(f32[528,128]{1,0:T(8,128)S(1)} %get-tuple-element.49), channel_id=1, source_target_pairs={{0,32},{32,0},{64,96},{96,64},{1,33},{33,1},{65,97},{97,65},{2,34}... | collective-permute-start | bytes 811016 | tf_op jit(solution)/shard_map/ppermute | solution.py:375
  129.5 10.9 %collective-permute-start.7 = (f32[528,128]{1,0:T(8,128)S(1)}, f32[528,128]{1,0:T(8,128)S(1)}, u32[]{:S(2)}, u32[]{:S(2)}) collective-permute-start(f32[528,128]{1,0:T(8,128)S(1)} %get-tuple-element.50), channel_id=1, source_target_pairs={{32,64},{64,32},{33,65},{65,33},{34,66},{66,34},{35,67},{67,35},{3... | collective-permute-start | bytes 811016 | tf_op jit(solution)/shard_map/ppermute | solution.py:376
  145.1 15.1 %all-to-all-start.3 = ((f32[32,64,128]{2,1,0:T(8,128)}), f32[32,64,128]{2,1,0:T(8,128)S(1)}, u32[]{:S(2)}, u32[]{:S(2)}) async-start(f32[32,64,128]{2,1,0:T(8,128)} %get-tuple-element.52), calls=%async_computation.3 | async-start | bytes 2097152 | tf_op jit(solution)/shard_map/all_to_all | solution.py:371

commit v4 on v3

--- a/solution.py
+++ b/solution.py
@@ -20,6 +20,7 @@
 INNER = CELL_ROWS * ROW
 VMEM = pl.BlockSpec(memory_space=pltpu.VMEM)
 SMEM = pl.BlockSpec(memory_space=pltpu.SMEM)
+ANY = pl.BlockSpec(memory_space=pl.ANY)
 F32 = jnp.float32
 
 
@@ -64,11 +65,20 @@
     return jnp.where(low, wide, turned), jnp.where(low, turned, wide)
 
 
+def pieces(value, count):
+    out = []
+    for _ in range(count):
+        out.append(value.astype(jnp.bfloat16))
+        value = value - out[-1].astype(F32)
+    return out
+
+
 def widen(prints, wide_ref):
-    source = lax.broadcasted_iota(jnp.int32, (128, 512), 0)
-    target = lax.broadcasted_iota(jnp.int32, (128, 512), 1)
-    copies = (source == (target >> 7) * 32 + (target & 31)).astype(F32)
-    wide = jnp.dot(prints, copies, precision=lax.Precision.HIGHEST, preferred_element_type=F32)
+    source = lax.broadcasted_iota(jnp.int32, (384, 512), 0) & 127
+    target = lax.broadcasted_iota(jnp.int32, (384, 512), 1)
+    copies = (source == (target >> 7) * 32 + (target & 31)).astype(jnp.bfloat16)
+    parts = jnp.concatenate(pieces(prints, 3), axis=1)
+    wide = jnp.dot(parts, copies, preferred_element_type=F32)
     for d in range(4):
         wide_ref[d] = wide[:, 128 * d : 128 * d + 128]
 
@@ -131,14 +141,6 @@
     bottom = field_ref[INNER:, :]
     near_out[...] = jnp.where(even, bottom, top)
     far_out[...] = jnp.where(even, top, bottom)
-
-
-def pieces(value, count):
-    out = []
-    for _ in range(count):
-        out.append(value.astype(jnp.bfloat16))
-        value = value - out[-1].astype(F32)
-    return out
 
 
 def pack_kernel(cells_ref, prints_ref, small_ref, layer_ref, out_ref):
@@ -224,19 +226,21 @@
             out_ref[g, pl.ds(pl.multiple_of(v * 8, 8), 8), :] = total
         return 0
 
-    lax.fori_loop(0, TX, tile, 0)
-
-    def squares(k, level):
-        if level == 0:
-            rows = prints_ref[pl.ds(k, 8, stride=OWNED), :]
-            return rows * rows
-        shift = 1 << (level - 1)
-        return merge_lanes(squares(k, level - 1), squares(k + shift, level - 1), shift, lane)
-
-    energy = squares(0, 6)
-    energy = energy + pltpu.roll(energy, 64, 1)
+    lax.fori_loop(0, TX, tile, 0, unroll=2)
+
+    squares = prints_ref[...] * prints_ref[...]
+    energy = lax.dot_general(
+        jnp.ones((8, 128), F32),
+        squares,
+        (((1,), (1,)), ((), ())),
+        precision=lax.Precision.HIGHEST,
+        preferred_element_type=F32,
+    )
+    rows = energy[:, 0:128]
+    for q in range(1, 4):
+        rows = jnp.where(sub == q, energy[:, 128 * q : 128 * q + 128], rows)
     for g in range(GROUP):
-        out_ref[g, 64:72, :] = energy
+        out_ref[g, 64:72, :] = rows
 
 
 def trace_kernel(
@@ -256,7 +260,7 @@
     m = lane & 31
     own = (m >> 2) * 8 + (m & 3) + jnp.where(sub < 4, 0, 4)
     for v in range(TX):
-        scale = pick_lanes(jnp.broadcast_to(energy[v : v + 1], (8, 128)), own)
+        scale = pick_lanes(jnp.broadcast_to(energy[v // 2 : v // 2 + 1], (8, 128)), own + 64 * (v % 2))
         value = jnp.maximum(old_ref[v] + total(8 * v) / (scale + RIDGE), 0.0)
         new_ref[v] = value
         power = value * value
@@ -269,7 +273,9 @@
     show_edges(field_ref, near_ref, up_ref, down_ref)
 
 
-def improve_prints(above_ref, below_ref, weight_ref, prints_ref, near_ref, places_ref, whole_ref, new_ref):
+def improve_prints(
+    above_ref, below_ref, weight_ref, prints_ref, near_ref, places_ref, whole_ref, new_ref, after=lambda v: None
+):
     sub, lane = iotas()
     add_halo(whole_ref, above_ref, below_ref, near_ref)
 
@@ -278,19 +284,20 @@
 
         def eight(q, _):
             base = pl.multiple_of(v * OWNED + q * 8, 8)
-            folded = []
+            terms = []
             for b in range(4):
                 pair = spread(value, q * 4 + b, sub, lane)
-                sides = []
                 for half in range(2):
-                    top, bottom = patch(v, q * 8 + half * 4 + b, places_ref)
-                    sides.append(
-                        merge_lanes(pair[half] * whole_ref[top, :], pair[half] * whole_ref[bottom, :], 64, lane)
-                    )
-                folded.append(merge_lanes(sides[0], sides[1], 32, lane))
-            low = merge_rows(folded[0], folded[1], 1, sub)
-            high = merge_rows(folded[2], folded[3], 1, sub)
-            step = merge_rows(low, high, 2, sub)
+                    for at in patch(v, q * 8 + half * 4 + b, places_ref):
+                        terms.append(pair[half] * whole_ref[at, :])
+            sides = []
+            for n in range(4):
+                low = merge_rows(terms[n], terms[4 + n], 1, sub)
+                high = merge_rows(terms[8 + n], terms[12 + n], 1, sub)
+                sides.append(merge_rows(low, high, 2, sub))
+            step = merge_lanes(
+                merge_lanes(sides[0], sides[1], 64, lane), merge_lanes(sides[2], sides[3], 64, lane), 32, lane
+            )
             turned = pltpu.roll(step, 4, 0)
             dx = (lane & 32) != 0
             swapped = jnp.where(dx, pltpu.roll(turned, 32, 1), pltpu.roll(turned, 96, 1))
@@ -298,7 +305,9 @@
             new_ref[pl.ds(base, 8), :] = jnp.maximum(prints_ref[pl.ds(base, 8), :] + step, 0.0)
             return 0
 
-        return lax.fori_loop(0, 8, eight, 0, unroll=8)
+        lax.fori_loop(0, 8, eight, 0, unroll=8)
+        after(v)
+        return 0
 
     lax.fori_loop(0, TX, tile, 0)
 
@@ -315,13 +324,20 @@
 
 
 def last_kernel(
-    old_ref, above_ref, below_ref, weight_ref, prints_ref, near_ref, places_ref, out_ref, whole_ref, new_ref
+    old_ref, above_ref, below_ref, weight_ref, prints_ref, near_ref, places_ref, out_ref, whole_ref, new_ref, sems
 ):
-    improve_prints(above_ref, below_ref, weight_ref, prints_ref, near_ref, places_ref, whole_ref, new_ref)
-    for j in range(TX):
-        rows = new_ref[j * OWNED : (j + 1) * OWNED, :]
+    def copy(v, z):
+        rows = new_ref.at[pl.ds(pl.multiple_of(v * OWNED, OWNED), OWNED)]
+        return pltpu.make_async_copy(rows, out_ref.at[v * TA + z], sems.at[v * TA + z])
+
+    def send(v):
         for z in range(TA):
-            out_ref[j * TA + z] = rows
+            copy(v, z).start()
+
+    improve_prints(above_ref, below_ref, weight_ref, prints_ref, near_ref, places_ref, whole_ref, new_ref, send)
+    for v in range(TX):
+        for z in range(TA):
+            copy(v, z).wait()
 
 
 def swap_lanes(parts, lane):
@@ -335,26 +351,32 @@
     return parts
 
 
-def finish_kernel(blocks_ref, out_ref):
+def finish_kernel(blocks_ref, out_ref, rows_ref, sems):
     lane = lax.broadcasted_iota(jnp.int32, (OWNED, 128), 1)
+    copies = []
     for z in range(TA):
         for a in range(2):
             rows = swap_lanes([blocks_ref[(4 * a + b) * TA + z] for b in range(4)], lane)
             for d in range(4):
-                start = d * 1024 + (z * 2 + a) * 128
-                out_ref[:, start : start + 128] = rows[d]
+                at = len(copies)
+                rows_ref[at] = rows[d]
+                columns = pl.ds(d * 1024 + (z * 2 + a) * 128, 128)
+                copies.append(pltpu.make_async_copy(rows_ref.at[at], out_ref.at[:, columns], sems.at[at]))
+                copies[-1].start()
+    for copy in copies:
+        copy.wait()
 
 
 def shape(*sizes, dtype=F32):
     return jax.ShapeDtypeStruct(sizes, dtype)
 
 
-def call(kernel, outs, places, scratch=(), smem=(), alias=None):
+def call(kernel, outs, places, scratch=(), smem=(), alias=None, left=()):
     return pl.pallas_call(
         kernel,
-        out_shape=outs,
+        out_shape=list(outs),
         in_specs=[SMEM if at in smem else VMEM for at in range(places)],
-        out_specs=jax.tree.map(lambda _: VMEM, outs),
+        out_specs=[ANY if at in left else VMEM for at in range(len(outs))],
         scratch_shapes=list(scratch),
         input_output_aliases={} if alias is None else {0: alias},
         compiler_params=pltpu.CompilerParams(vmem_limit_bytes=16 << 20),
@@ -386,9 +408,14 @@
     own = traces.reshape(frames, 8, 2, 4).transpose(2, 0, 1, 3).reshape(2, 128)
     spots = jnp.concatenate([anchor_row, anchor_col]).astype(F32).reshape(1, 128)
     got = exchange(
-        call(pack_kernel, shape(GROUP, 168, 128, dtype=jnp.bfloat16), 4, smem=(3,))(
+        call(
+            pack_kernel,
+            (shape(GROUP, 168, 128, dtype=jnp.bfloat16),),
+            4,
+            smem=(3,),
+        )(
             blocks.reshape(GROUP, 128, 128), footprints, jnp.concatenate([own, spots]), layer.reshape(1)
-        )
+        )[0]
     )
     cells, prints, activity, places = call(
         unpack_kernel,
@@ -424,11 +451,18 @@
                 last_kernel,
                 (shape(GROUP, OWNED, 128), FIELD_SHAPE),
                 7,
-                (pltpu.VMEM((COUNT, 128), F32),),
+                (pltpu.VMEM((COUNT, 128), F32), pltpu.SemaphoreType.DMA((GROUP,))),
+                left=(0,),
                 smem=(5, 6),
                 alias=1,
             )(field, above, below, weight, prints, near, places)
-    footprints_out = call(finish_kernel, shape(OWNED, 4096), 1)(exchange(sent))
+    footprints_out = call(
+        finish_kernel,
+        (shape(OWNED, 4096),),
+        1,
+        (pltpu.VMEM((GROUP, OWNED, 128), F32), pltpu.SemaphoreType.DMA((GROUP,))),
+        left=(0,),
+    )(exchange(sent))[0]
     mine = lax.dynamic_index_in_dim(activity, column, 0, keepdims=False).reshape(2, TA, 128)
     mine = lax.dynamic_index_in_dim(mine, layer, 1, keepdims=False)
     traces_out = mine.reshape(2, frames, 8, 4).transpose(1, 2, 0, 3).reshape(frames, OWNED)

time: 163 us -> 158 us (0.969)
  Pallas kernels: 38 us -> 33.5 us
    pallas_call x2, Pallas kernels: 9.94 us -> 6.55 us  [shards(): call(update_kernel, (shape(GROUP, 72, 128), FIELD_SHAPE), 7, smem=(5, 6),...]
where the time goes in v4:
time: 158 us
  waiting for transfers between devices  46.5 us (29%)
  starting transfers between devices  38 us (24%)
  blocking collectives  33.9 us (21%)
  Pallas kernels  33.5 us (21%)
  local copies, waits for them, and re-layouts  4.14 us (3%)
    all_to_all x2, blocking collectives, exchange(): return lax.all_to_all(blocks, AXES, 0, 0, tiled=True)  33.9 us
    all_to_all x2, waiting for transfers between devices, exchange(): return lax.all_to_all(blocks, AXES, 0, 0, tiled=True)  29.1 us
    ppermute x4, starting transfers between devices, halo(): return (near, lax.ppermute(far, 'ty', [(1, 2), (2, 1)]))  21.8 us
    ppermute x4, waiting for transfers between devices, halo(): return (near, lax.ppermute(far, 'ty', [(1, 2), (2, 1)]))  17.4 us
    all_to_all x2, starting transfers between devices, exchange(): return lax.all_to_all(blocks, AXES, 0, 0, tiled=True)  13.7 us
    pallas_call x2, Pallas kernels, shards(): call(update_kernel, (shape(GROUP, 72, 128), FIELD_SHAPE), 7, smem=(5, 6),...  6.55 us
    pallas_call x1, Pallas kernels, shards(): call(print_kernel, (shape(COUNT, 128), WIDE_SHAPE, FIELD_SHAPE, EDGE_SHAP...  6.47 us
    pallas_call x2, Pallas kernels, shards(): call(trace_kernel, (shape(TX, 8, 128), shape(TX, 8, 128), FIELD_SHAPE, ED...  6.37 us
  transfers between devices with their start and end apart: 10, of which 6 were waited for; matrix products, arithmetic and copies ran while one was open for 1% of the time, Pallas kernels for 0%

profile of v4, /device:TPU:1, one launch (start us, length us, event | category | flops | bytes accessed | tf_op | source)
XLA Modules:
  0.0 157.6 jit_solution(16675891441540159904)
XLA Ops:
  0.6 0.0 copy-start
  0.6 0.9 reshape.65
  1.5 0.1 reshape.66
  1.6 2.3 %copy.16 = bf16[4,4,16,8,2,128]{5,4,0,2,1,3:T(2,128)(2,1)S(1)} copy(bf16[4,4,16,8,2,128]{5,4,3,2,1,0:T(2,128)(2,1)} %bitcast.14) | data formatting | bytes 2097152 | tf_op jit(solution)/shard_map/reshape | solution.py:407
  4.0 0.8 add_convert_fusion
  4.7 0.0 copy-done
  4.7 1.4 shard_map.68
  6.1 9.8 %all-to-all-start = ((bf16[32,168,128]{2,1,0:T(8,128)(2,1)}), bf16[32,168,128]{2,1,0:T(8,128)(2,1)S(1)}, u32[]{:S(2)}, u32[]{:S(2)}) async-start(bf16[32,168,128]{2,1,0:T(8,128)(2,1)} %shard_map.68), calls=%async_computation | async-start | bytes 2752512 | tf_op jit(solution)/shard_map/all_to_all | solution.py:393
  15.9 18.8 %all-to-all-done.got_ref = bf16[32,168,128]{2,1,0:T(8,128)(2,1)S(1)} async-done(((bf16[32,168,128]{2,1,0:T(8,128)(2,1)}), bf16[32,168,128]{2,1,0:T(8,128)(2,1)S(1)}, u32[]{:S(2)}, u32[]{:S(2)}) %all-to-all-start) | async-done | bytes 1376288 | tf_op jit(solution)/shard_map/all_to_all | solution.py:393
  34.7 2.8 %shard_map.69 = (f32[4224,128]{1,0:T(8,128)S(1)}, f32[512,128]{1,0:T(8,128)S(1)}, f32[8,8,128]{2,1,0:T(8,128)S(1)}, s32[8,128]{1,0:T(8,128)S(1)}) custom-call(bf16[32,168,128]{2,1,0:T(8,128)(2,1)S(1)} %all-to-all-done.got_ref), custom_call_target="tpu_custom_call" | custom-call | tf_op jit(solution)/shard_map/pallas_call | solution.py:420
  37.5 3.4 %shard_map.70 = (f32[4,512,128]{2,1,0:T(8,128)S(1)}, f32[4752,128]{1,0:T(8,128)S(1)}, f32[528,128]{1,0:T(8,128)S(1)}, f32[528,128]{1,0:T(8,128)S(1)}) custom-call(f32[4224,128]{1,0:T(8,128)S(1)} %get-tuple-element.28.movie_ref, f32[512,128]{1,0:T(8,128)S(1)} %get-tuple-element.29.prints_ref, f32[8,8,128]{2,1,0:T(8,128)S(1)} %get-tuple-element.30.activity_ref.old_ref, ...), custom_call_target="tpu_custom_call" | custom-call | tf_op jit(solution)/shard_map/pallas_call | solution.py:425
  40.9 2.1 %collective-permute-start = (f32[528,128]{1,0:T(8,128)S(1)}, f32[528,128]{1,0:T(8,128)S(1)}, u32[]{:S(2)}, u32[]{:S(2)}) collective-permute-start(f32[528,128]{1,0:T(8,128)S(1)} %get-tuple-element.33), channel_id=1, source_target_pairs={{0,32},{32,0},{64,96},{96,64},{1,33},{33,1},{65,97},{97,65},{2,34}... | collective-permute-start | bytes 811016 | tf_op jit(solution)/shard_map/ppermute | solution.py:397
  43.0 4.3 %collective-permute-start.1 = (f32[528,128]{1,0:T(8,128)S(1)}, f32[528,128]{1,0:T(8,128)S(1)}, u32[]{:S(2)}, u32[]{:S(2)}) collective-permute-start(f32[528,128]{1,0:T(8,128)S(1)} %get-tuple-element.34), channel_id=1, source_target_pairs={{32,64},{64,32},{33,65},{65,33},{34,66},{66,34},{35,67},{67,35},{3... | collective-permute-start | bytes 811016 | tf_op jit(solution)/shard_map/ppermute | solution.py:398
  47.3 0.0 collective-permute-done.above_ref
  47.3 5.0 %collective-permute-done.1.below_ref = f32[528,128]{1,0:T(8,128)S(1)} collective-permute-done((f32[528,128]{1,0:T(8,128)S(1)}, f32[528,128]{1,0:T(8,128)S(1)}, u32[]{:S(2)}, u32[]{:S(2)}) %collective-permute-start.1) | collective-permute-done | bytes 270368 | tf_op jit(solution)/shard_map/ppermute | solution.py:398
  52.3 3.3 %shard_map.71 = (f32[32,72,128]{2,1,0:T(8,128)S(1)}, f32[4752,128]{1,0:T(8,128)S(1)}) custom-call(f32[4752,128]{1,0:T(8,128)S(1)} %get-tuple-element.32.old_ref, f32[528,128]{1,0:T(8,128)S(1)} %collective-permute-done.above_ref, f32[528,128]{1,0:T(8,128)S(1)} %collective-permute-done.1.below_ref, ...), custom_call_target="tpu_custom_call", output_to_operand_aliasing={{1}: (0, {})} | custom-call | tf_op jit(solution)/shard_map/pallas_call | solution.py:430
  55.5 17.8 %all_to_all.20.parts_ref = f32[32,72,128]{2,1,0:T(8,128)S(1)} all-to-all(f32[32,72,128]{2,1,0:T(8,128)S(1)} %get-tuple-element.36), channel_id=1, replica_groups=mesh['ty'=4,'tx'=8,'ta'=4] {'tx','ta'}, dimensions={0} | all-to-all | bytes 2359296 | tf_op jit(solution)/shard_map/all_to_all | solution.py:393
  73.3 3.2 %shard_map.72 = (f32[8,8,128]{2,1,0:T(8,128)S(1)}, f32[8,8,128]{2,1,0:T(8,128)S(1)}, f32[4752,128]{1,0:T(8,128)S(1)}, f32[528,128]{1,0:T(8,128)S(1)}, f32[528,128]{1,0:T(8,128)S(1)}) custom-call(f32[32,72,128]{2,1,0:T(8,128)S(1)} %all_to_all.20.parts_ref, f32[8,8,128]{2,1,0:T(8,128)S(1)} %get-tuple-element.30.activity_ref.old_ref, ...), custom_call_target="tpu_custom_call" | custom-call | tf_op jit(solution)/shard_map/pallas_call | solution.py:434
  76.5 0.1 collective-permute-start.2
  76.6 5.7 %collective-permute-start.3 = (f32[528,128]{1,0:T(8,128)S(1)}, f32[528,128]{1,0:T(8,128)S(1)}, u32[]{:S(2)}, u32[]{:S(2)}) collective-permute-start(f32[528,128]{1,0:T(8,128)S(1)} %get-tuple-element.39), channel_id=1, source_target_pairs={{32,64},{64,32},{33,65},{65,33},{34,66},{66,34},{35,67},{67,35},{3... | collective-permute-start | bytes 811016 | tf_op jit(solution)/shard_map/ppermute | solution.py:398
  82.3 0.0 collective-permute-done.2.above_ref
  82.3 4.1 %collective-permute-done.3.below_ref = f32[528,128]{1,0:T(8,128)S(1)} collective-permute-done((f32[528,128]{1,0:T(8,128)S(1)}, f32[528,128]{1,0:T(8,128)S(1)}, u32[]{:S(2)}, u32[]{:S(2)}) %collective-permute-start.3) | collective-permute-done | bytes 270368 | tf_op jit(solution)/shard_map/ppermute | solution.py:398
  86.4 6.5 %shard_map.73 = (f32[512,128]{1,0:T(8,128)S(1)}, f32[4,512,128]{2,1,0:T(8,128)S(1)}, f32[4752,128]{1,0:T(8,128)S(1)}, f32[528,128]{1,0:T(8,128)S(1)}, f32[528,128]{1,0:T(8,128)S(1)}, /*index=5*/f32[4752,128]{1,0:T(8,128)S(1)}) custom-call(f32[4752,128]{1,0:T(8,128)S(1)} %get-tuple-element.37.old_ref, ...), custom_call_target="tpu_custom_call", output_to_operand_aliasing={{5}: (0, {})} | custom-call | tf_op jit(solution)/shard_map/pallas_call | solution.py:442
  92.9 0.1 collective-permute-start.4
  93.0 5.2 %collective-permute-start.5 = (f32[528,128]{1,0:T(8,128)S(1)}, f32[528,128]{1,0:T(8,128)S(1)}, u32[]{:S(2)}, u32[]{:S(2)}) collective-permute-start(f32[528,128]{1,0:T(8,128)S(1)} %get-tuple-element.44), channel_id=1, source_target_pairs={{32,64},{64,32},{33,65},{65,33},{34,66},{66,34},{35,67},{67,35},{3... | collective-permute-start | bytes 811016 | tf_op jit(solution)/shard_map/ppermute | solution.py:398
  98.2 0.0 collective-permute-done.4.above_ref
  98.2 4.1 %collective-permute-done.5.below_ref = f32[528,128]{1,0:T(8,128)S(1)} collective-permute-done((f32[528,128]{1,0:T(8,128)S(1)}, f32[528,128]{1,0:T(8,128)S(1)}, u32[]{:S(2)}, u32[]{:S(2)}) %collective-permute-start.5) | collective-permute-done | bytes 270368 | tf_op jit(solution)/shard_map/ppermute | solution.py:398
  102.3 3.3 %shard_map.74 = (f32[32,72,128]{2,1,0:T(8,128)S(1)}, f32[4752,128]{1,0:T(8,128)S(1)}) custom-call(f32[4752,128]{1,0:T(8,128)S(1)} %get-tuple-element.42.old_ref, f32[528,128]{1,0:T(8,128)S(1)} %collective-permute-done.4.above_ref, f32[528,128]{1,0:T(8,128)S(1)} %collective-permute-done.5.below_ref, ...), custom_call_target="tpu_custom_call", output_to_operand_aliasing={{1}: (0, {})} | custom-call | tf_op jit(solution)/shard_map/pallas_call | solution.py:430
  105.6 16.2 %all_to_all.21.parts_ref = f32[32,72,128]{2,1,0:T(8,128)S(1)} all-to-all(f32[32,72,128]{2,1,0:T(8,128)S(1)} %get-tuple-element.47), channel_id=1, replica_groups=mesh['ty'=4,'tx'=8,'ta'=4] {'tx','ta'}, dimensions={0} | all-to-all | bytes 2359296 | tf_op jit(solution)/shard_map/all_to_all | solution.py:393
  121.8 3.2 %shard_map.75 = (f32[8,8,128]{2,1,0:T(8,128)S(1)}, f32[8,8,128]{2,1,0:T(8,128)S(1)}, f32[4752,128]{1,0:T(8,128)S(1)}, f32[528,128]{1,0:T(8,128)S(1)}, f32[528,128]{1,0:T(8,128)S(1)}) custom-call(f32[32,72,128]{2,1,0:T(8,128)S(1)} %all_to_all.21.parts_ref, f32[8,8,128]{2,1,0:T(8,128)S(1)} %get-tuple-element.41.activity_ref.old_ref, ...), custom_call_target="tpu_custom_call" | custom-call | tf_op jit(solution)/shard_map/pallas_call | solution.py:434
  124.9 0.1 collective-permute-start.6
  125.0 6.7 %collective-permute-start.7 = (f32[528,128]{1,0:T(8,128)S(1)}, f32[528,128]{1,0:T(8,128)S(1)}, u32[]{:S(2)}, u32[]{:S(2)}) collective-permute-start(f32[528,128]{1,0:T(8,128)S(1)} %get-tuple-element.50), channel_id=1, source_target_pairs={{32,64},{64,32},{33,65},{65,33},{34,66},{66,34},{35,67},{67,35},{3... | collective-permute-start | bytes 811016 | tf_op jit(solution)/shard_map/ppermute | solution.py:398
  131.8 0.0 collective-permute-done.6.above_ref
  131.8 4.1 %collective-permute-done.7.below_ref = f32[528,128]{1,0:T(8,128)S(1)} collective-permute-done((f32[528,128]{1,0:T(8,128)S(1)}, f32[528,128]{1,0:T(8,128)S(1)}, u32[]{:S(2)}, u32[]{:S(2)}) %collective-permute-start.7) | collective-permute-done | bytes 270368 | tf_op jit(solution)/shard_map/ppermute | solution.py:398
  135.9 4.7 %shard_map.76 = (f32[32,64,128]{2,1,0:T(8,128)}, f32[4752,128]{1,0:T(8,128)S(1)}) custom-call(f32[4752,128]{1,0:T(8,128)S(1)} %get-tuple-element.48.old_ref, f32[528,128]{1,0:T(8,128)S(1)} %collective-permute-done.6.above_ref, f32[528,128]{1,0:T(8,128)S(1)} %collective-permute-done.7.below_ref, ...), custom_call_target="tpu_custom_call", output_to_operand_aliasing={{1}: (0, {})} | custom-call | tf_op jit(solution)/shard_map/pallas_call | solution.py:450
  140.6 3.9 %all-to-all-start.3 = ((f32[32,64,128]{2,1,0:T(8,128)}), f32[32,64,128]{2,1,0:T(8,128)S(1)}, u32[]{:S(2)}, u32[]{:S(2)}) async-start(f32[32,64,128]{2,1,0:T(8,128)} %get-tuple-element.52), calls=%async_computation.3 | async-start | bytes 2097152 | tf_op jit(solution)/shard_map/all_to_all | solution.py:393
  144.6 0.1 reshape.70
  144.7 0.7 reshape.71
  145.4 10.3 %all-to-all-done.3.blocks_ref = f32[32,64,128]{2,1,0:T(8,128)S(1)} async-done(((f32[32,64,128]{2,1,0:T(8,128)}), f32[32,64,128]{2,1,0:T(8,128)S(1)}, u32[]{:S(2)}, u32[]{:S(2)}) %all-to-all-start.3) | async-done | bytes 1048608 | tf_op jit(solution)/shard_map/all_to_all | solution.py:393
  155.7 1.9 %shard_map.77 = f32[64,4096]{1,0:T(8,128)} custom-call(f32[32,64,128]{2,1,0:T(8,128)S(1)} %all-to-all-done.3.blocks_ref), custom_call_target="tpu_custom_call" | custom-call | tf_op jit(solution)/shard_map/pallas_call | solution.py:459
  (5 shorter events, 0.1 us)
Async XLA Ops:
  0.6 4.1 %copy-start = (f32[64,4096]{1,0:T(8,128)S(1)}, f32[64,4096]{1,0:T(8,128)}, u32[]{:S(2)}) copy-start(f32[64,4096]{1,0:T(8,128)} %prints_ref.1) | copy-start | bytes 3145732
  6.1 28.6 %all-to-all-start = ((bf16[32,168,128]{2,1,0:T(8,128)(2,1)}), bf16[32,168,128]{2,1,0:T(8,128)(2,1)S(1)}, u32[]{:S(2)}, u32[]{:S(2)}) async-start(bf16[32,168,128]{2,1,0:T(8,128)(2,1)} %shard_map.68), calls=%async_computation | async-start | bytes 2752512 | tf_op jit(solution)/shard_map/all_to_all | solution.py:393
  40.9 6.4 %collective-permute-start = (f32[528,128]{1,0:T(8,128)S(1)}, f32[528,128]{1,0:T(8,128)S(1)}, u32[]{:S(2)}, u32[]{:S(2)}) collective-permute-start(f32[528,128]{1,0:T(8,128)S(1)} %get-tuple-element.33), channel_id=1, source_target_pairs={{0,32},{32,0},{64,96},{96,64},{1,33},{33,1},{65,97},{97,65},{2,34}... | collective-permute-start | bytes 811016 | tf_op jit(solution)/shard_map/ppermute | solution.py:397
  43.0 9.3 %collective-permute-start.1 = (f32[528,128]{1,0:T(8,128)S(1)}, f32[528,128]{1,0:T(8,128)S(1)}, u32[]{:S(2)}, u32[]{:S(2)}) collective-permute-start(f32[528,128]{1,0:T(8,128)S(1)} %get-tuple-element.34), channel_id=1, source_target_pairs={{32,64},{64,32},{33,65},{65,33},{34,66},{66,34},{35,67},{67,35},{3... | collective-permute-start | bytes 811016 | tf_op jit(solution)/shard_map/ppermute | solution.py:398
  76.5 5.8 %collective-permute-start.2 = (f32[528,128]{1,0:T(8,128)S(1)}, f32[528,128]{1,0:T(8,128)S(1)}, u32[]{:S(2)}, u32[]{:S(2)}) collective-permute-start(f32[528,128]{1,0:T(8,128)S(1)} %get-tuple-element.38), channel_id=1, source_target_pairs={{0,32},{32,0},{64,96},{96,64},{1,33},{33,1},{65,97},{97,65},{2,34}... | collective-permute-start | bytes 811016 | tf_op jit(solution)/shard_map/ppermute | solution.py:397
  76.6 9.8 %collective-permute-start.3 = (f32[528,128]{1,0:T(8,128)S(1)}, f32[528,128]{1,0:T(8,128)S(1)}, u32[]{:S(2)}, u32[]{:S(2)}) collective-permute-start(f32[528,128]{1,0:T(8,128)S(1)} %get-tuple-element.39), channel_id=1, source_target_pairs={{32,64},{64,32},{33,65},{65,33},{34,66},{66,34},{35,67},{67,35},{3... | collective-permute-start | bytes 811016 | tf_op jit(solution)/shard_map/ppermute | solution.py:398
  92.9 5.3 %collective-permute-start.4 = (f32[528,128]{1,0:T(8,128)S(1)}, f32[528,128]{1,0:T(8,128)S(1)}, u32[]{:S(2)}, u32[]{:S(2)}) collective-permute-start(f32[528,128]{1,0:T(8,128)S(1)} %get-tuple-element.43), channel_id=1, source_target_pairs={{0,32},{32,0},{64,96},{96,64},{1,33},{33,1},{65,97},{97,65},{2,34}... | collective-permute-start | bytes 811016 | tf_op jit(solution)/shard_map/ppermute | solution.py:397
  93.0 9.3 %collective-permute-start.5 = (f32[528,128]{1,0:T(8,128)S(1)}, f32[528,128]{1,0:T(8,128)S(1)}, u32[]{:S(2)}, u32[]{:S(2)}) collective-permute-start(f32[528,128]{1,0:T(8,128)S(1)} %get-tuple-element.44), channel_id=1, source_target_pairs={{32,64},{64,32},{33,65},{65,33},{34,66},{66,34},{35,67},{67,35},{3... | collective-permute-start | bytes 811016 | tf_op jit(solution)/shard_map/ppermute | solution.py:398
  124.9 6.8 %collective-permute-start.6 = (f32[528,128]{1,0:T(8,128)S(1)}, f32[528,128]{1,0:T(8,128)S(1)}, u32[]{:S(2)}, u32[]{:S(2)}) collective-permute-start(f32[528,128]{1,0:T(8,128)S(1)} %get-tuple-element.49), channel_id=1, source_target_pairs={{0,32},{32,0},{64,96},{96,64},{1,33},{33,1},{65,97},{97,65},{2,34}... | collective-permute-start | bytes 811016 | tf_op jit(solution)/shard_map/ppermute | solution.py:397
  125.0 10.9 %collective-permute-start.7 = (f32[528,128]{1,0:T(8,128)S(1)}, f32[528,128]{1,0:T(8,128)S(1)}, u32[]{:S(2)}, u32[]{:S(2)}) collective-permute-start(f32[528,128]{1,0:T(8,128)S(1)} %get-tuple-element.50), channel_id=1, source_target_pairs={{32,64},{64,32},{33,65},{65,33},{34,66},{66,34},{35,67},{67,35},{3... | collective-permute-start | bytes 811016 | tf_op jit(solution)/shard_map/ppermute | solution.py:398
  140.6 15.1 %all-to-all-start.3 = ((f32[32,64,128]{2,1,0:T(8,128)}), f32[32,64,128]{2,1,0:T(8,128)S(1)}, u32[]{:S(2)}, u32[]{:S(2)}) async-start(f32[32,64,128]{2,1,0:T(8,128)} %get-tuple-element.52), calls=%async_computation.3 | async-start | bytes 2097152 | tf_op jit(solution)/shard_map/all_to_all | solution.py:393

commit v5 on v4

v5 whole, which is shorter than its diff:
```python
import functools

import jax
import jax.numpy as jnp
from jax import lax
from jax.experimental import pallas as pl
from jax.experimental.pallas import tpu as pltpu
from jax.sharding import PartitionSpec as P

ITERS = 2
RIDGE = 1.0
TX = 8
TA = 4
GROUP = TX * TA
OWNED = 64
COUNT = TX * OWNED
ROW = (TX * 8 + 2) * TA
CELL_ROWS = 16
FIELD = (CELL_ROWS + 2) * ROW
INNER = CELL_ROWS * ROW
VMEM = pl.BlockSpec(memory_space=pltpu.VMEM)
SMEM = pl.BlockSpec(memory_space=pltpu.SMEM)
ANY = pl.BlockSpec(memory_space=pl.ANY)
F32 = jnp.float32


def iotas():
    return (
        lax.broadcasted_iota(jnp.int32, (8, 128), 0),
        lax.broadcasted_iota(jnp.int32, (8, 128), 1),
    )


def pick_lanes(value, index):
    return jnp.take_along_axis(value, index, axis=1, mode="promise_in_bounds")


def pick_rows(value, index):
    return jnp.take_along_axis(value, index, axis=0, mode="promise_in_bounds")


def merge_lanes(first, second, shift, lane):
    if shift == 64:
        high = lane >= 64
        return jnp.where(high, second, first) + pltpu.roll(jnp.where(high, first, second), 64, 1)
    return jnp.where(
        (lane & shift) != 0,
        second + pltpu.roll(second, shift, 1),
        first + pltpu.roll(first, 128 - shift, 1),
    )


def merge_rows(first, second, shift, sub):
    return jnp.where(
        (sub & shift) != 0,
        second + pltpu.roll(second, shift, 0),
        first + pltpu.roll(first, 8 - shift, 0),
    )


def spread(value, m, sub, lane):
    wide = pick_lanes(value, (lane & 96) + m)
    turned = pltpu.roll(wide, 4, 0)
    low = sub < 4
    return jnp.where(low, wide, turned), jnp.where(low, turned, wide)


def pieces(value, count):
    out = []
    for _ in range(count):
        out.append(value.astype(jnp.bfloat16))
        value = value - out[-1].astype(F32)
    return out


def widen(prints, wide_ref):
    source = lax.broadcasted_iota(jnp.int32, (384, 512), 0) & 127
    target = lax.broadcasted_iota(jnp.int32, (384, 512), 1)
    copies = (source == (target >> 7) * 32 + (target & 31)).astype(jnp.bfloat16)
    parts = jnp.concatenate(pieces(prints, 3), axis=1)
    wide = jnp.dot(parts, copies, preferred_element_type=F32)
    for d in range(4):
        wide_ref[d] = wide[:, 128 * d : 128 * d + 128]


def print_pair(wide_ref, neuron, sub):
    rows = [jnp.broadcast_to(wide_ref[d, pl.ds(neuron, 1), :], (8, 128)) for d in range(4)]
    return jnp.where(sub < 4, rows[0], rows[1]), jnp.where(sub < 4, rows[2], rows[3])


def patch(v, k, places_ref):
    start = pl.multiple_of(places_ref[v, k], 4)
    return pl.ds(start, 8), pl.ds(start + ROW, 8)


def subtract_some(activity_ref, wide_ref, table_ref, field_ref, count, group_of):
    sub, lane = iotas()
    for first in range(2):
        tiles = [first + 2 * t for t in range(4)]
        values = [activity_ref[v] for v in tiles]

        def some(at, _):
            q = group_of(at)
            for b in range(4):
                pairs = [spread(value, q * 4 + b, sub, lane) for value in values]
                for half in range(2):
                    spots, changed = [], []
                    for v, pair in zip(tiles, pairs):
                        k = q * 8 + half * 4 + b
                        for at, side in zip(patch(v, k, table_ref), print_pair(wide_ref, v * OWNED + k, sub)):
                            spots.append(at)
                            changed.append(field_ref[at, :] - pair[half] * side)
                    for at, value in zip(spots, changed):
                        field_ref[at, :] = value
            return 0

        lax.fori_loop(0, count, some, 0)


def subtract_outer(activity_ref, wide_ref, table_ref, field_ref):
    start, stop = table_ref[16, 4], table_ref[16, 5]
    subtract_some(
        activity_ref,
        wide_ref,
        table_ref,
        field_ref,
        start + 8 - stop,
        lambda at: at + jnp.where(at >= start, stop - start, 0),
    )


def subtract_inner(activity_ref, wide_ref, table_ref, field_ref):
    start, stop = table_ref[16, 4], table_ref[16, 5]
    subtract_some(activity_ref, wide_ref, table_ref, field_ref, stop - start, lambda at: at + start)


def start_field(movie_ref, field_ref):
    field_ref[0:ROW, :] = jnp.zeros((ROW, 128), F32)
    field_ref[ROW + INNER :, :] = jnp.zeros((ROW, 128), F32)

    def one(r, _):
        field_ref[pl.ds((r + 1) * ROW, ROW), :] = movie_ref[pl.ds(r * ROW, ROW), :]
        return 0

    lax.fori_loop(0, CELL_ROWS, one, 0)


def add_edge(field_ref, edge_ref, low):
    rows = pl.ds(pl.multiple_of(jnp.where(low, INNER, 0), 8), 2 * ROW)
    field_ref[rows, :] += edge_ref[...]


def show_edges(field_ref, near_ref, near_out, far_out):
    even = near_ref[0] == 0
    top = field_ref[0 : 2 * ROW, :]
    bottom = field_ref[INNER:, :]
    near_out[...] = jnp.where(even, bottom, top)
    far_out[...] = jnp.where(even, top, bottom)


def pack_kernel(cells_ref, prints_ref, small_ref, layer_ref, out_ref, ranks_ref):
    lane = lax.broadcasted_iota(jnp.int32, (16, 128), 1)
    rows = pl.ds(pl.multiple_of(layer_ref[0] * 16, 16), 16)
    down = lax.broadcasted_iota(jnp.int32, (OWNED, OWNED), 0)
    right = lax.broadcasted_iota(jnp.int32, (OWNED, OWNED), 1)
    theirs = jnp.broadcast_to(small_ref[4:5, :], (OWNED, OWNED))
    ours = dot((down == right).astype(F32), theirs, 1)
    before = (theirs < ours) | ((theirs == ours) & (right < down))
    ranks = jnp.sum(before.astype(F32), axis=1, keepdims=True).astype(jnp.int32)
    order = (right == ranks).astype(F32)
    names = right[0:1].astype(F32)
    tail = [piece.astype(F32) for piece in pieces(small_ref[0:4, :], 3)]
    tail = dot(jnp.concatenate(tail + [small_ref[4:6, :], names, jnp.zeros((1, OWNED), F32)], axis=0), order, 0)
    tail = jnp.concatenate([tail[0:8], tail[8:16]], axis=1)
    tail = jnp.concatenate([tail, tail], axis=0).astype(jnp.bfloat16)
    places = dot(jnp.broadcast_to(names, (8, OWNED)), order, 1)
    ranks_ref[...] = jnp.concatenate([places, jnp.zeros((8, OWNED), F32)], axis=1).astype(jnp.int32)
    for a in range(8):
        blocks = swap_lanes(
            [prints_ref[rows, d * 1024 + a * 128 : d * 1024 + a * 128 + 128] for d in range(4)], lane
        )
        for b in range(4):
            shard = 4 * a + b
            dest = (shard % TX) * TA + shard // TX
            out_ref[dest, 0:128, :] = cells_ref[dest]
            for at, piece in enumerate(pieces(blocks[b], 2)):
                out_ref[dest, 128 + 16 * at : 144 + 16 * at, :] = piece
            out_ref[dest, 160:168, :] = tail[0:8]


def dot(left, right, axis):
    return lax.dot_general(left, right, (((1,), (axis,)), ((), ())), preferred_element_type=F32)


def own_lanes(sub, lane):
    m = lane & 31
    return (m >> 2) * 8 + (m & 3) + jnp.where(sub < 4, 0, 4)


def unpack_kernel(got_ref, near_ref, movie_ref, prints_ref, activity_ref, table_ref):
    sub, lane = iotas()
    skew = (lane - 16 * sub) & 127
    turn = ((lane >> 4) - sub) & 7
    back = (lane + 16 * sub) & 127
    for r in range(CELL_ROWS):
        movie_ref[r * ROW : r * ROW + 8, :] = jnp.zeros((8, 128), F32)
        movie_ref[(r + 1) * ROW - 8 : (r + 1) * ROW, :] = jnp.zeros((8, 128), F32)

    def block(g, _):
        base = (1 + 8 * (g // TA)) * TA + g % TA
        for t in range(8):
            both = got_ref[g, 16 * t : 16 * t + 16, :].astype(F32)
            for h in range(2):
                value = both[8 * h : 8 * h + 8]
                value = pick_lanes(pick_rows(pick_lanes(value, skew), turn), back)
                movie_ref[pl.ds(base + (2 * t + h) * ROW, 8, stride=TA), :] = value
        high, low = [got_ref[g, 128 + 16 * at : 144 + 16 * at, :].astype(F32) for at in range(2)]
        prints_ref[pl.ds(pl.multiple_of(g * 16, 16), 16), :] = high + low
        return 0

    lax.fori_loop(0, GROUP, block, 0, unroll=2)
    own = own_lanes(sub, lane)
    found = []
    for v in range(TX):
        tails = [got_ref[v * TA + z, 160:168, :].astype(F32) for z in range(TA)]
        turned = [pltpu.roll(tail, 64, 1) for tail in tails]
        values = [tail[0:4] + (tail[4:8] + other[0:4]) for tail, other in zip(tails, turned)]
        activity = jnp.zeros((8, 128), F32)
        for f in range(4):
            rows = jnp.concatenate([value[f : f + 1] for value in values] * 2, axis=0)
            activity = jnp.where((lane >> 5) == f, pick_lanes(rows, own), activity)
        activity_ref[v] = activity
        found.append(turned[0][4:7])
    row, col, name = [jnp.concatenate([one[at : at + 1] for one in found], axis=0) for at in range(3)]
    table_ref[0:8, :] = ((row + 1) * ROW + (col + (8 * sub.astype(F32) + 1)) * TA).astype(jnp.int32)
    table_ref[8:16, :] = name.astype(jnp.int32)
    real = lane < OWNED

    def most(mask):
        count = jnp.sum(jnp.where(real & mask, 1.0, 0.0), axis=1, keepdims=True)
        return jnp.max(count, axis=0, keepdims=True).astype(jnp.int32)

    top = (most(row < 0.5) + 7) >> 3
    bottom = (OWNED - most(row > 13.5)) >> 3
    even = near_ref[0] == 0
    limits = (
        jnp.where(even, top, 0),
        jnp.where(even, 8, bottom),
        jnp.where(even, 0, bottom),
        jnp.where(even, top, 8),
        top,
        jnp.maximum(top, bottom),
    )
    line = jnp.zeros((8, 128), jnp.int32)
    for at, limit in enumerate(limits):
        line = jnp.where(lane == at, limit, line)
    table_ref[16:24, :] = line


def first_kernel(
    movie_ref, raw_ref, activity_ref, near_ref, table_ref, prints_ref, wide_ref, field_ref, up_ref, down_ref
):
    def some(q, _):
        for v in range(TX):
            rows = [raw_ref[pl.ds(v * OWNED + table_ref[8 + v, q * 8 + n], 1), :] for n in range(8)]
            prints_ref[pl.ds(pl.multiple_of(v * OWNED + q * 8, 8), 8), :] = jnp.concatenate(rows, axis=0)
        return 0

    lax.fori_loop(0, 8, some, 0)
    widen(prints_ref[...], wide_ref)
    start_field(movie_ref, field_ref)
    subtract_outer(activity_ref, wide_ref, table_ref, field_ref)
    show_edges(field_ref, near_ref, up_ref, down_ref)


def fold_updates(field_ref, wide_ref, table_ref, part_ref, first, last):
    sub, lane = iotas()

    def leaf(v, q, b):
        folded = []
        for half in range(2):
            k = q * 8 + half * 4 + b
            upper, lower = print_pair(wide_ref, v * OWNED + k, sub)
            top, bottom = patch(v, k, table_ref)
            value = upper * field_ref[top, :] + lower * field_ref[bottom, :]
            folded.append(value + pltpu.roll(value, 4, 0))
        return jnp.where(sub < 4, folded[0], folded[1])

    def eight(q, _):
        for v in range(TX):
            low = merge_lanes(leaf(v, q, 0), leaf(v, q, 1), 1, lane)
            high = merge_lanes(leaf(v, q, 2), leaf(v, q, 3), 1, lane)
            part_ref[v * 8 + q] = merge_lanes(low, high, 2, lane)
        return 0

    lax.fori_loop(first, last, eight, 0)


def early_update_kernel(
    old_ref, near_ref_in, activity_ref, wide_ref, near_ref, table_ref, field_ref, part_ref
):
    subtract_inner(activity_ref, wide_ref, table_ref, field_ref)
    add_edge(field_ref, near_ref_in, near_ref[0] == 0)
    fold_updates(field_ref, wide_ref, table_ref, part_ref, table_ref[16, 0], table_ref[16, 1])


def update_kernel(
    old_ref, early_ref, far_ref, prints_ref, wide_ref, near_ref, table_ref, out_ref, field_ref, part_ref
):
    sub, lane = iotas()
    add_edge(field_ref, far_ref, near_ref[0] != 0)
    fold_updates(field_ref, wide_ref, table_ref, part_ref, table_ref[16, 2], table_ref[16, 3])
    for v in range(TX):
        parts = [part_ref[v * 8 + q] for q in range(8)]
        for shift in (4, 8, 16):
            parts = [merge_lanes(parts[n], parts[n + 1], shift, lane) for n in range(0, len(parts), 2)]
        for g in range(GROUP):
            out_ref[g, 8 * v : 8 * v + 8, :] = parts[0]
    squares = prints_ref[...] * prints_ref[...]
    energy = lax.dot_general(
        jnp.ones((8, 128), F32),
        squares,
        (((1,), (1,)), ((), ())),
        precision=lax.Precision.HIGHEST,
        preferred_element_type=F32,
    )
    rows = energy[:, 0:128]
    for q in range(1, 4):
        rows = jnp.where(sub == q, energy[:, 128 * q : 128 * q + 128], rows)
    for g in range(GROUP):
        out_ref[g, 64:72, :] = rows


def trace_kernel(
    parts_ref, old_ref, movie_ref, wide_ref, near_ref, places_ref, new_ref, weight_ref, field_ref, up_ref, down_ref
):
    sub, lane = iotas()
    start_field(movie_ref, field_ref)

    def total(start):
        rows = pl.ds(start, 8)
        value = parts_ref[0, rows, :]
        for g in range(1, GROUP):
            value = value + parts_ref[g, rows, :]
        return value

    energy = total(64)
    own = own_lanes(sub, lane)
    for v in range(TX):
        scale = pick_lanes(jnp.broadcast_to(energy[v // 2 : v // 2 + 1], (8, 128)), own + 64 * (v % 2))
        value = jnp.maximum(old_ref[v] + total(8 * v) / (scale + RIDGE), 0.0)
        new_ref[v] = value
        power = value * value
        power = power + pltpu.roll(power, 64, 1)
        power = power + pltpu.roll(power, 32, 1)
        power = merge_rows(power, power, 1, sub)
        power = merge_rows(power, power, 2, sub)
        weight_ref[v] = value / (power + RIDGE)
    subtract_outer(new_ref, wide_ref, places_ref, field_ref)
    show_edges(field_ref, near_ref, up_ref, down_ref)


def improve_prints(weight_ref, prints_ref, table_ref, field_ref, new_ref, first, last):
    sub, lane = iotas()

    def one(v, q):
        base = pl.multiple_of(v * OWNED + q * 8, 8)
        terms = []
        for b in range(4):
            pair = spread(weight_ref[v], q * 4 + b, sub, lane)
            for half in range(2):
                for at in patch(v, q * 8 + half * 4 + b, table_ref):
                    terms.append(pair[half] * field_ref[at, :])
        sides = []
        for n in range(4):
            low = merge_rows(terms[n], terms[4 + n], 1, sub)
            high = merge_rows(terms[8 + n], terms[12 + n], 1, sub)
            sides.append(merge_rows(low, high, 2, sub))
        step = merge_lanes(
            merge_lanes(sides[0], sides[1], 64, lane), merge_lanes(sides[2], sides[3], 64, lane), 32, lane
        )
        turned = pltpu.roll(step, 4, 0)
        dx = (lane & 32) != 0
        swapped = jnp.where(dx, pltpu.roll(turned, 32, 1), pltpu.roll(turned, 96, 1))
        step = jnp.where(dx == (sub >= 4), step, swapped)
        new_ref[pl.ds(base, 8), :] = jnp.maximum(prints_ref[pl.ds(base, 8), :] + step, 0.0)

    def eight(q, _):
        for v in range(TX):
            one(v, q)
        return 0

    lax.fori_loop(first, last, eight, 0)


def early_print_kernel(
    old_ref, near_ref_in, activity_ref, wide_ref, weight_ref, prints_ref, near_ref, table_ref, field_ref, new_ref
):
    subtract_inner(activity_ref, wide_ref, table_ref, field_ref)
    add_edge(field_ref, near_ref_in, near_ref[0] == 0)
    improve_prints(weight_ref, prints_ref, table_ref, field_ref, new_ref, table_ref[16, 0], table_ref[16, 1])


def finish_prints(far_ref, weight_ref, prints_ref, near_ref, table_ref, field_ref, new_ref):
    add_edge(field_ref, far_ref, near_ref[0] != 0)
    improve_prints(weight_ref, prints_ref, table_ref, field_ref, new_ref, table_ref[16, 2], table_ref[16, 3])


def print_kernel(
    old_ref, early_ref, far_ref, weight_ref, activity_ref, movie_ref, prints_ref, near_ref, table_ref,
    field_ref, new_ref, wide_ref, next_ref, up_ref, down_ref,
):
    finish_prints(far_ref, weight_ref, prints_ref, near_ref, table_ref, field_ref, new_ref)
    widen(new_ref[...], wide_ref)
    start_field(movie_ref, next_ref)
    subtract_outer(activity_ref, wide_ref, table_ref, next_ref)
    show_edges(next_ref, near_ref, up_ref, down_ref)


def last_kernel(
    old_ref, early_ref, far_ref, weight_ref, prints_ref, near_ref, table_ref,
    field_ref, new_ref, out_ref, raw_ref, sems,
):
    finish_prints(far_ref, weight_ref, prints_ref, near_ref, table_ref, field_ref, new_ref)
    copies = []

    def some(q, _):
        for v in range(TX):
            rows = new_ref[pl.ds(pl.multiple_of(v * OWNED + q * 8, 8), 8), :]
            for n in range(8):
                raw_ref[pl.ds(v * OWNED + table_ref[8 + v, q * 8 + n], 1), :] = rows[n : n + 1]
        return 0

    lax.fori_loop(0, 8, some, 0)
    for v in range(TX):
        for z in range(TA):
            rows = raw_ref.at[pl.ds(v * OWNED, OWNED)]
            copies.append(pltpu.make_async_copy(rows, out_ref.at[v * TA + z], sems.at[v * TA + z]))
            copies[-1].start()
    for copy in copies:
        copy.wait()


def traces_kernel(activity_ref, ranks_ref, spot_ref, out_ref):
    sub, lane = iotas()
    value = activity_ref[spot_ref[0]]
    ranks = ranks_ref[...]
    m = (ranks >> 3) * 4 + (ranks & 3)
    mine = sub == ((ranks >> 2) & 1) * 4 + spot_ref[1]
    for f in range(4):
        found = jnp.where(mine, pick_lanes(value, f * 32 + m), 0.0)
        out_ref[f : f + 1, :] = jnp.sum(found, axis=0, keepdims=True)[:, 0:OWNED]


def swap_lanes(parts, lane):
    for shift in (1, 2):
        high = (lane & (32 * shift)) != 0
        turned = []
        for b in range(4):
            other = pltpu.roll(parts[b ^ shift], 32 * shift if b & shift == 0 else 128 - 32 * shift, 1)
            turned.append(jnp.where(high, other, parts[b]) if b & shift == 0 else jnp.where(high, parts[b], other))
        parts = turned
    return parts


def finish_kernel(blocks_ref, out_ref, rows_ref, sems):
    lane = lax.broadcasted_iota(jnp.int32, (OWNED, 128), 1)
    copies = []
    for z in range(TA):
        for a in range(2):
            rows = swap_lanes([blocks_ref[(4 * a + b) * TA + z] for b in range(4)], lane)
            for d in range(4):
                at = len(copies)
                rows_ref[at] = rows[d]
                columns = pl.ds(d * 1024 + (z * 2 + a) * 128, 128)
                copies.append(pltpu.make_async_copy(rows_ref.at[at], out_ref.at[:, columns], sems.at[at]))
                copies[-1].start()
    for copy in copies:
        copy.wait()


def shape(*sizes, dtype=F32):
    return jax.ShapeDtypeStruct(sizes, dtype)


def call(kernel, outs, operands, scratch=(), smem=(), alias=(), left=(), work=1):
    return pl.pallas_call(
        kernel,
        out_shape=list(outs),
        in_specs=[SMEM if at in smem else VMEM for at in range(operands)],
        out_specs=[ANY if at in left else VMEM for at in range(len(outs))],
        scratch_shapes=list(scratch),
        input_output_aliases=dict(alias),
        compiler_params=pltpu.CompilerParams(vmem_limit_bytes=16 << 20),
        cost_estimate=pl.CostEstimate(flops=work << 20, bytes_accessed=work << 20, transcendentals=0),
    )


FIELD_SHAPE = shape(FIELD, 128)
EDGE_SHAPE = shape(2 * ROW, 128)
PRINT_SHAPE = shape(COUNT, 128)
TRACE_SHAPE = shape(TX, 8, 128)
WIDE_SHAPE = shape(4, COUNT, 128)
AXES = ("tx", "ta")


def exchange(blocks):
    return lax.all_to_all(blocks, AXES, 0, 0, tiled=True)


def halo(near, far):
    near = lax.ppermute(near, "ty", [(0, 1), (1, 0), (2, 3), (3, 2)])
    return near, lax.ppermute(far, "ty", [(1, 2), (2, 1)])


def shards(movie, footprints, traces, anchor_row, anchor_col):
    layer = lax.axis_index("ta")
    column = lax.axis_index("tx")
    frames = traces.shape[0]
    near = (lax.axis_index("ty") % 2).reshape(1)
    blocks = movie.reshape(frames, 4, CELL_ROWS, TX, 2, 128).transpose(3, 1, 2, 0, 4, 5)
    small = jnp.concatenate([traces, jnp.stack([anchor_row, anchor_col]).astype(F32)])
    sent, ranks = call(
        pack_kernel, (shape(GROUP, 168, 128, dtype=jnp.bfloat16), shape(8, 128, dtype=jnp.int32)), 4, smem=(3,)
    )(blocks.reshape(GROUP, 128, 128), footprints, small, layer.reshape(1))
    cells, raw, activity, table = call(
        unpack_kernel,
        (shape(INNER, 128), PRINT_SHAPE, TRACE_SHAPE, shape(24, 128, dtype=jnp.int32)),
        2,
        smem=(1,),
    )(exchange(sent), near)
    prints, wide, field, left, right = call(
        first_kernel, (PRINT_SHAPE, WIDE_SHAPE, FIELD_SHAPE, EDGE_SHAPE, EDGE_SHAPE), 5, smem=(3, 4)
    )(cells, raw, activity, near, table)
    for sweep in range(ITERS):
        left, right = halo(left, right)
        field, part = call(
            early_update_kernel, (FIELD_SHAPE, shape(64, 8, 128)), 6, smem=(4, 5), alias=((0, 0),), work=8
        )(field, left, activity, wide, near, table)
        sums, _, _ = call(
            update_kernel,
            (shape(GROUP, 72, 128), FIELD_SHAPE, shape(64, 8, 128)),
            7,
            smem=(5, 6),
            alias=((0, 1), (1, 2)),
        )(field, part, right, prints, wide, near, table)
        activity, weight, field, left, right = call(
            trace_kernel, (TRACE_SHAPE, TRACE_SHAPE, FIELD_SHAPE, EDGE_SHAPE, EDGE_SHAPE), 6, smem=(4, 5)
        )(exchange(sums), activity, cells, wide, near, table)
        left, right = halo(left, right)
        field, new = call(early_print_kernel, (FIELD_SHAPE, PRINT_SHAPE), 8, smem=(6, 7), alias=((0, 0),), work=8)(
            field, left, activity, wide, weight, prints, near, table
        )
        if sweep + 1 < ITERS:
            _, prints, wide, field, left, right = call(
                print_kernel,
                (FIELD_SHAPE, PRINT_SHAPE, WIDE_SHAPE, FIELD_SHAPE, EDGE_SHAPE, EDGE_SHAPE),
                9,
                smem=(7, 8),
                alias=((0, 0), (1, 1)),
            )(field, new, right, weight, activity, cells, prints, near, table)
        else:
            _, _, sent = call(
                last_kernel,
                (FIELD_SHAPE, PRINT_SHAPE, shape(GROUP, OWNED, 128)),
                7,
                (pltpu.VMEM((COUNT, 128), F32), pltpu.SemaphoreType.DMA((GROUP,))),
                smem=(5, 6),
                alias=((0, 0), (1, 1)),
                left=(2,),
            )(field, new, right, weight, prints, near, table)
    footprints_out = call(
        finish_kernel,
        (shape(OWNED, 4096),),
        1,
        (pltpu.VMEM((GROUP, OWNED, 128), F32), pltpu.SemaphoreType.DMA((GROUP,))),
        left=(0,),
    )(exchange(sent))[0]
    traces_out = call(traces_kernel, (shape(4, OWNED),), 3, smem=(2,))(activity, ranks, jnp.stack([column, layer]))[0]
    return footprints_out, traces_out


def solution(mesh):
    placed = (
        P("ta", None, "ty", "tx"),
        P(("ty", "tx"), None),
        P("ta", ("ty", "tx")),
        P(("ty", "tx")),
        P(("ty", "tx")),
    )
    return jax.shard_map(
        shards,
        mesh=mesh,
        in_specs=placed,
        out_specs=(P(("ty", "tx"), None), P("ta", ("ty", "tx"))),
        check_vma=False,
    )
```

time: 158 us -> 155 us (0.981)
  waiting for transfers between devices: 46.5 us -> 38.1 us
  Pallas kernels: 33.5 us -> 40.7 us
  starting transfers between devices: 38 us -> 31.3 us
  blocking collectives: 33.9 us -> 39.5 us
  local copies, waits for them, and re-layouts: 4.14 us -> 2.4 us
    ppermute x4, waiting for transfers between devices: 17.4 us -> 6.86 us  [halo(): return (near, lax.ppermute(far, 'ty', [(1, 2), (2, 1)]))]
    pallas_call x9 -> x14, Pallas kernels: 31.6 us -> 38.8 us  [the longest x2 8.32 us: shards(): call(early_print_kernel, (FIELD_SHAPE, PRINT_SHAPE), 8, smem=(6, 7), alia...]
    ppermute x4, starting transfers between devices: 21.8 us -> 15.2 us  [halo(): return (near, lax.ppermute(far, 'ty', [(1, 2), (2, 1)]))]
    all_to_all x2, blocking collectives: 33.9 us -> 39.5 us  [exchange(): return lax.all_to_all(blocks, AXES, 0, 0, tiled=True)]
    all_to_all x2, waiting for transfers between devices: 29.1 us -> 31.3 us  [exchange(): return lax.all_to_all(blocks, AXES, 0, 0, tiled=True)]
    reshape x4 -> x0, local copies, waits for them, and re-layouts: 1.76 us -> none  [the longest x2 0.98 us: shards(): own = traces.reshape(frames, 8, 2, 4).transpose(2, 0, 1, 3).reshape(2, 128)]
  transfers between devices with their start and end apart: 10 -> 10, of which waited for: 6 -> 6; matrix products, arithmetic and copies ran while one was open for 1% -> 0% of each run, Pallas kernels for 0% -> 10%
where the time goes in v5:
time: 155 us; the launch traced here: 154 us
  Pallas kernels  40.7 us (26%)
  blocking collectives  39.5 us (25%)
  waiting for transfers between devices  38.1 us (25%)
  starting transfers between devices  31.3 us (20%)
  local copies, waits for them, and re-layouts  2.4 us (2%)
    all_to_all x2, blocking collectives, exchange(): return lax.all_to_all(blocks, AXES, 0, 0, tiled=True)  39.5 us
    all_to_all x2, waiting for transfers between devices, exchange(): return lax.all_to_all(blocks, AXES, 0, 0, tiled=True)  31.3 us
    ppermute x4, starting transfers between devices, halo(): return (near, lax.ppermute(far, 'ty', [(1, 2), (2, 1)]))  15.2 us
    all_to_all x2, starting transfers between devices, exchange(): return lax.all_to_all(blocks, AXES, 0, 0, tiled=True)  13.7 us
    pallas_call x2, Pallas kernels, shards(): call(early_print_kernel, (FIELD_SHAPE, PRINT_SHAPE), 8, smem=(6, 7), alia...  8.32 us
    ppermute x4, waiting for transfers between devices, halo(): return (near, lax.ppermute(far, 'ty', [(1, 2), (2, 1)]))  6.86 us
    pallas_call x2, Pallas kernels, shards(): call(early_update_kernel, (FIELD_SHAPE, shape(64, 8, 128)), 6, smem=(4, 5...  6.68 us
    pallas_call x2, Pallas kernels, shards(): call(trace_kernel, (TRACE_SHAPE, TRACE_SHAPE, FIELD_SHAPE, EDGE_SHAPE, ED...  4.61 us
  transfers between devices with their start and end apart: 10, of which 6 were waited for; matrix products, arithmetic and copies ran while one was open for 0% of the time, Pallas kernels for 10%

profile of v5, /device:TPU:1, one launch (start us, length us, event | category | flops | bytes accessed | tf_op | source)
XLA Modules:
  0.0 154.4 jit_solution(16409480330353968617)
XLA Ops:
  0.6 0.0 copy-start
  0.6 2.4 %copy.19 = bf16[4,4,16,8,2,128]{5,4,0,2,1,3:T(2,128)(2,1)S(1)} copy(bf16[4,4,16,8,2,128]{5,4,3,2,1,0:T(2,128)(2,1)} %bitcast.10) | data formatting | bytes 2097152 | tf_op jit(solution)/shard_map/reshape | solution.py:521
  3.0 0.7 add_convert_fusion
  3.7 0.7 pad_maximum_fusion.small_ref
  4.4 0.0 copy-done
  4.4 1.8 %shard_map.68 = (bf16[32,168,128]{2,1,0:T(8,128)(2,1)}, s32[8,128]{1,0:T(8,128)S(1)}) custom-call(bf16[32,128,128]{2,1,0:T(8,128)(2,1)S(1)} %bitcast.9, f32[64,4096]{1,0:T(8,128)S(1)} %copy-done, f32[6,64]{1,0:T(8,128)S(1)} %pad_maximum_fusion.small_ref, s32[1]{0:T(128)} %bitcast.5.layer_ref), custom_call_target="tpu_custom_call" | custom-call | flops 1048576 | bytes 1048576 | tf_op jit(solution)/shard_map/pallas_call | solution.py:523
  6.2 9.8 %all-to-all-start = ((bf16[32,168,128]{2,1,0:T(8,128)(2,1)}), bf16[32,168,128]{2,1,0:T(8,128)(2,1)S(1)}, u32[]{:S(2)}, u32[]{:S(2)}) async-start(bf16[32,168,128]{2,1,0:T(8,128)(2,1)} %get-tuple-element.39), calls=%async_computation | async-start | bytes 2752512 | tf_op jit(solution)/shard_map/all_to_all | solution.py:508
  16.0 18.8 %all-to-all-done.got_ref = bf16[32,168,128]{2,1,0:T(8,128)(2,1)S(1)} async-done(((bf16[32,168,128]{2,1,0:T(8,128)(2,1)}), bf16[32,168,128]{2,1,0:T(8,128)(2,1)S(1)}, u32[]{:S(2)}, u32[]{:S(2)}) %all-to-all-start) | async-done | bytes 1376288 | tf_op jit(solution)/shard_map/all_to_all | solution.py:508
  34.8 2.9 %shard_map.69 = (f32[4224,128]{1,0:T(8,128)S(1)}, f32[512,128]{1,0:T(8,128)S(1)}, f32[8,8,128]{2,1,0:T(8,128)S(1)}, s32[24,128]{1,0:T(8,128)S(1)}) custom-call(bf16[32,168,128]{2,1,0:T(8,128)(2,1)S(1)} %all-to-all-done.got_ref, s32[1]{0:T(128)} %bitcast.6.near_ref), custom_call_target="tpu_custom_call" | custom-call | flops 1048576 | bytes 1048576 | tf_op jit(solution)/shard_map/pallas_call | solution.py:526
  37.7 3.3 %shard_map.70 = (f32[512,128]{1,0:T(8,128)S(1)}, f32[4,512,128]{2,1,0:T(8,128)S(1)}, f32[4752,128]{1,0:T(8,128)S(1)}, f32[528,128]{1,0:T(8,128)S(1)}, f32[528,128]{1,0:T(8,128)S(1)}) custom-call(f32[4224,128]{1,0:T(8,128)S(1)} %get-tuple-element.40.movie_ref, f32[512,128]{1,0:T(8,128)S(1)} %get-tuple-element.41.raw_ref, ...), custom_call_target="tpu_custom_call" | custom-call | flops 1048576 | bytes 1048576 | tf_op jit(solution)/shard_map/pallas_call | solution.py:532
  41.0 2.1 %collective-permute-start = (f32[528,128]{1,0:T(8,128)S(1)}, f32[528,128]{1,0:T(8,128)S(1)}, u32[]{:S(2)}, u32[]{:S(2)}) collective-permute-start(f32[528,128]{1,0:T(8,128)S(1)} %get-tuple-element.45), channel_id=1, source_target_pairs={{0,32},{32,0},{64,96},{96,64},{1,33},{33,1},{65,97},{97,65},{2,34}... | collective-permute-start | bytes 811016 | tf_op jit(solution)/shard_map/ppermute | solution.py:512
  43.1 4.2 %collective-permute-start.1 = (f32[528,128]{1,0:T(8,128)S(1)}, f32[528,128]{1,0:T(8,128)S(1)}, u32[]{:S(2)}, u32[]{:S(2)}) collective-permute-start(f32[528,128]{1,0:T(8,128)S(1)} %get-tuple-element.49), channel_id=1, source_target_pairs={{32,64},{64,32},{33,65},{65,33},{34,66},{66,34},{35,67},{67,35},{3... | collective-permute-start | bytes 811016 | tf_op jit(solution)/shard_map/ppermute | solution.py:513
  47.4 0.0 collective-permute-done.near_ref_in
  47.4 3.3 %shard_map.71 = (f32[4752,128]{1,0:T(8,128)S(1)}, f32[64,8,128]{2,1,0:T(8,128)S(1)}) custom-call(f32[4752,128]{1,0:T(8,128)S(1)} %get-tuple-element.44.old_ref, f32[528,128]{1,0:T(8,128)S(1)} %collective-permute-done.near_ref_in, f32[8,8,128]{2,1,0:T(8,128)S(1)} %get-tuple-element.42.activity_ref.old_ref, ...), custom_call_target="tpu_custom_call", output_to_operand_aliasing={{0}: (0, {})} | custom-call | flops 8388608 | bytes 8388608 | tf_op jit(solution)/shard_map/pallas_call | solution.py:537
  50.7 1.7 %collective-permute-done.1.far_ref = f32[528,128]{1,0:T(8,128)S(1)} collective-permute-done((f32[528,128]{1,0:T(8,128)S(1)}, f32[528,128]{1,0:T(8,128)S(1)}, u32[]{:S(2)}, u32[]{:S(2)}) %collective-permute-start.1) | collective-permute-done | bytes 270368 | tf_op jit(solution)/shard_map/ppermute | solution.py:513
  52.4 1.6 %shard_map.72 = (f32[32,72,128]{2,1,0:T(8,128)S(1)}, f32[4752,128]{1,0:T(8,128)S(1)}, f32[64,8,128]{2,1,0:T(8,128)S(1)}) custom-call(f32[4752,128]{1,0:T(8,128)S(1)} %get-tuple-element.47.old_ref, f32[64,8,128]{2,1,0:T(8,128)S(1)} %get-tuple-element.48.early_ref, ...), custom_call_target="tpu_custom_call", output_to_operand_aliasing={{1}: (0, {}), {2}: (1, {})} | custom-call | flops 1048576 | bytes 1048576 | tf_op jit(solution)/shard_map/pallas_call | solution.py:540
  54.0 20.4 %all_to_all.20.parts_ref = f32[32,72,128]{2,1,0:T(8,128)S(1)} all-to-all(f32[32,72,128]{2,1,0:T(8,128)S(1)} %get-tuple-element.51), channel_id=1, replica_groups=mesh['ty'=4,'tx'=8,'ta'=4] {'tx','ta'}, dimensions={0} | all-to-all | bytes 2359296 | tf_op jit(solution)/shard_map/all_to_all | solution.py:508
  74.4 2.3 %shard_map.73 = (f32[8,8,128]{2,1,0:T(8,128)S(1)}, f32[8,8,128]{2,1,0:T(8,128)S(1)}, f32[4752,128]{1,0:T(8,128)S(1)}, f32[528,128]{1,0:T(8,128)S(1)}, f32[528,128]{1,0:T(8,128)S(1)}) custom-call(f32[32,72,128]{2,1,0:T(8,128)S(1)} %all_to_all.20.parts_ref, f32[8,8,128]{2,1,0:T(8,128)S(1)} %get-tuple-element.42.activity_ref.old_ref, ...), custom_call_target="tpu_custom_call" | custom-call | flops 1048576 | bytes 1048576 | tf_op jit(solution)/shard_map/pallas_call | solution.py:547
  76.7 0.1 collective-permute-start.2
  76.8 3.8 %collective-permute-start.3 = (f32[528,128]{1,0:T(8,128)S(1)}, f32[528,128]{1,0:T(8,128)S(1)}, u32[]{:S(2)}, u32[]{:S(2)}) collective-permute-start(f32[528,128]{1,0:T(8,128)S(1)} %get-tuple-element.58), channel_id=1, source_target_pairs={{32,64},{64,32},{33,65},{65,33},{34,66},{66,34},{35,67},{67,35},{3... | collective-permute-start | bytes 811016 | tf_op jit(solution)/shard_map/ppermute | solution.py:513
  80.7 0.0 collective-permute-done.2.near_ref_in
  80.7 4.2 %shard_map.74 = (f32[4752,128]{1,0:T(8,128)S(1)}, f32[512,128]{1,0:T(8,128)S(1)}) custom-call(f32[4752,128]{1,0:T(8,128)S(1)} %get-tuple-element.52.old_ref, f32[528,128]{1,0:T(8,128)S(1)} %collective-permute-done.2.near_ref_in, f32[8,8,128]{2,1,0:T(8,128)S(1)} %get-tuple-element.54.activity_ref.old_ref, ...), custom_call_target="tpu_custom_call", output_to_operand_aliasing={{0}: (0, {})} | custom-call | flops 8388608 | bytes 8388608 | tf_op jit(solution)/shard_map/pallas_call | solution.py:551
  84.8 1.3 collective-permute-done.3.far_ref
  86.1 3.3 %shard_map.75 = (f32[4752,128]{1,0:T(8,128)S(1)}, f32[512,128]{1,0:T(8,128)S(1)}, f32[4,512,128]{2,1,0:T(8,128)S(1)}, f32[4752,128]{1,0:T(8,128)S(1)}, f32[528,128]{1,0:T(8,128)S(1)}, /*index=5*/f32[528,128]{1,0:T(8,128)S(1)}) custom-call(f32[4752,128]{1,0:T(8,128)S(1)} %get-tuple-element.56.old_ref, ...), custom_call_target="tpu_custom_call", output_to_operand_aliasing={{0}: (0, {}), {1}: (1, {})} | custom-call | flops 1048576 | bytes 1048576 | tf_op jit(solution)/shard_map/pallas_call | solution.py:555
  89.4 0.1 collective-permute-start.4
  89.5 3.8 %collective-permute-start.5 = (f32[528,128]{1,0:T(8,128)S(1)}, f32[528,128]{1,0:T(8,128)S(1)}, u32[]{:S(2)}, u32[]{:S(2)}) collective-permute-start(f32[528,128]{1,0:T(8,128)S(1)} %get-tuple-element.64), channel_id=1, source_target_pairs={{32,64},{64,32},{33,65},{65,33},{34,66},{66,34},{35,67},{67,35},{3... | collective-permute-start | bytes 811016 | tf_op jit(solution)/shard_map/ppermute | solution.py:513
  93.3 0.0 collective-permute-done.4.near_ref_in
  93.4 3.3 %shard_map.76 = (f32[4752,128]{1,0:T(8,128)S(1)}, f32[64,8,128]{2,1,0:T(8,128)S(1)}) custom-call(f32[4752,128]{1,0:T(8,128)S(1)} %get-tuple-element.59.old_ref, f32[528,128]{1,0:T(8,128)S(1)} %collective-permute-done.4.near_ref_in, f32[8,8,128]{2,1,0:T(8,128)S(1)} %get-tuple-element.54.activity_ref.old_ref, ...), custom_call_target="tpu_custom_call", output_to_operand_aliasing={{0}: (0, {})} | custom-call | flops 8388608 | bytes 8388608 | tf_op jit(solution)/shard_map/pallas_call | solution.py:537
  96.7 2.1 %collective-permute-done.5.far_ref = f32[528,128]{1,0:T(8,128)S(1)} collective-permute-done((f32[528,128]{1,0:T(8,128)S(1)}, f32[528,128]{1,0:T(8,128)S(1)}, u32[]{:S(2)}, u32[]{:S(2)}) %collective-permute-start.5) | collective-permute-done | bytes 270368 | tf_op jit(solution)/shard_map/ppermute | solution.py:513
  98.8 1.6 %shard_map.77 = (f32[32,72,128]{2,1,0:T(8,128)S(1)}, f32[4752,128]{1,0:T(8,128)S(1)}, f32[64,8,128]{2,1,0:T(8,128)S(1)}) custom-call(f32[4752,128]{1,0:T(8,128)S(1)} %get-tuple-element.62.old_ref, f32[64,8,128]{2,1,0:T(8,128)S(1)} %get-tuple-element.63.early_ref, ...), custom_call_target="tpu_custom_call", output_to_operand_aliasing={{1}: (0, {}), {2}: (1, {})} | custom-call | flops 1048576 | bytes 1048576 | tf_op jit(solution)/shard_map/pallas_call | solution.py:540
  100.4 19.1 %all_to_all.21.parts_ref = f32[32,72,128]{2,1,0:T(8,128)S(1)} all-to-all(f32[32,72,128]{2,1,0:T(8,128)S(1)} %get-tuple-element.66), channel_id=1, replica_groups=mesh['ty'=4,'tx'=8,'ta'=4] {'tx','ta'}, dimensions={0} | all-to-all | bytes 2359296 | tf_op jit(solution)/shard_map/all_to_all | solution.py:508
  119.5 2.3 %shard_map.78 = (f32[8,8,128]{2,1,0:T(8,128)S(1)}, f32[8,8,128]{2,1,0:T(8,128)S(1)}, f32[4752,128]{1,0:T(8,128)S(1)}, f32[528,128]{1,0:T(8,128)S(1)}, f32[528,128]{1,0:T(8,128)S(1)}) custom-call(f32[32,72,128]{2,1,0:T(8,128)S(1)} %all_to_all.21.parts_ref, f32[8,8,128]{2,1,0:T(8,128)S(1)} %get-tuple-element.54.activity_ref.old_ref, ...), custom_call_target="tpu_custom_call" | custom-call | flops 1048576 | bytes 1048576 | tf_op jit(solution)/shard_map/pallas_call | solution.py:547
  121.8 0.1 collective-permute-start.6
  121.9 3.3 %collective-permute-start.7 = (f32[528,128]{1,0:T(8,128)S(1)}, f32[528,128]{1,0:T(8,128)S(1)}, u32[]{:S(2)}, u32[]{:S(2)}) collective-permute-start(f32[528,128]{1,0:T(8,128)S(1)} %get-tuple-element.73), channel_id=1, source_target_pairs={{32,64},{64,32},{33,65},{65,33},{34,66},{66,34},{35,67},{67,35},{3... | collective-permute-start | bytes 811016 | tf_op jit(solution)/shard_map/ppermute | solution.py:513
  125.2 0.0 collective-permute-done.6.near_ref_in
  125.2 4.2 %shard_map.79 = (f32[4752,128]{1,0:T(8,128)S(1)}, f32[512,128]{1,0:T(8,128)S(1)}) custom-call(f32[4752,128]{1,0:T(8,128)S(1)} %get-tuple-element.67.old_ref, f32[528,128]{1,0:T(8,128)S(1)} %collective-permute-done.6.near_ref_in, f32[8,8,128]{2,1,0:T(8,128)S(1)} %get-tuple-element.69.activity_ref, ...), custom_call_target="tpu_custom_call", output_to_operand_aliasing={{0}: (0, {})} | custom-call | flops 8388608 | bytes 8388608 | tf_op jit(solution)/shard_map/pallas_call | solution.py:551
  129.4 1.8 %collective-permute-done.7.far_ref = f32[528,128]{1,0:T(8,128)S(1)} collective-permute-done((f32[528,128]{1,0:T(8,128)S(1)}, f32[528,128]{1,0:T(8,128)S(1)}, u32[]{:S(2)}, u32[]{:S(2)}) %collective-permute-start.7) | collective-permute-done | bytes 270368 | tf_op jit(solution)/shard_map/ppermute | solution.py:513
  131.2 3.6 %shard_map.80 = (f32[4752,128]{1,0:T(8,128)S(1)}, f32[512,128]{1,0:T(8,128)S(1)}, f32[32,64,128]{2,1,0:T(8,128)}) custom-call(f32[4752,128]{1,0:T(8,128)S(1)} %get-tuple-element.71.old_ref, f32[512,128]{1,0:T(8,128)S(1)} %get-tuple-element.72.early_ref, f32[528,128]{1,0:T(8,128)S(1)} %collective-permute-done.7.far_ref, ...), custom_call_target="tpu_custom_call", output_to_operand_aliasing={{0}: (0, {}), {1}: (1, {})} | custom-call | flops 1048576 | bytes 1048576 | tf_op jit(solution)/shard_map/pallas_call | solution.py:563
  134.8 3.9 %all-to-all-start.3 = ((f32[32,64,128]{2,1,0:T(8,128)}), f32[32,64,128]{2,1,0:T(8,128)S(1)}, u32[]{:S(2)}, u32[]{:S(2)}) async-start(f32[32,64,128]{2,1,0:T(8,128)} %get-tuple-element.74), calls=%async_computation.3 | async-start | bytes 2097152 | tf_op jit(solution)/shard_map/all_to_all | solution.py:508
  138.8 0.1 pad_add_fusion.spot_ref
  138.8 1.2 shard_map.82
  140.0 12.5 %all-to-all-done.3.blocks_ref = f32[32,64,128]{2,1,0:T(8,128)S(1)} async-done(((f32[32,64,128]{2,1,0:T(8,128)}), f32[32,64,128]{2,1,0:T(8,128)S(1)}, u32[]{:S(2)}, u32[]{:S(2)}) %all-to-all-start.3) | async-done | bytes 1048608 | tf_op jit(solution)/shard_map/all_to_all | solution.py:508
  152.5 1.9 %shard_map.81 = f32[64,4096]{1,0:T(8,128)} custom-call(f32[32,64,128]{2,1,0:T(8,128)S(1)} %all-to-all-done.3.blocks_ref), custom_call_target="tpu_custom_call" | custom-call | flops 1048576 | bytes 1048576 | tf_op jit(solution)/shard_map/pallas_call | solution.py:572
Async XLA Ops:
  0.6 3.8 %copy-start = (f32[64,4096]{1,0:T(8,128)S(1)}, f32[64,4096]{1,0:T(8,128)}, u32[]{:S(2)}) copy-start(f32[64,4096]{1,0:T(8,128)} %prints_ref.1) | copy-start | bytes 3145732
  6.2 28.6 %all-to-all-start = ((bf16[32,168,128]{2,1,0:T(8,128)(2,1)}), bf16[32,168,128]{2,1,0:T(8,128)(2,1)S(1)}, u32[]{:S(2)}, u32[]{:S(2)}) async-start(bf16[32,168,128]{2,1,0:T(8,128)(2,1)} %get-tuple-element.39), calls=%async_computation | async-start | bytes 2752512 | tf_op jit(solution)/shard_map/all_to_all | solution.py:508
  41.0 6.4 %collective-permute-start = (f32[528,128]{1,0:T(8,128)S(1)}, f32[528,128]{1,0:T(8,128)S(1)}, u32[]{:S(2)}, u32[]{:S(2)}) collective-permute-start(f32[528,128]{1,0:T(8,128)S(1)} %get-tuple-element.45), channel_id=1, source_target_pairs={{0,32},{32,0},{64,96},{96,64},{1,33},{33,1},{65,97},{97,65},{2,34}... | collective-permute-start | bytes 811016 | tf_op jit(solution)/shard_map/ppermute | solution.py:512
  43.1 9.3 %collective-permute-start.1 = (f32[528,128]{1,0:T(8,128)S(1)}, f32[528,128]{1,0:T(8,128)S(1)}, u32[]{:S(2)}, u32[]{:S(2)}) collective-permute-start(f32[528,128]{1,0:T(8,128)S(1)} %get-tuple-element.49), channel_id=1, source_target_pairs={{32,64},{64,32},{33,65},{65,33},{34,66},{66,34},{35,67},{67,35},{3... | collective-permute-start | bytes 811016 | tf_op jit(solution)/shard_map/ppermute | solution.py:513
  76.7 3.9 %collective-permute-start.2 = (f32[528,128]{1,0:T(8,128)S(1)}, f32[528,128]{1,0:T(8,128)S(1)}, u32[]{:S(2)}, u32[]{:S(2)}) collective-permute-start(f32[528,128]{1,0:T(8,128)S(1)} %get-tuple-element.53), channel_id=1, source_target_pairs={{0,32},{32,0},{64,96},{96,64},{1,33},{33,1},{65,97},{97,65},{2,34}... | collective-permute-start | bytes 811016 | tf_op jit(solution)/shard_map/ppermute | solution.py:512
  76.8 9.3 %collective-permute-start.3 = (f32[528,128]{1,0:T(8,128)S(1)}, f32[528,128]{1,0:T(8,128)S(1)}, u32[]{:S(2)}, u32[]{:S(2)}) collective-permute-start(f32[528,128]{1,0:T(8,128)S(1)} %get-tuple-element.58), channel_id=1, source_target_pairs={{32,64},{64,32},{33,65},{65,33},{34,66},{66,34},{35,67},{67,35},{3... | collective-permute-start | bytes 811016 | tf_op jit(solution)/shard_map/ppermute | solution.py:513
  89.4 3.9 %collective-permute-start.4 = (f32[528,128]{1,0:T(8,128)S(1)}, f32[528,128]{1,0:T(8,128)S(1)}, u32[]{:S(2)}, u32[]{:S(2)}) collective-permute-start(f32[528,128]{1,0:T(8,128)S(1)} %get-tuple-element.60), channel_id=1, source_target_pairs={{0,32},{32,0},{64,96},{96,64},{1,33},{33,1},{65,97},{97,65},{2,34}... | collective-permute-start | bytes 811016 | tf_op jit(solution)/shard_map/ppermute | solution.py:512
  89.5 9.3 %collective-permute-start.5 = (f32[528,128]{1,0:T(8,128)S(1)}, f32[528,128]{1,0:T(8,128)S(1)}, u32[]{:S(2)}, u32[]{:S(2)}) collective-permute-start(f32[528,128]{1,0:T(8,128)S(1)} %get-tuple-element.64), channel_id=1, source_target_pairs={{32,64},{64,32},{33,65},{65,33},{34,66},{66,34},{35,67},{67,35},{3... | collective-permute-start | bytes 811016 | tf_op jit(solution)/shard_map/ppermute | solution.py:513
  121.8 3.4 %collective-permute-start.6 = (f32[528,128]{1,0:T(8,128)S(1)}, f32[528,128]{1,0:T(8,128)S(1)}, u32[]{:S(2)}, u32[]{:S(2)}) collective-permute-start(f32[528,128]{1,0:T(8,128)S(1)} %get-tuple-element.68), channel_id=1, source_target_pairs={{0,32},{32,0},{64,96},{96,64},{1,33},{33,1},{65,97},{97,65},{2,34}... | collective-permute-start | bytes 811016 | tf_op jit(solution)/shard_map/ppermute | solution.py:512
  121.9 9.3 %collective-permute-start.7 = (f32[528,128]{1,0:T(8,128)S(1)}, f32[528,128]{1,0:T(8,128)S(1)}, u32[]{:S(2)}, u32[]{:S(2)}) collective-permute-start(f32[528,128]{1,0:T(8,128)S(1)} %get-tuple-element.73), channel_id=1, source_target_pairs={{32,64},{64,32},{33,65},{65,33},{34,66},{66,34},{35,67},{67,35},{3... | collective-permute-start | bytes 811016 | tf_op jit(solution)/shard_map/ppermute | solution.py:513
  134.8 17.7 %all-to-all-start.3 = ((f32[32,64,128]{2,1,0:T(8,128)}), f32[32,64,128]{2,1,0:T(8,128)S(1)}, u32[]{:S(2)}, u32[]{:S(2)}) async-start(f32[32,64,128]{2,1,0:T(8,128)} %get-tuple-element.74), calls=%async_computation.3 | async-start | bytes 2097152 | tf_op jit(solution)/shard_map/all_to_all | solution.py:508

commit v6 on v5

--- a/solution.py
+++ b/solution.py
@@ -315,7 +315,8 @@
         for shift in (4, 8, 16):
             parts = [merge_lanes(parts[n], parts[n + 1], shift, lane) for n in range(0, len(parts), 2)]
         for g in range(GROUP):
-            out_ref[g, 8 * v : 8 * v + 8, :] = parts[0]
+            out_ref[g, 2 * v] = parts[0][0:4]
+            out_ref[g, 2 * v + 1] = parts[0][4:8]
     squares = prints_ref[...] * prints_ref[...]
     energy = lax.dot_general(
         jnp.ones((8, 128), F32),
@@ -328,7 +329,7 @@
     for q in range(1, 4):
         rows = jnp.where(sub == q, energy[:, 128 * q : 128 * q + 128], rows)
     for g in range(GROUP):
-        out_ref[g, 64:72, :] = rows
+        out_ref[g, 16] = rows[0:4]
 
 
 def trace_kernel(
@@ -337,18 +338,17 @@
     sub, lane = iotas()
     start_field(movie_ref, field_ref)
 
-    def total(start):
-        rows = pl.ds(start, 8)
-        value = parts_ref[0, rows, :]
+    def total(at):
+        value = parts_ref[0, at]
         for g in range(1, GROUP):
-            value = value + parts_ref[g, rows, :]
+            value = value + parts_ref[g, at]
         return value
 
-    energy = total(64)
+    energy = total(16)
     own = own_lanes(sub, lane)
     for v in range(TX):
         scale = pick_lanes(jnp.broadcast_to(energy[v // 2 : v // 2 + 1], (8, 128)), own + 64 * (v % 2))
-        value = jnp.maximum(old_ref[v] + total(8 * v) / (scale + RIDGE), 0.0)
+        value = jnp.maximum(old_ref[v] + jnp.concatenate([total(2 * v), total(2 * v + 1)], axis=0) / (scale + RIDGE), 0.0)
         new_ref[v] = value
         power = value * value
         power = power + pltpu.roll(power, 64, 1)
@@ -539,7 +539,7 @@
         )(field, left, activity, wide, near, table)
         sums, _, _ = call(
             update_kernel,
-            (shape(GROUP, 72, 128), FIELD_SHAPE, shape(64, 8, 128)),
+            (shape(GROUP, 17, 4, 128), FIELD_SHAPE, shape(64, 8, 128)),
             7,
             smem=(5, 6),
             alias=((0, 1), (1, 2)),

time: 155 us -> 154 us (level)
  transfers between devices with their start and end apart: 10 -> 10, of which waited for: 6 -> 6; matrix products, arithmetic and copies ran while one was open for 0% -> 0% of each run, Pallas kernels for 10% -> 11%
where the time goes in v6:
time: 154 us; the launch traced here: 153 us
  Pallas kernels  40.8 us (26%)
  waiting for transfers between devices  38.3 us (25%)
  blocking collectives  38.3 us (25%)
  starting transfers between devices  31.1 us (20%)
  local copies, waits for them, and re-layouts  2.4 us (2%)
    all_to_all x2, blocking collectives, exchange(): return lax.all_to_all(blocks, AXES, 0, 0, tiled=True)  38.3 us
    all_to_all x2, waiting for transfers between devices, exchange(): return lax.all_to_all(blocks, AXES, 0, 0, tiled=True)  31.3 us
    ppermute x4, starting transfers between devices, halo(): return (near, lax.ppermute(far, 'ty', [(1, 2), (2, 1)]))  15 us
    all_to_all x2, starting transfers between devices, exchange(): return lax.all_to_all(blocks, AXES, 0, 0, tiled=True)  13.7 us
    pallas_call x2, Pallas kernels, shards(): call(early_print_kernel, (FIELD_SHAPE, PRINT_SHAPE), 8, smem=(6, 7), alia...  8.31 us
    ppermute x4, waiting for transfers between devices, halo(): return (near, lax.ppermute(far, 'ty', [(1, 2), (2, 1)]))  7.05 us
    pallas_call x2, Pallas kernels, shards(): call(early_update_kernel, (FIELD_SHAPE, shape(64, 8, 128)), 6, smem=(4, 5...  6.67 us
    pallas_call x2, Pallas kernels, shards(): call(trace_kernel, (TRACE_SHAPE, TRACE_SHAPE, FIELD_SHAPE, EDGE_SHAPE, ED...  4.66 us
  transfers between devices with their start and end apart: 10, of which 6 were waited for; matrix products, arithmetic and copies ran while one was open for 0% of the time, Pallas kernels for 11%

profile of v6, /device:TPU:1, one launch (start us, length us, event | category | flops | bytes accessed | tf_op | source)
XLA Modules:
  0.0 153.3 jit_solution(6132735888521400722)
XLA Ops:
  0.6 0.0 copy-start
  0.6 2.4 %copy.19 = bf16[4,4,16,8,2,128]{5,4,0,2,1,3:T(2,128)(2,1)S(1)} copy(bf16[4,4,16,8,2,128]{5,4,3,2,1,0:T(2,128)(2,1)} %bitcast.10) | data formatting | bytes 2097152 | tf_op jit(solution)/shard_map/reshape | solution.py:521
  3.0 0.7 add_convert_fusion
  3.7 0.7 pad_maximum_fusion.small_ref
  4.4 0.0 copy-done
  4.4 1.8 %shard_map.68 = (bf16[32,168,128]{2,1,0:T(8,128)(2,1)}, s32[8,128]{1,0:T(8,128)S(1)}) custom-call(bf16[32,128,128]{2,1,0:T(8,128)(2,1)S(1)} %bitcast.9, f32[64,4096]{1,0:T(8,128)S(1)} %copy-done, f32[6,64]{1,0:T(8,128)S(1)} %pad_maximum_fusion.small_ref, s32[1]{0:T(128)} %bitcast.5.layer_ref), custom_call_target="tpu_custom_call" | custom-call | flops 1048576 | bytes 1048576 | tf_op jit(solution)/shard_map/pallas_call | solution.py:523
  6.2 9.8 %all-to-all-start = ((bf16[32,168,128]{2,1,0:T(8,128)(2,1)}), bf16[32,168,128]{2,1,0:T(8,128)(2,1)S(1)}, u32[]{:S(2)}, u32[]{:S(2)}) async-start(bf16[32,168,128]{2,1,0:T(8,128)(2,1)} %get-tuple-element.39), calls=%async_computation | async-start | bytes 2752512 | tf_op jit(solution)/shard_map/all_to_all | solution.py:508
  16.0 18.8 %all-to-all-done.got_ref = bf16[32,168,128]{2,1,0:T(8,128)(2,1)S(1)} async-done(((bf16[32,168,128]{2,1,0:T(8,128)(2,1)}), bf16[32,168,128]{2,1,0:T(8,128)(2,1)S(1)}, u32[]{:S(2)}, u32[]{:S(2)}) %all-to-all-start) | async-done | bytes 1376288 | tf_op jit(solution)/shard_map/all_to_all | solution.py:508
  34.8 2.9 %shard_map.69 = (f32[4224,128]{1,0:T(8,128)S(1)}, f32[512,128]{1,0:T(8,128)S(1)}, f32[8,8,128]{2,1,0:T(8,128)S(1)}, s32[24,128]{1,0:T(8,128)S(1)}) custom-call(bf16[32,168,128]{2,1,0:T(8,128)(2,1)S(1)} %all-to-all-done.got_ref, s32[1]{0:T(128)} %bitcast.6.near_ref), custom_call_target="tpu_custom_call" | custom-call | flops 1048576 | bytes 1048576 | tf_op jit(solution)/shard_map/pallas_call | solution.py:526
  37.7 3.3 %shard_map.70 = (f32[512,128]{1,0:T(8,128)S(1)}, f32[4,512,128]{2,1,0:T(8,128)S(1)}, f32[4752,128]{1,0:T(8,128)S(1)}, f32[528,128]{1,0:T(8,128)S(1)}, f32[528,128]{1,0:T(8,128)S(1)}) custom-call(f32[4224,128]{1,0:T(8,128)S(1)} %get-tuple-element.40.movie_ref, f32[512,128]{1,0:T(8,128)S(1)} %get-tuple-element.41.raw_ref, ...), custom_call_target="tpu_custom_call" | custom-call | flops 1048576 | bytes 1048576 | tf_op jit(solution)/shard_map/pallas_call | solution.py:532
  41.0 2.1 %collective-permute-start = (f32[528,128]{1,0:T(8,128)S(1)}, f32[528,128]{1,0:T(8,128)S(1)}, u32[]{:S(2)}, u32[]{:S(2)}) collective-permute-start(f32[528,128]{1,0:T(8,128)S(1)} %get-tuple-element.45), channel_id=1, source_target_pairs={{0,32},{32,0},{64,96},{96,64},{1,33},{33,1},{65,97},{97,65},{2,34}... | collective-permute-start | bytes 811016 | tf_op jit(solution)/shard_map/ppermute | solution.py:512
  43.1 4.3 %collective-permute-start.1 = (f32[528,128]{1,0:T(8,128)S(1)}, f32[528,128]{1,0:T(8,128)S(1)}, u32[]{:S(2)}, u32[]{:S(2)}) collective-permute-start(f32[528,128]{1,0:T(8,128)S(1)} %get-tuple-element.49), channel_id=1, source_target_pairs={{32,64},{64,32},{33,65},{65,33},{34,66},{66,34},{35,67},{67,35},{3... | collective-permute-start | bytes 811016 | tf_op jit(solution)/shard_map/ppermute | solution.py:513
  47.4 0.0 collective-permute-done.near_ref_in
  47.4 3.3 %shard_map.71 = (f32[4752,128]{1,0:T(8,128)S(1)}, f32[64,8,128]{2,1,0:T(8,128)S(1)}) custom-call(f32[4752,128]{1,0:T(8,128)S(1)} %get-tuple-element.44.old_ref, f32[528,128]{1,0:T(8,128)S(1)} %collective-permute-done.near_ref_in, f32[8,8,128]{2,1,0:T(8,128)S(1)} %get-tuple-element.42.activity_ref.old_ref, ...), custom_call_target="tpu_custom_call", output_to_operand_aliasing={{0}: (0, {})} | custom-call | flops 8388608 | bytes 8388608 | tf_op jit(solution)/shard_map/pallas_call | solution.py:537
  50.7 1.7 %collective-permute-done.1.far_ref = f32[528,128]{1,0:T(8,128)S(1)} collective-permute-done((f32[528,128]{1,0:T(8,128)S(1)}, f32[528,128]{1,0:T(8,128)S(1)}, u32[]{:S(2)}, u32[]{:S(2)}) %collective-permute-start.1) | collective-permute-done | bytes 270368 | tf_op jit(solution)/shard_map/ppermute | solution.py:513
  52.4 1.6 %shard_map.72 = (f32[32,17,4,128]{3,2,1,0:T(4,128)S(1)}, f32[4752,128]{1,0:T(8,128)S(1)}, f32[64,8,128]{2,1,0:T(8,128)S(1)}) custom-call(f32[4752,128]{1,0:T(8,128)S(1)} %get-tuple-element.47.old_ref, f32[64,8,128]{2,1,0:T(8,128)S(1)} %get-tuple-element.48.early_ref, ...), custom_call_target="tpu_custom_call", output_to_operand_aliasing={{1}: (0, {}), {2}: (1, {})} | custom-call | flops 1048576 | bytes 1048576 | tf_op jit(solution)/shard_map/pallas_call | solution.py:540
  54.0 19.9 %all_to_all.20.parts_ref = f32[32,17,4,128]{3,2,1,0:T(4,128)S(1)} all-to-all(f32[32,17,4,128]{3,2,1,0:T(4,128)S(1)} %get-tuple-element.51), channel_id=1, replica_groups=mesh['ty'=4,'tx'=8,'ta'=4] {'tx','ta'}, dimensions={0} | all-to-all | bytes 2228224 | tf_op jit(solution)/shard_map/all_to_all | solution.py:508
  73.8 2.3 %shard_map.73 = (f32[8,8,128]{2,1,0:T(8,128)S(1)}, f32[8,8,128]{2,1,0:T(8,128)S(1)}, f32[4752,128]{1,0:T(8,128)S(1)}, f32[528,128]{1,0:T(8,128)S(1)}, f32[528,128]{1,0:T(8,128)S(1)}) custom-call(f32[32,17,4,128]{3,2,1,0:T(4,128)S(1)} %all_to_all.20.parts_ref, f32[8,8,128]{2,1,0:T(8,128)S(1)} %get-tuple-element.42.activity_ref.old_ref, ...), custom_call_target="tpu_custom_call" | custom-call | flops 1048576 | bytes 1048576 | tf_op jit(solution)/shard_map/pallas_call | solution.py:547
  76.2 0.1 collective-permute-start.2
  76.3 3.8 %collective-permute-start.3 = (f32[528,128]{1,0:T(8,128)S(1)}, f32[528,128]{1,0:T(8,128)S(1)}, u32[]{:S(2)}, u32[]{:S(2)}) collective-permute-start(f32[528,128]{1,0:T(8,128)S(1)} %get-tuple-element.58), channel_id=1, source_target_pairs={{32,64},{64,32},{33,65},{65,33},{34,66},{66,34},{35,67},{67,35},{3... | collective-permute-start | bytes 811016 | tf_op jit(solution)/shard_map/ppermute | solution.py:513
  80.1 0.0 collective-permute-done.2.near_ref_in
  80.1 4.2 %shard_map.74 = (f32[4752,128]{1,0:T(8,128)S(1)}, f32[512,128]{1,0:T(8,128)S(1)}) custom-call(f32[4752,128]{1,0:T(8,128)S(1)} %get-tuple-element.52.old_ref, f32[528,128]{1,0:T(8,128)S(1)} %collective-permute-done.2.near_ref_in, f32[8,8,128]{2,1,0:T(8,128)S(1)} %get-tuple-element.54.activity_ref.old_ref, ...), custom_call_target="tpu_custom_call", output_to_operand_aliasing={{0}: (0, {})} | custom-call | flops 8388608 | bytes 8388608 | tf_op jit(solution)/shard_map/pallas_call | solution.py:551
  84.2 1.3 collective-permute-done.3.far_ref
  85.5 3.3 %shard_map.75 = (f32[4752,128]{1,0:T(8,128)S(1)}, f32[512,128]{1,0:T(8,128)S(1)}, f32[4,512,128]{2,1,0:T(8,128)S(1)}, f32[4752,128]{1,0:T(8,128)S(1)}, f32[528,128]{1,0:T(8,128)S(1)}, /*index=5*/f32[528,128]{1,0:T(8,128)S(1)}) custom-call(f32[4752,128]{1,0:T(8,128)S(1)} %get-tuple-element.56.old_ref, ...), custom_call_target="tpu_custom_call", output_to_operand_aliasing={{0}: (0, {}), {1}: (1, {})} | custom-call | flops 1048576 | bytes 1048576 | tf_op jit(solution)/shard_map/pallas_call | solution.py:555
  88.9 0.1 collective-permute-start.4
  89.0 3.8 %collective-permute-start.5 = (f32[528,128]{1,0:T(8,128)S(1)}, f32[528,128]{1,0:T(8,128)S(1)}, u32[]{:S(2)}, u32[]{:S(2)}) collective-permute-start(f32[528,128]{1,0:T(8,128)S(1)} %get-tuple-element.64), channel_id=1, source_target_pairs={{32,64},{64,32},{33,65},{65,33},{34,66},{66,34},{35,67},{67,35},{3... | collective-permute-start | bytes 811016 | tf_op jit(solution)/shard_map/ppermute | solution.py:513
  92.8 0.0 collective-permute-done.4.near_ref_in
  92.8 3.3 %shard_map.76 = (f32[4752,128]{1,0:T(8,128)S(1)}, f32[64,8,128]{2,1,0:T(8,128)S(1)}) custom-call(f32[4752,128]{1,0:T(8,128)S(1)} %get-tuple-element.59.old_ref, f32[528,128]{1,0:T(8,128)S(1)} %collective-permute-done.4.near_ref_in, f32[8,8,128]{2,1,0:T(8,128)S(1)} %get-tuple-element.54.activity_ref.old_ref, ...), custom_call_target="tpu_custom_call", output_to_operand_aliasing={{0}: (0, {})} | custom-call | flops 8388608 | bytes 8388608 | tf_op jit(solution)/shard_map/pallas_call | solution.py:537
  96.1 2.2 %collective-permute-done.5.far_ref = f32[528,128]{1,0:T(8,128)S(1)} collective-permute-done((f32[528,128]{1,0:T(8,128)S(1)}, f32[528,128]{1,0:T(8,128)S(1)}, u32[]{:S(2)}, u32[]{:S(2)}) %collective-permute-start.5) | collective-permute-done | bytes 270368 | tf_op jit(solution)/shard_map/ppermute | solution.py:513
  98.3 1.6 %shard_map.77 = (f32[32,17,4,128]{3,2,1,0:T(4,128)S(1)}, f32[4752,128]{1,0:T(8,128)S(1)}, f32[64,8,128]{2,1,0:T(8,128)S(1)}) custom-call(f32[4752,128]{1,0:T(8,128)S(1)} %get-tuple-element.62.old_ref, f32[64,8,128]{2,1,0:T(8,128)S(1)} %get-tuple-element.63.early_ref, ...), custom_call_target="tpu_custom_call", output_to_operand_aliasing={{1}: (0, {}), {2}: (1, {})} | custom-call | flops 1048576 | bytes 1048576 | tf_op jit(solution)/shard_map/pallas_call | solution.py:540
  99.9 18.5 %all_to_all.21.parts_ref = f32[32,17,4,128]{3,2,1,0:T(4,128)S(1)} all-to-all(f32[32,17,4,128]{3,2,1,0:T(4,128)S(1)} %get-tuple-element.66), channel_id=1, replica_groups=mesh['ty'=4,'tx'=8,'ta'=4] {'tx','ta'}, dimensions={0} | all-to-all | bytes 2228224 | tf_op jit(solution)/shard_map/all_to_all | solution.py:508
  118.3 2.3 %shard_map.78 = (f32[8,8,128]{2,1,0:T(8,128)S(1)}, f32[8,8,128]{2,1,0:T(8,128)S(1)}, f32[4752,128]{1,0:T(8,128)S(1)}, f32[528,128]{1,0:T(8,128)S(1)}, f32[528,128]{1,0:T(8,128)S(1)}) custom-call(f32[32,17,4,128]{3,2,1,0:T(4,128)S(1)} %all_to_all.21.parts_ref, f32[8,8,128]{2,1,0:T(8,128)S(1)} %get-tuple-element.54.activity_ref.old_ref, ...), custom_call_target="tpu_custom_call" | custom-call | flops 1048576 | bytes 1048576 | tf_op jit(solution)/shard_map/pallas_call | solution.py:547
  120.7 0.1 collective-permute-start.6
  120.8 3.2 %collective-permute-start.7 = (f32[528,128]{1,0:T(8,128)S(1)}, f32[528,128]{1,0:T(8,128)S(1)}, u32[]{:S(2)}, u32[]{:S(2)}) collective-permute-start(f32[528,128]{1,0:T(8,128)S(1)} %get-tuple-element.73), channel_id=1, source_target_pairs={{32,64},{64,32},{33,65},{65,33},{34,66},{66,34},{35,67},{67,35},{3... | collective-permute-start | bytes 811016 | tf_op jit(solution)/shard_map/ppermute | solution.py:513
  123.9 0.0 collective-permute-done.6.near_ref_in
  124.0 4.2 %shard_map.79 = (f32[4752,128]{1,0:T(8,128)S(1)}, f32[512,128]{1,0:T(8,128)S(1)}) custom-call(f32[4752,128]{1,0:T(8,128)S(1)} %get-tuple-element.67.old_ref, f32[528,128]{1,0:T(8,128)S(1)} %collective-permute-done.6.near_ref_in, f32[8,8,128]{2,1,0:T(8,128)S(1)} %get-tuple-element.69.activity_ref, ...), custom_call_target="tpu_custom_call", output_to_operand_aliasing={{0}: (0, {})} | custom-call | flops 8388608 | bytes 8388608 | tf_op jit(solution)/shard_map/pallas_call | solution.py:551
  128.1 1.9 %collective-permute-done.7.far_ref = f32[528,128]{1,0:T(8,128)S(1)} collective-permute-done((f32[528,128]{1,0:T(8,128)S(1)}, f32[528,128]{1,0:T(8,128)S(1)}, u32[]{:S(2)}, u32[]{:S(2)}) %collective-permute-start.7) | collective-permute-done | bytes 270368 | tf_op jit(solution)/shard_map/ppermute | solution.py:513
  130.0 3.6 %shard_map.80 = (f32[4752,128]{1,0:T(8,128)S(1)}, f32[512,128]{1,0:T(8,128)S(1)}, f32[32,64,128]{2,1,0:T(8,128)}) custom-call(f32[4752,128]{1,0:T(8,128)S(1)} %get-tuple-element.71.old_ref, f32[512,128]{1,0:T(8,128)S(1)} %get-tuple-element.72.early_ref, f32[528,128]{1,0:T(8,128)S(1)} %collective-permute-done.7.far_ref, ...), custom_call_target="tpu_custom_call", output_to_operand_aliasing={{0}: (0, {}), {1}: (1, {})} | custom-call | flops 1048576 | bytes 1048576 | tf_op jit(solution)/shard_map/pallas_call | solution.py:563
  133.7 3.9 %all-to-all-start.3 = ((f32[32,64,128]{2,1,0:T(8,128)}), f32[32,64,128]{2,1,0:T(8,128)S(1)}, u32[]{:S(2)}, u32[]{:S(2)}) async-start(f32[32,64,128]{2,1,0:T(8,128)} %get-tuple-element.74), calls=%async_computation.3 | async-start | bytes 2097152 | tf_op jit(solution)/shard_map/all_to_all | solution.py:508
  137.6 0.1 pad_add_fusion.spot_ref
  137.7 1.2 shard_map.82
  138.9 12.5 %all-to-all-done.3.blocks_ref = f32[32,64,128]{2,1,0:T(8,128)S(1)} async-done(((f32[32,64,128]{2,1,0:T(8,128)}), f32[32,64,128]{2,1,0:T(8,128)S(1)}, u32[]{:S(2)}, u32[]{:S(2)}) %all-to-all-start.3) | async-done | bytes 1048608 | tf_op jit(solution)/shard_map/all_to_all | solution.py:508
  151.4 1.9 %shard_map.81 = f32[64,4096]{1,0:T(8,128)} custom-call(f32[32,64,128]{2,1,0:T(8,128)S(1)} %all-to-all-done.3.blocks_ref), custom_call_target="tpu_custom_call" | custom-call | flops 1048576 | bytes 1048576 | tf_op jit(solution)/shard_map/pallas_call | solution.py:572
Async XLA Ops:
  0.6 3.8 %copy-start = (f32[64,4096]{1,0:T(8,128)S(1)}, f32[64,4096]{1,0:T(8,128)}, u32[]{:S(2)}) copy-start(f32[64,4096]{1,0:T(8,128)} %prints_ref.1) | copy-start | bytes 3145732
  6.2 28.6 %all-to-all-start = ((bf16[32,168,128]{2,1,0:T(8,128)(2,1)}), bf16[32,168,128]{2,1,0:T(8,128)(2,1)S(1)}, u32[]{:S(2)}, u32[]{:S(2)}) async-start(bf16[32,168,128]{2,1,0:T(8,128)(2,1)} %get-tuple-element.39), calls=%async_computation | async-start | bytes 2752512 | tf_op jit(solution)/shard_map/all_to_all | solution.py:508
  41.0 6.4 %collective-permute-start = (f32[528,128]{1,0:T(8,128)S(1)}, f32[528,128]{1,0:T(8,128)S(1)}, u32[]{:S(2)}, u32[]{:S(2)}) collective-permute-start(f32[528,128]{1,0:T(8,128)S(1)} %get-tuple-element.45), channel_id=1, source_target_pairs={{0,32},{32,0},{64,96},{96,64},{1,33},{33,1},{65,97},{97,65},{2,34}... | collective-permute-start | bytes 811016 | tf_op jit(solution)/shard_map/ppermute | solution.py:512
  43.1 9.3 %collective-permute-start.1 = (f32[528,128]{1,0:T(8,128)S(1)}, f32[528,128]{1,0:T(8,128)S(1)}, u32[]{:S(2)}, u32[]{:S(2)}) collective-permute-start(f32[528,128]{1,0:T(8,128)S(1)} %get-tuple-element.49), channel_id=1, source_target_pairs={{32,64},{64,32},{33,65},{65,33},{34,66},{66,34},{35,67},{67,35},{3... | collective-permute-start | bytes 811016 | tf_op jit(solution)/shard_map/ppermute | solution.py:513
  76.2 3.9 %collective-permute-start.2 = (f32[528,128]{1,0:T(8,128)S(1)}, f32[528,128]{1,0:T(8,128)S(1)}, u32[]{:S(2)}, u32[]{:S(2)}) collective-permute-start(f32[528,128]{1,0:T(8,128)S(1)} %get-tuple-element.53), channel_id=1, source_target_pairs={{0,32},{32,0},{64,96},{96,64},{1,33},{33,1},{65,97},{97,65},{2,34}... | collective-permute-start | bytes 811016 | tf_op jit(solution)/shard_map/ppermute | solution.py:512
  76.3 9.3 %collective-permute-start.3 = (f32[528,128]{1,0:T(8,128)S(1)}, f32[528,128]{1,0:T(8,128)S(1)}, u32[]{:S(2)}, u32[]{:S(2)}) collective-permute-start(f32[528,128]{1,0:T(8,128)S(1)} %get-tuple-element.58), channel_id=1, source_target_pairs={{32,64},{64,32},{33,65},{65,33},{34,66},{66,34},{35,67},{67,35},{3... | collective-permute-start | bytes 811016 | tf_op jit(solution)/shard_map/ppermute | solution.py:513
  88.9 3.9 %collective-permute-start.4 = (f32[528,128]{1,0:T(8,128)S(1)}, f32[528,128]{1,0:T(8,128)S(1)}, u32[]{:S(2)}, u32[]{:S(2)}) collective-permute-start(f32[528,128]{1,0:T(8,128)S(1)} %get-tuple-element.60), channel_id=1, source_target_pairs={{0,32},{32,0},{64,96},{96,64},{1,33},{33,1},{65,97},{97,65},{2,34}... | collective-permute-start | bytes 811016 | tf_op jit(solution)/shard_map/ppermute | solution.py:512
  89.0 9.3 %collective-permute-start.5 = (f32[528,128]{1,0:T(8,128)S(1)}, f32[528,128]{1,0:T(8,128)S(1)}, u32[]{:S(2)}, u32[]{:S(2)}) collective-permute-start(f32[528,128]{1,0:T(8,128)S(1)} %get-tuple-element.64), channel_id=1, source_target_pairs={{32,64},{64,32},{33,65},{65,33},{34,66},{66,34},{35,67},{67,35},{3... | collective-permute-start | bytes 811016 | tf_op jit(solution)/shard_map/ppermute | solution.py:513
  120.7 3.3 %collective-permute-start.6 = (f32[528,128]{1,0:T(8,128)S(1)}, f32[528,128]{1,0:T(8,128)S(1)}, u32[]{:S(2)}, u32[]{:S(2)}) collective-permute-start(f32[528,128]{1,0:T(8,128)S(1)} %get-tuple-element.68), channel_id=1, source_target_pairs={{0,32},{32,0},{64,96},{96,64},{1,33},{33,1},{65,97},{97,65},{2,34}... | collective-permute-start | bytes 811016 | tf_op jit(solution)/shard_map/ppermute | solution.py:512
  120.8 9.3 %collective-permute-start.7 = (f32[528,128]{1,0:T(8,128)S(1)}, f32[528,128]{1,0:T(8,128)S(1)}, u32[]{:S(2)}, u32[]{:S(2)}) collective-permute-start(f32[528,128]{1,0:T(8,128)S(1)} %get-tuple-element.73), channel_id=1, source_target_pairs={{32,64},{64,32},{33,65},{65,33},{34,66},{66,34},{35,67},{67,35},{3... | collective-permute-start | bytes 811016 | tf_op jit(solution)/shard_map/ppermute | solution.py:513
  133.7 17.7 %all-to-all-start.3 = ((f32[32,64,128]{2,1,0:T(8,128)}), f32[32,64,128]{2,1,0:T(8,128)S(1)}, u32[]{:S(2)}, u32[]{:S(2)}) async-start(f32[32,64,128]{2,1,0:T(8,128)} %get-tuple-element.74), calls=%async_computation.3 | async-start | bytes 2097152 | tf_op jit(solution)/shard_map/all_to_all | solution.py:508

commit v7 on v6

--- a/solution.py
+++ b/solution.py
@@ -297,15 +297,28 @@
 
 
 def early_update_kernel(
-    old_ref, near_ref_in, activity_ref, wide_ref, near_ref, table_ref, field_ref, part_ref
+    old_ref, near_ref_in, activity_ref, prints_ref, wide_ref, near_ref, table_ref, field_ref, part_ref, energy_ref
 ):
+    sub, lane = iotas()
+    squares = prints_ref[...] * prints_ref[...]
+    energy = lax.dot_general(
+        jnp.ones((8, 128), F32),
+        squares,
+        (((1,), (1,)), ((), ())),
+        precision=lax.Precision.HIGHEST,
+        preferred_element_type=F32,
+    )
+    rows = energy[:, 0:128]
+    for q in range(1, 4):
+        rows = jnp.where(sub == q, energy[:, 128 * q : 128 * q + 128], rows)
+    energy_ref[...] = rows
     subtract_inner(activity_ref, wide_ref, table_ref, field_ref)
     add_edge(field_ref, near_ref_in, near_ref[0] == 0)
     fold_updates(field_ref, wide_ref, table_ref, part_ref, table_ref[16, 0], table_ref[16, 1])
 
 
 def update_kernel(
-    old_ref, early_ref, far_ref, prints_ref, wide_ref, near_ref, table_ref, out_ref, field_ref, part_ref
+    old_ref, early_ref, far_ref, energy_ref, wide_ref, near_ref, table_ref, out_ref, field_ref, part_ref
 ):
     sub, lane = iotas()
     add_edge(field_ref, far_ref, near_ref[0] != 0)
@@ -317,17 +330,7 @@
         for g in range(GROUP):
             out_ref[g, 2 * v] = parts[0][0:4]
             out_ref[g, 2 * v + 1] = parts[0][4:8]
-    squares = prints_ref[...] * prints_ref[...]
-    energy = lax.dot_general(
-        jnp.ones((8, 128), F32),
-        squares,
-        (((1,), (1,)), ((), ())),
-        precision=lax.Precision.HIGHEST,
-        preferred_element_type=F32,
-    )
-    rows = energy[:, 0:128]
-    for q in range(1, 4):
-        rows = jnp.where(sub == q, energy[:, 128 * q : 128 * q + 128], rows)
+    rows = energy_ref[...]
     for g in range(GROUP):
         out_ref[g, 16] = rows[0:4]
 
@@ -534,16 +537,21 @@
     )(cells, raw, activity, near, table)
     for sweep in range(ITERS):
         left, right = halo(left, right)
-        field, part = call(
-            early_update_kernel, (FIELD_SHAPE, shape(64, 8, 128)), 6, smem=(4, 5), alias=((0, 0),), work=8
-        )(field, left, activity, wide, near, table)
+        field, part, energy = call(
+            early_update_kernel,
+            (FIELD_SHAPE, shape(64, 8, 128), shape(8, 128)),
+            7,
+            smem=(5, 6),
+            alias=((0, 0),),
+            work=8,
+        )(field, left, activity, prints, wide, near, table)
         sums, _, _ = call(
             update_kernel,
             (shape(GROUP, 17, 4, 128), FIELD_SHAPE, shape(64, 8, 128)),
             7,
             smem=(5, 6),
             alias=((0, 1), (1, 2)),
-        )(field, part, right, prints, wide, near, table)
+        )(field, part, right, energy, wide, near, table)
         activity, weight, field, left, right = call(
             trace_kernel, (TRACE_SHAPE, TRACE_SHAPE, FIELD_SHAPE, EDGE_SHAPE, EDGE_SHAPE), 6, smem=(4, 5)
         )(exchange(sums), activity, cells, wide, near, table)

time: 154 us -> 154 us (level)
  no operation moved by 1% of the time
where the time goes in v7:
time: 154 us
  Pallas kernels  41.3 us (27%)
  blocking collectives  38.9 us (25%)
  waiting for transfers between devices  37.5 us (24%)
  starting transfers between devices  31.3 us (20%)
  local copies, waits for them, and re-layouts  2.4 us (2%)
    all_to_all x2, blocking collectives, exchange(): return lax.all_to_all(blocks, AXES, 0, 0, tiled=True)  38.9 us
    all_to_all x2, waiting for transfers between devices, exchange(): return lax.all_to_all(blocks, AXES, 0, 0, tiled=True)  31.3 us
    ppermute x4, starting transfers between devices, halo(): return (near, lax.ppermute(far, 'ty', [(1, 2), (2, 1)]))  15.2 us
    all_to_all x2, starting transfers between devices, exchange(): return lax.all_to_all(blocks, AXES, 0, 0, tiled=True)  13.7 us
    pallas_call x2, Pallas kernels, shards(): call(early_print_kernel, (FIELD_SHAPE, PRINT_SHAPE), 8, smem=(6, 7), alia...  8.32 us
    pallas_call x2, Pallas kernels, shards(): call(early_update_kernel, (FIELD_SHAPE, shape(64, 8, 128), shape(8, 128))...  7.31 us
    ppermute x4, waiting for transfers between devices, halo(): return (near, lax.ppermute(far, 'ty', [(1, 2), (2, 1)]))  6.2 us
    pallas_call x2, Pallas kernels, shards(): call(trace_kernel, (TRACE_SHAPE, TRACE_SHAPE, FIELD_SHAPE, EDGE_SHAPE, ED...  4.64 us
  transfers between devices with their start and end apart: 10, of which 6 were waited for; matrix products, arithmetic and copies ran while one was open for 0% of the time, Pallas kernels for 11%

profile of v7, /device:TPU:1, one launch (start us, length us, event | category | flops | bytes accessed | tf_op | source)
XLA Modules:
  0.0 153.7 jit_solution(17537830901223882296)
XLA Ops:
  0.6 0.0 copy-start
  0.6 2.4 %copy.19 = bf16[4,4,16,8,2,128]{5,4,0,2,1,3:T(2,128)(2,1)S(1)} copy(bf16[4,4,16,8,2,128]{5,4,3,2,1,0:T(2,128)(2,1)} %bitcast.10) | data formatting | bytes 2097152 | tf_op jit(solution)/shard_map/reshape | solution.py:524
  3.0 0.7 add_convert_fusion
  3.7 0.7 pad_maximum_fusion.small_ref
  4.4 0.0 copy-done
  4.4 1.8 %shard_map.68 = (bf16[32,168,128]{2,1,0:T(8,128)(2,1)}, s32[8,128]{1,0:T(8,128)S(1)}) custom-call(bf16[32,128,128]{2,1,0:T(8,128)(2,1)S(1)} %bitcast.9, f32[64,4096]{1,0:T(8,128)S(1)} %copy-done, f32[6,64]{1,0:T(8,128)S(1)} %pad_maximum_fusion.small_ref, s32[1]{0:T(128)} %bitcast.5.layer_ref), custom_call_target="tpu_custom_call" | custom-call | flops 1048576 | bytes 1048576 | tf_op jit(solution)/shard_map/pallas_call | solution.py:526
  6.2 9.8 %all-to-all-start = ((bf16[32,168,128]{2,1,0:T(8,128)(2,1)}), bf16[32,168,128]{2,1,0:T(8,128)(2,1)S(1)}, u32[]{:S(2)}, u32[]{:S(2)}) async-start(bf16[32,168,128]{2,1,0:T(8,128)(2,1)} %get-tuple-element.41), calls=%async_computation | async-start | bytes 2752512 | tf_op jit(solution)/shard_map/all_to_all | solution.py:511
  16.0 18.8 %all-to-all-done.got_ref = bf16[32,168,128]{2,1,0:T(8,128)(2,1)S(1)} async-done(((bf16[32,168,128]{2,1,0:T(8,128)(2,1)}), bf16[32,168,128]{2,1,0:T(8,128)(2,1)S(1)}, u32[]{:S(2)}, u32[]{:S(2)}) %all-to-all-start) | async-done | bytes 1376288 | tf_op jit(solution)/shard_map/all_to_all | solution.py:511
  34.8 2.9 %shard_map.69 = (f32[4224,128]{1,0:T(8,128)S(1)}, f32[512,128]{1,0:T(8,128)S(1)}, f32[8,8,128]{2,1,0:T(8,128)S(1)}, s32[24,128]{1,0:T(8,128)S(1)}) custom-call(bf16[32,168,128]{2,1,0:T(8,128)(2,1)S(1)} %all-to-all-done.got_ref, s32[1]{0:T(128)} %bitcast.6.near_ref), custom_call_target="tpu_custom_call" | custom-call | flops 1048576 | bytes 1048576 | tf_op jit(solution)/shard_map/pallas_call | solution.py:529
  37.7 3.3 %shard_map.70 = (f32[512,128]{1,0:T(8,128)S(1)}, f32[4,512,128]{2,1,0:T(8,128)S(1)}, f32[4752,128]{1,0:T(8,128)S(1)}, f32[528,128]{1,0:T(8,128)S(1)}, f32[528,128]{1,0:T(8,128)S(1)}) custom-call(f32[4224,128]{1,0:T(8,128)S(1)} %get-tuple-element.42.movie_ref, f32[512,128]{1,0:T(8,128)S(1)} %get-tuple-element.43.raw_ref, ...), custom_call_target="tpu_custom_call" | custom-call | flops 1048576 | bytes 1048576 | tf_op jit(solution)/shard_map/pallas_call | solution.py:535
  41.0 2.1 %collective-permute-start = (f32[528,128]{1,0:T(8,128)S(1)}, f32[528,128]{1,0:T(8,128)S(1)}, u32[]{:S(2)}, u32[]{:S(2)}) collective-permute-start(f32[528,128]{1,0:T(8,128)S(1)} %get-tuple-element.47), channel_id=1, source_target_pairs={{0,32},{32,0},{64,96},{96,64},{1,33},{33,1},{65,97},{97,65},{2,34}... | collective-permute-start | bytes 811016 | tf_op jit(solution)/shard_map/ppermute | solution.py:515
  43.1 4.3 %collective-permute-start.1 = (f32[528,128]{1,0:T(8,128)S(1)}, f32[528,128]{1,0:T(8,128)S(1)}, u32[]{:S(2)}, u32[]{:S(2)}) collective-permute-start(f32[528,128]{1,0:T(8,128)S(1)} %get-tuple-element.52), channel_id=1, source_target_pairs={{32,64},{64,32},{33,65},{65,33},{34,66},{66,34},{35,67},{67,35},{3... | collective-permute-start | bytes 811016 | tf_op jit(solution)/shard_map/ppermute | solution.py:516
  47.4 0.0 collective-permute-done.near_ref_in
  47.4 3.7 %shard_map.71 = (f32[4752,128]{1,0:T(8,128)S(1)}, f32[64,8,128]{2,1,0:T(8,128)S(1)}, f32[8,128]{1,0:T(8,128)S(1)}) custom-call(f32[4752,128]{1,0:T(8,128)S(1)} %get-tuple-element.46.old_ref, f32[528,128]{1,0:T(8,128)S(1)} %collective-permute-done.near_ref_in, ...), custom_call_target="tpu_custom_call", output_to_operand_aliasing={{0}: (0, {})} | custom-call | flops 8388608 | bytes 8388608 | tf_op jit(solution)/shard_map/pallas_call | solution.py:540
  51.0 1.3 collective-permute-done.1.far_ref
  52.4 1.5 shard_map.72
  53.9 20.2 %all_to_all.20.parts_ref = f32[32,17,4,128]{3,2,1,0:T(4,128)S(1)} all-to-all(f32[32,17,4,128]{3,2,1,0:T(4,128)S(1)} %get-tuple-element.54), channel_id=1, replica_groups=mesh['ty'=4,'tx'=8,'ta'=4] {'tx','ta'}, dimensions={0} | all-to-all | bytes 2228224 | tf_op jit(solution)/shard_map/all_to_all | solution.py:511
  74.1 2.3 %shard_map.73 = (f32[8,8,128]{2,1,0:T(8,128)S(1)}, f32[8,8,128]{2,1,0:T(8,128)S(1)}, f32[4752,128]{1,0:T(8,128)S(1)}, f32[528,128]{1,0:T(8,128)S(1)}, f32[528,128]{1,0:T(8,128)S(1)}) custom-call(f32[32,17,4,128]{3,2,1,0:T(4,128)S(1)} %all_to_all.20.parts_ref, f32[8,8,128]{2,1,0:T(8,128)S(1)} %get-tuple-element.44.activity_ref.old_ref, ...), custom_call_target="tpu_custom_call" | custom-call | flops 1048576 | bytes 1048576 | tf_op jit(solution)/shard_map/pallas_call | solution.py:555
  76.4 0.1 collective-permute-start.2
  76.5 3.8 %collective-permute-start.3 = (f32[528,128]{1,0:T(8,128)S(1)}, f32[528,128]{1,0:T(8,128)S(1)}, u32[]{:S(2)}, u32[]{:S(2)}) collective-permute-start(f32[528,128]{1,0:T(8,128)S(1)} %get-tuple-element.61), channel_id=1, source_target_pairs={{32,64},{64,32},{33,65},{65,33},{34,66},{66,34},{35,67},{67,35},{3... | collective-permute-start | bytes 811016 | tf_op jit(solution)/shard_map/ppermute | solution.py:516
  80.3 0.0 collective-permute-done.2.near_ref_in
  80.3 4.2 %shard_map.74 = (f32[4752,128]{1,0:T(8,128)S(1)}, f32[512,128]{1,0:T(8,128)S(1)}) custom-call(f32[4752,128]{1,0:T(8,128)S(1)} %get-tuple-element.55.old_ref, f32[528,128]{1,0:T(8,128)S(1)} %collective-permute-done.2.near_ref_in, f32[8,8,128]{2,1,0:T(8,128)S(1)} %get-tuple-element.57.activity_ref.old_ref, ...), custom_call_target="tpu_custom_call", output_to_operand_aliasing={{0}: (0, {})} | custom-call | flops 8388608 | bytes 8388608 | tf_op jit(solution)/shard_map/pallas_call | solution.py:559
  84.5 1.3 collective-permute-done.3.far_ref
  85.8 3.3 %shard_map.75 = (f32[4752,128]{1,0:T(8,128)S(1)}, f32[512,128]{1,0:T(8,128)S(1)}, f32[4,512,128]{2,1,0:T(8,128)S(1)}, f32[4752,128]{1,0:T(8,128)S(1)}, f32[528,128]{1,0:T(8,128)S(1)}, /*index=5*/f32[528,128]{1,0:T(8,128)S(1)}) custom-call(f32[4752,128]{1,0:T(8,128)S(1)} %get-tuple-element.59.old_ref, ...), custom_call_target="tpu_custom_call", output_to_operand_aliasing={{0}: (0, {}), {1}: (1, {})} | custom-call | flops 1048576 | bytes 1048576 | tf_op jit(solution)/shard_map/pallas_call | solution.py:563
  89.1 0.1 collective-permute-start.4
  89.2 3.8 %collective-permute-start.5 = (f32[528,128]{1,0:T(8,128)S(1)}, f32[528,128]{1,0:T(8,128)S(1)}, u32[]{:S(2)}, u32[]{:S(2)}) collective-permute-start(f32[528,128]{1,0:T(8,128)S(1)} %get-tuple-element.68), channel_id=1, source_target_pairs={{32,64},{64,32},{33,65},{65,33},{34,66},{66,34},{35,67},{67,35},{3... | collective-permute-start | bytes 811016 | tf_op jit(solution)/shard_map/ppermute | solution.py:516
  93.0 0.0 collective-permute-done.4.near_ref_in
  93.0 3.7 %shard_map.76 = (f32[4752,128]{1,0:T(8,128)S(1)}, f32[64,8,128]{2,1,0:T(8,128)S(1)}, f32[8,128]{1,0:T(8,128)S(1)}) custom-call(f32[4752,128]{1,0:T(8,128)S(1)} %get-tuple-element.62.old_ref, f32[528,128]{1,0:T(8,128)S(1)} %collective-permute-done.4.near_ref_in, ...), custom_call_target="tpu_custom_call", output_to_operand_aliasing={{0}: (0, {})} | custom-call | flops 8388608 | bytes 8388608 | tf_op jit(solution)/shard_map/pallas_call | solution.py:540
  96.7 1.8 %collective-permute-done.5.far_ref = f32[528,128]{1,0:T(8,128)S(1)} collective-permute-done((f32[528,128]{1,0:T(8,128)S(1)}, f32[528,128]{1,0:T(8,128)S(1)}, u32[]{:S(2)}, u32[]{:S(2)}) %collective-permute-start.5) | collective-permute-done | bytes 270368 | tf_op jit(solution)/shard_map/ppermute | solution.py:516
  98.5 1.5 %shard_map.77 = (f32[32,17,4,128]{3,2,1,0:T(4,128)S(1)}, f32[4752,128]{1,0:T(8,128)S(1)}, f32[64,8,128]{2,1,0:T(8,128)S(1)}) custom-call(f32[4752,128]{1,0:T(8,128)S(1)} %get-tuple-element.66.old_ref, f32[64,8,128]{2,1,0:T(8,128)S(1)} %get-tuple-element.67.early_ref, ...), custom_call_target="tpu_custom_call", output_to_operand_aliasing={{1}: (0, {}), {2}: (1, {})} | custom-call | flops 1048576 | bytes 1048576 | tf_op jit(solution)/shard_map/pallas_call | solution.py:548
  100.0 18.8 %all_to_all.21.parts_ref = f32[32,17,4,128]{3,2,1,0:T(4,128)S(1)} all-to-all(f32[32,17,4,128]{3,2,1,0:T(4,128)S(1)} %get-tuple-element.70), channel_id=1, replica_groups=mesh['ty'=4,'tx'=8,'ta'=4] {'tx','ta'}, dimensions={0} | all-to-all | bytes 2228224 | tf_op jit(solution)/shard_map/all_to_all | solution.py:511
  118.8 2.3 %shard_map.78 = (f32[8,8,128]{2,1,0:T(8,128)S(1)}, f32[8,8,128]{2,1,0:T(8,128)S(1)}, f32[4752,128]{1,0:T(8,128)S(1)}, f32[528,128]{1,0:T(8,128)S(1)}, f32[528,128]{1,0:T(8,128)S(1)}) custom-call(f32[32,17,4,128]{3,2,1,0:T(4,128)S(1)} %all_to_all.21.parts_ref, f32[8,8,128]{2,1,0:T(8,128)S(1)} %get-tuple-element.57.activity_ref.old_ref, ...), custom_call_target="tpu_custom_call" | custom-call | flops 1048576 | bytes 1048576 | tf_op jit(solution)/shard_map/pallas_call | solution.py:555
  121.1 0.1 collective-permute-start.6
  121.2 3.3 %collective-permute-start.7 = (f32[528,128]{1,0:T(8,128)S(1)}, f32[528,128]{1,0:T(8,128)S(1)}, u32[]{:S(2)}, u32[]{:S(2)}) collective-permute-start(f32[528,128]{1,0:T(8,128)S(1)} %get-tuple-element.77), channel_id=1, source_target_pairs={{32,64},{64,32},{33,65},{65,33},{34,66},{66,34},{35,67},{67,35},{3... | collective-permute-start | bytes 811016 | tf_op jit(solution)/shard_map/ppermute | solution.py:516
  124.5 0.0 collective-permute-done.6.near_ref_in
  124.5 4.2 %shard_map.79 = (f32[4752,128]{1,0:T(8,128)S(1)}, f32[512,128]{1,0:T(8,128)S(1)}) custom-call(f32[4752,128]{1,0:T(8,128)S(1)} %get-tuple-element.71.old_ref, f32[528,128]{1,0:T(8,128)S(1)} %collective-permute-done.6.near_ref_in, f32[8,8,128]{2,1,0:T(8,128)S(1)} %get-tuple-element.73.activity_ref, ...), custom_call_target="tpu_custom_call", output_to_operand_aliasing={{0}: (0, {})} | custom-call | flops 8388608 | bytes 8388608 | tf_op jit(solution)/shard_map/pallas_call | solution.py:559
  128.7 1.8 %collective-permute-done.7.far_ref = f32[528,128]{1,0:T(8,128)S(1)} collective-permute-done((f32[528,128]{1,0:T(8,128)S(1)}, f32[528,128]{1,0:T(8,128)S(1)}, u32[]{:S(2)}, u32[]{:S(2)}) %collective-permute-start.7) | collective-permute-done | bytes 270368 | tf_op jit(solution)/shard_map/ppermute | solution.py:516
  130.5 3.6 %shard_map.80 = (f32[4752,128]{1,0:T(8,128)S(1)}, f32[512,128]{1,0:T(8,128)S(1)}, f32[32,64,128]{2,1,0:T(8,128)}) custom-call(f32[4752,128]{1,0:T(8,128)S(1)} %get-tuple-element.75.old_ref, f32[512,128]{1,0:T(8,128)S(1)} %get-tuple-element.76.early_ref, f32[528,128]{1,0:T(8,128)S(1)} %collective-permute-done.7.far_ref, ...), custom_call_target="tpu_custom_call", output_to_operand_aliasing={{0}: (0, {}), {1}: (1, {})} | custom-call | flops 1048576 | bytes 1048576 | tf_op jit(solution)/shard_map/pallas_call | solution.py:571
  134.1 3.9 %all-to-all-start.3 = ((f32[32,64,128]{2,1,0:T(8,128)}), f32[32,64,128]{2,1,0:T(8,128)S(1)}, u32[]{:S(2)}, u32[]{:S(2)}) async-start(f32[32,64,128]{2,1,0:T(8,128)} %get-tuple-element.78), calls=%async_computation.3 | async-start | bytes 2097152 | tf_op jit(solution)/shard_map/all_to_all | solution.py:511
  138.1 0.1 pad_add_fusion.spot_ref
  138.1 1.2 shard_map.82
  139.3 12.5 %all-to-all-done.3.blocks_ref = f32[32,64,128]{2,1,0:T(8,128)S(1)} async-done(((f32[32,64,128]{2,1,0:T(8,128)}), f32[32,64,128]{2,1,0:T(8,128)S(1)}, u32[]{:S(2)}, u32[]{:S(2)}) %all-to-all-start.3) | async-done | bytes 1048608 | tf_op jit(solution)/shard_map/all_to_all | solution.py:511
  151.8 1.9 %shard_map.81 = f32[64,4096]{1,0:T(8,128)} custom-call(f32[32,64,128]{2,1,0:T(8,128)S(1)} %all-to-all-done.3.blocks_ref), custom_call_target="tpu_custom_call" | custom-call | flops 1048576 | bytes 1048576 | tf_op jit(solution)/shard_map/pallas_call | solution.py:580
Async XLA Ops:
  0.6 3.8 %copy-start = (f32[64,4096]{1,0:T(8,128)S(1)}, f32[64,4096]{1,0:T(8,128)}, u32[]{:S(2)}) copy-start(f32[64,4096]{1,0:T(8,128)} %prints_ref.1) | copy-start | bytes 3145732
  6.2 28.6 %all-to-all-start = ((bf16[32,168,128]{2,1,0:T(8,128)(2,1)}), bf16[32,168,128]{2,1,0:T(8,128)(2,1)S(1)}, u32[]{:S(2)}, u32[]{:S(2)}) async-start(bf16[32,168,128]{2,1,0:T(8,128)(2,1)} %get-tuple-element.41), calls=%async_computation | async-start | bytes 2752512 | tf_op jit(solution)/shard_map/all_to_all | solution.py:511
  41.0 6.4 %collective-permute-start = (f32[528,128]{1,0:T(8,128)S(1)}, f32[528,128]{1,0:T(8,128)S(1)}, u32[]{:S(2)}, u32[]{:S(2)}) collective-permute-start(f32[528,128]{1,0:T(8,128)S(1)} %get-tuple-element.47), channel_id=1, source_target_pairs={{0,32},{32,0},{64,96},{96,64},{1,33},{33,1},{65,97},{97,65},{2,34}... | collective-permute-start | bytes 811016 | tf_op jit(solution)/shard_map/ppermute | solution.py:515
  43.1 9.3 %collective-permute-start.1 = (f32[528,128]{1,0:T(8,128)S(1)}, f32[528,128]{1,0:T(8,128)S(1)}, u32[]{:S(2)}, u32[]{:S(2)}) collective-permute-start(f32[528,128]{1,0:T(8,128)S(1)} %get-tuple-element.52), channel_id=1, source_target_pairs={{32,64},{64,32},{33,65},{65,33},{34,66},{66,34},{35,67},{67,35},{3... | collective-permute-start | bytes 811016 | tf_op jit(solution)/shard_map/ppermute | solution.py:516
  76.4 3.9 %collective-permute-start.2 = (f32[528,128]{1,0:T(8,128)S(1)}, f32[528,128]{1,0:T(8,128)S(1)}, u32[]{:S(2)}, u32[]{:S(2)}) collective-permute-start(f32[528,128]{1,0:T(8,128)S(1)} %get-tuple-element.56), channel_id=1, source_target_pairs={{0,32},{32,0},{64,96},{96,64},{1,33},{33,1},{65,97},{97,65},{2,34}... | collective-permute-start | bytes 811016 | tf_op jit(solution)/shard_map/ppermute | solution.py:515
  76.5 9.3 %collective-permute-start.3 = (f32[528,128]{1,0:T(8,128)S(1)}, f32[528,128]{1,0:T(8,128)S(1)}, u32[]{:S(2)}, u32[]{:S(2)}) collective-permute-start(f32[528,128]{1,0:T(8,128)S(1)} %get-tuple-element.61), channel_id=1, source_target_pairs={{32,64},{64,32},{33,65},{65,33},{34,66},{66,34},{35,67},{67,35},{3... | collective-permute-start | bytes 811016 | tf_op jit(solution)/shard_map/ppermute | solution.py:516
  89.1 3.9 %collective-permute-start.4 = (f32[528,128]{1,0:T(8,128)S(1)}, f32[528,128]{1,0:T(8,128)S(1)}, u32[]{:S(2)}, u32[]{:S(2)}) collective-permute-start(f32[528,128]{1,0:T(8,128)S(1)} %get-tuple-element.63), channel_id=1, source_target_pairs={{0,32},{32,0},{64,96},{96,64},{1,33},{33,1},{65,97},{97,65},{2,34}... | collective-permute-start | bytes 811016 | tf_op jit(solution)/shard_map/ppermute | solution.py:515
  89.2 9.3 %collective-permute-start.5 = (f32[528,128]{1,0:T(8,128)S(1)}, f32[528,128]{1,0:T(8,128)S(1)}, u32[]{:S(2)}, u32[]{:S(2)}) collective-permute-start(f32[528,128]{1,0:T(8,128)S(1)} %get-tuple-element.68), channel_id=1, source_target_pairs={{32,64},{64,32},{33,65},{65,33},{34,66},{66,34},{35,67},{67,35},{3... | collective-permute-start | bytes 811016 | tf_op jit(solution)/shard_map/ppermute | solution.py:516
  121.1 3.4 %collective-permute-start.6 = (f32[528,128]{1,0:T(8,128)S(1)}, f32[528,128]{1,0:T(8,128)S(1)}, u32[]{:S(2)}, u32[]{:S(2)}) collective-permute-start(f32[528,128]{1,0:T(8,128)S(1)} %get-tuple-element.72), channel_id=1, source_target_pairs={{0,32},{32,0},{64,96},{96,64},{1,33},{33,1},{65,97},{97,65},{2,34}... | collective-permute-start | bytes 811016 | tf_op jit(solution)/shard_map/ppermute | solution.py:515
  121.2 9.3 %collective-permute-start.7 = (f32[528,128]{1,0:T(8,128)S(1)}, f32[528,128]{1,0:T(8,128)S(1)}, u32[]{:S(2)}, u32[]{:S(2)}) collective-permute-start(f32[528,128]{1,0:T(8,128)S(1)} %get-tuple-element.77), channel_id=1, source_target_pairs={{32,64},{64,32},{33,65},{65,33},{34,66},{66,34},{35,67},{67,35},{3... | collective-permute-start | bytes 811016 | tf_op jit(solution)/shard_map/ppermute | solution.py:516
  134.1 17.7 %all-to-all-start.3 = ((f32[32,64,128]{2,1,0:T(8,128)}), f32[32,64,128]{2,1,0:T(8,128)S(1)}, u32[]{:S(2)}, u32[]{:S(2)}) async-start(f32[32,64,128]{2,1,0:T(8,128)} %get-tuple-element.78), calls=%async_computation.3 | async-start | bytes 2097152 | tf_op jit(solution)/shard_map/all_to_all | solution.py:511
